TPU v7x, 128 devices: a whole 4x4x4 slice. The times are simulated.
128 devices in a mesh: lon: 32 (over x_hi, z, y), ch: 4 (over x_lo, core).
Axes of the slice: x: 4 (x_hi: 2, x_lo: 2; x = x_hi * 2 + x_lo), y: 4, z: 4, core: 2. Of those that a mesh axis runs over, the one named last changes fastest.
Arguments:
- ocean_state: bfloat16 [400, 64, 4096], P('ch', None, 'lon'), may hold values from -6 to 6
- sea_mask: int32 [64, 4096], P(None, 'lon'), may hold values 0 or 1
- kernel: float32 [400, 49], P('ch'), may hold values from -0.875 to 0.875
- conv_bias: float32 [400], P('ch'), may hold values from -3 to 3
- norm_gain: float32 [400], replicated, may hold values from 0.1 to 1.9
- norm_bias: float32 [400], replicated, may hold values from -2 to 2
- weight_in: bfloat16 [400, 1600], replicated, may hold values from -0.3125 to 0.3125
- bias_in: float32 [1600], replicated, may hold values from -3 to 3
- weight_out: bfloat16 [1600, 400], replicated, may hold values from -0.15625 to 0.15625
- bias_out: float32 [400], replicated, may hold values from -3 to 3
- layer_scale: float32 [400], P('ch'), may hold values from 0.5 to 2
- cotangent: bfloat16 [400, 64, 4096], P('ch', None, 'lon'), may hold values from -6 to 6
Outputs:
- updated: bfloat16 [400, 64, 4096], P('ch', None, 'lon')
- grad_state: bfloat16 [400, 64, 4096], P('ch', None, 'lon')
- grad_weight_in: float32 [400, 1600], replicated
- grad_weight_out: float32 [1600, 400], replicated
Inputs may be any that keep to these rules, and one draw needn't show every extreme that they name: `sea_mask`: 1 marks an ocean cell, 0 a land cell.
All inputs are finite; a program needn't handle non-finite values. No bound on the sum of `sea_mask` on one device may be relied on, other than what follows from the above.
Results may differ from a plain program's by a relative error of at most 0.0077.
Values may be sent and summed in bfloat16 or wider, within the bound.
No kernel may reach another device: no remote copies, remote signals or barrier semaphores. Data moves between devices by JAX's collectives and lax.ppermute only.
A program may use at most 192 MiB of HBM per device.

v0:
```python
import functools
import math

import jax
import jax.numpy as jnp
from jax import lax
from jax.experimental import pallas as pl
from jax.experimental.pallas import tpu as pltpu
from jax.sharding import PartitionSpec as P

KW = 7
RIM = KW // 2
C = 400
HID = 1600
ROWS = 64
LANES = 128
LC = 100
CP = 104
QR = 16
HR = 8
GROUP = 8
VMEM = 63 << 20
BF = jnp.bfloat16
F32 = jnp.float32

root_coef = math.sqrt(2.0 / math.pi)
cubic_coef = 0.044715
norm_eps = 1e-06


def dotg(a, b, ca, cb):
    return lax.dot_general(a, b, (((ca,), (cb,)), ((), ())), preferred_element_type=F32)


def cost(micros):
    return pl.CostEstimate(flops=0, bytes_accessed=int(micros * 3.3e6), transcendentals=0)


def full(shape):
    return pl.BlockSpec(shape, lambda *i: (0,) * len(shape), pipeline_mode=pl.Buffered(1))


def ch_swap(x, k):
    return lax.ppermute(x, "ch", [(i, i ^ k) for i in range(4)])


def lon_shift(x, d):
    return lax.ppermute(x, "lon", [(i, (i + d) % 32) for i in range(32)])


def lon_swap(x, k):
    return lax.ppermute(x, "lon", [(i, i ^ k) for i in range(32)])


def share_kernel(me_ref, cot_ref, mask_ref, scale_ref, *refs):
    out_ref = refs[-1]
    cells = cot_ref[...].astype(F32)
    cells = jnp.concatenate([cells, jnp.zeros((CP - LC, QR, LANES), F32)], axis=0)
    cells = jnp.swapaxes(cells, 0, 1)
    mask = mask_ref[...].astype(F32)
    out_ref[...] = ((cells * mask[:, None, :]) * scale_ref[...][None]).astype(BF)


def branch_share(me, cotangent, sea_mask, scale, k, after):
    return pl.pallas_call(
        share_kernel,
        out_shape=jax.ShapeDtypeStruct((QR, CP, LANES), BF),
        grid_spec=pltpu.PrefetchScalarGridSpec(
            num_scalar_prefetch=1,
            grid=(1,),
            in_specs=[
                pl.BlockSpec((LC, QR, LANES), lambda i, me: (0, me[0] ^ k, 0)),
                pl.BlockSpec((QR, LANES), lambda i, me: (me[0] ^ k, 0)),
                pl.BlockSpec((CP, 1), lambda i, me: (0, 0)),
            ]
            + [pl.BlockSpec(memory_space=pl.ANY)] * len(after),
            out_specs=pl.BlockSpec((QR, CP, LANES), lambda i, me: (0, 0, 0)),
        ),
        compiler_params=pltpu.CompilerParams(vmem_limit_bytes=VMEM),
        cost_estimate=cost(1.2),
        name="branch_share",
    )(me, cotangent, sea_mask, scale, *after)


def conv_channel(cells, rim, pattern, lane, band):
    moved = []
    for off in range(-RIM, RIM + 1):
        if off == 0:
            moved.append(cells.astype(BF))
        else:
            edge = lane < off if off > 0 else lane >= LANES + off
            moved.append(pltpu.roll(jnp.where(edge, rim, cells), (-off) % LANES, 1).astype(BF))
    stacked = jnp.concatenate(moved, axis=0)
    tiles = []
    for t in range(4):
        row = jnp.broadcast_to(pattern[t : t + 1, :], (ROWS, LANES))
        row = pltpu.roll(row, 0, 1, stride=1, stride_axis=0)
        tiles.append(jnp.where(band, row, 0.0).astype(BF))
    banded = jnp.concatenate(tiles, axis=1)[:, : KW * ROWS]
    return jnp.dot(banded, stacked, preferred_element_type=F32)


def masks():
    lane = lax.broadcasted_iota(jnp.int32, (ROWS, LANES), 1)
    row = lax.broadcasted_iota(jnp.int32, (ROWS, LANES), 0)
    away = (lane & (ROWS - 1)) - row
    return lane, (away >= -RIM) & (away <= RIM)


def forward_kernel(me_ref, state_ref, rim_ref, pat_ref, bias_ref, *refs):
    held = refs[-1]
    step = pl.program_id(0)
    lane, band = masks()
    outs = []
    for c in range(GROUP):
        total = conv_channel(
            state_ref[c].astype(F32), rim_ref[c].astype(F32), pat_ref[c], lane, band
        )
        total = total + bias_ref[c]
        outs.append(jnp.where(step * GROUP + c < LC, total, 0.0))
    held[...] = jnp.swapaxes(jnp.stack(outs, 0), 0, 1).reshape(4, QR, GROUP, LANES)
    me = me_ref[0]
    for k in range(4):
        share = held[me ^ k].astype(BF)
        refs[k][...] = share[:HR]
        refs[4 + k][...] = share[HR:]


def conv_forward(me, state, rim, pattern, bias):
    share = jax.ShapeDtypeStruct((HR, CP, LANES), BF)
    return pl.pallas_call(
        forward_kernel,
        out_shape=[share] * 8,
        grid_spec=pltpu.PrefetchScalarGridSpec(
            num_scalar_prefetch=1,
            grid=(CP // GROUP,),
            in_specs=[
                pl.BlockSpec((GROUP, ROWS, LANES), lambda i, me: (i, 0, 0)),
                pl.BlockSpec((GROUP, ROWS, LANES), lambda i, me: (i, 0, 0)),
                pl.BlockSpec((GROUP, 4, LANES), lambda i, me: (i, 0, 0)),
                pl.BlockSpec((GROUP, 1, LANES), lambda i, me: (i, 0, 0)),
            ],
            out_specs=[pl.BlockSpec((HR, GROUP, LANES), lambda i, me: (0, i, 0))] * 8,
            scratch_shapes=[pltpu.VMEM((4, QR, GROUP, LANES), F32)],
        ),
        compiler_params=pltpu.CompilerParams(vmem_limit_bytes=VMEM),
        cost_estimate=cost(9),
        name="conv_forward",
    )(me, state, rim, pattern, bias)


def backward_kernel(me_ref, *refs):
    pieces = refs[:8]
    rims_in, pat_ref, cot_ref, mask_ref, out_ref, held, held_rim = refs[8:]
    lane, band = masks()
    me = me_ref[0]
    for k in range(4):
        held[me ^ k, :HR] = pieces[k][...].astype(F32)
        held[me ^ k, HR:] = pieces[4 + k][...].astype(F32)
        held_rim[me ^ k, :HR] = rims_in[k].astype(F32)
        held_rim[me ^ k, HR:] = rims_in[4 + k].astype(F32)
    cells = jnp.swapaxes(held[...].reshape(ROWS, GROUP, LANES), 0, 1)
    rims = jnp.swapaxes(held_rim[...].reshape(ROWS, GROUP, LANES), 0, 1)
    mask = mask_ref[...].astype(F32)
    for c in range(GROUP):
        total = conv_channel(cells[c], rims[c], pat_ref[c], lane, band)
        out_ref[c] = (cot_ref[c].astype(F32) * mask + total).astype(BF)


def conv_backward(me, pieces, rims, pattern, cotangent, sea_mask):
    return pl.pallas_call(
        backward_kernel,
        out_shape=jax.ShapeDtypeStruct((LC, ROWS, LANES), BF),
        grid_spec=pltpu.PrefetchScalarGridSpec(
            num_scalar_prefetch=1,
            grid=(CP // GROUP,),
            in_specs=[pl.BlockSpec((HR, GROUP, LANES), lambda i, me: (0, i, 0))] * 8
            + [
                pl.BlockSpec((8, HR, GROUP, LANES), lambda i, me: (0, 0, i, 0)),
                pl.BlockSpec((GROUP, 4, LANES), lambda i, me: (i, 0, 0)),
                pl.BlockSpec((GROUP, ROWS, LANES), lambda i, me: (i, 0, 0)),
                pl.BlockSpec((ROWS, LANES), lambda i, me: (0, 0)),
            ],
            out_specs=pl.BlockSpec((GROUP, ROWS, LANES), lambda i, me: (i, 0, 0)),
            scratch_shapes=[pltpu.VMEM((4, QR, GROUP, LANES), F32)] * 2,
        ),
        compiler_params=pltpu.CompilerParams(vmem_limit_bytes=VMEM),
        cost_estimate=cost(10),
        name="conv_backward",
    )(me, *pieces, rims, pattern, cotangent, sea_mask)


SUB = 4
CELLS = SUB * LANES
HT = 400
PIECE = 328
WIRE = 16 * PIECE


def mlp_kernel(half, me_ref, core_ref, *refs):
    xs, gs = refs[:4], refs[4:8]
    win_t, win, wout, wout_t, vec, bias_in = refs[8:14]
    if half:
        hid_in, cells_in = refs[14:16]
        grad_out, branch_out, wires = refs[17:21], refs[21:25], refs[25:27]
        hidden, cells, hid_a, cells_a, held, sems = refs[27:]
        copies = (
            pltpu.make_async_copy(hid_in, hid_a, sems.at[0]),
            pltpu.make_async_copy(cells_in, cells_a, sems.at[1]),
        )
    else:
        grad_out, branch_out = refs[14:18], refs[18:22]
        hidden, cells = refs[22:]
    step = pl.program_id(0)
    me = me_ref[0]
    if half:

        @pl.when(step == 0)
        def _():
            for copy in copies:
                copy.start()

        lanes = pl.ds(pl.multiple_of(step * CELLS, CELLS), CELLS)
    else:
        lanes = slice(0, CELLS)

    def gather(pieces):
        return jnp.concatenate(
            [
                jnp.concatenate([p[r].astype(F32) for r in range(SUB)], axis=1)
                for p in pieces
            ],
            axis=0,
        )

    gain = vec[:, 0:1]
    values = gather(xs)
    mean_val = jnp.sum(values, axis=0, keepdims=True) / C
    square = jnp.sum(values * values, axis=0, keepdims=True) / C
    inv_std = lax.rsqrt(square - mean_val * mean_val + norm_eps)
    normed = (values - mean_val) * inv_std * gain + vec[:, 1:2]
    grads = gather(gs)
    for k in range(4):
        rows = slice(k * CP, (k + 1) * CP)
        cells[0, me ^ k, :, lanes] = normed[rows].astype(cells.dtype)
        cells[1, me ^ k, :, lanes] = grads[rows].astype(cells.dtype)
    normed, grads = normed.astype(BF), grads.astype(BF)
    for t in range(HID // HT):
        rows = slice(t * HT, (t + 1) * HT)
        pre = jnp.dot(win_t[rows, :], normed, preferred_element_type=F32) + bias_in[rows, :]
        gact = jnp.dot(wout[rows, :], grads, preferred_element_type=F32)
        sq = pre * pre
        tangent = jnp.tanh(pre * (root_coef + (root_coef * cubic_coef) * sq))
        side = 0.5 + 0.5 * tangent
        value = pre * side
        slope = side + value * (1.0 - side) * (
            2.0 * root_coef + (6.0 * root_coef * cubic_coef) * sq
        )
        hidden[0, rows, lanes] = (gact * slope).astype(BF)
        hidden[1, rows, lanes] = value.astype(BF)
    x_grad = jnp.dot(win[...], hidden[0, :, lanes], preferred_element_type=F32) * gain
    centred = (values - mean_val) * inv_std
    first = jnp.sum(x_grad, axis=0, keepdims=True) / C
    second = jnp.sum(x_grad * centred, axis=0, keepdims=True) / C
    x_grad = inv_std * (x_grad - first - centred * second)
    branch = jnp.dot(wout_t[...], hidden[1, :, lanes], preferred_element_type=F32)
    branch = branch + vec[:, 2:3]
    for k in range(4):
        for r in range(SUB):
            here = slice(r * LANES, (r + 1) * LANES)
            grad_out[k][r] = x_grad[k * CP : (k + 1) * CP, here].astype(BF)
            branch_out[k][r] = branch[k * CP : (k + 1) * CP, here].astype(BF)
    if not half:
        return

    @pl.when(step == 1)
    def _():
        for copy in copies:
            copy.wait()
        core = core_ref[0]
        for out, slot in ((wires[0], core), (wires[1], 1 - core)):
            cells_b = cells[slot].reshape(4 * CP, 2 * CELLS).astype(BF)
            held[...] = dotg(hid_a[slot], cells_a[slot], 1, 1) + dotg(hidden[slot], cells_b, 1, 1)
            for t in range(3):
                out[t * HID : (t + 1) * HID, :] = held[:, t * LANES : (t + 1) * LANES].astype(BF)
            rest = [held[q * 400 : (q + 1) * 400, 3 * LANES :] for q in range(4)]
            out[3 * HID : 3 * HID + 400, :] = jnp.concatenate(rest, axis=1).astype(BF)
            out[3 * HID + 400 :, :] = jnp.zeros((WIRE - 3 * HID - 400, LANES), BF)


def mlp(half, me, core, xs, gs, weights, vec, bias_in, saved=(), after=()):
    any_space = pl.BlockSpec(memory_space=pl.ANY)

    def whole(shape):
        return pl.BlockSpec(
            shape, lambda i, me, core: (0,) * len(shape), pipeline_mode=pl.Buffered(1)
        )

    piece = pl.BlockSpec((SUB, CP, LANES), lambda i, me, core: (i, 0, 0))
    later = pl.BlockSpec((SUB, CP, LANES), lambda i, me, core: (2 * half + i, 0, 0))
    if half:
        shapes = [jax.ShapeDtypeStruct((WIRE, LANES), BF)] * 2
        specs = [whole((WIRE, LANES))] * 2
        scratch = [
            pltpu.VMEM((2, HID, 2 * CELLS), BF),
            pltpu.VMEM((2, 4, CP, 2 * CELLS), F32),
            pltpu.VMEM((2, HID, 2 * CELLS), BF),
            pltpu.VMEM((2, 4 * CP, 2 * CELLS), BF),
            pltpu.VMEM((HID, 4 * CP), F32),
            pltpu.SemaphoreType.DMA((2,)),
        ]
    else:
        shapes = [
            jax.ShapeDtypeStruct((2, HID, 2 * CELLS), BF),
            jax.ShapeDtypeStruct((2, 4, CP, 2 * CELLS), BF),
        ]
        specs = [
            pl.BlockSpec((2, HID, CELLS), lambda i, me, core: (0, 0, i)),
            pl.BlockSpec((2, 4, CP, CELLS), lambda i, me, core: (0, 0, 0, i)),
        ]
        scratch = []
    outs = pl.pallas_call(
        functools.partial(mlp_kernel, half),
        out_shape=[jax.ShapeDtypeStruct((HR, CP, LANES), BF)] * 8 + shapes,
        grid_spec=pltpu.PrefetchScalarGridSpec(
            num_scalar_prefetch=2,
            grid=(2,),
            in_specs=[piece] * 4
            + [later] * 4
            + [
                whole((HID, 4 * CP)),
                whole((4 * CP, HID)),
                whole((HID, 4 * CP)),
                whole((4 * CP, HID)),
                whole((4 * CP, 3)),
                whole((HID, 1)),
            ]
            + [any_space] * (len(saved) + len(after)),
            out_specs=[piece] * 8 + specs,
            scratch_shapes=scratch,
        ),
        compiler_params=pltpu.CompilerParams(vmem_limit_bytes=VMEM),
        cost_estimate=cost(22 if half else 14),
        name="mlp_b" if half else "mlp_a",
    )(me, core, *xs, *gs, *weights, vec, bias_in, *saved, *after)
    return outs[:4], outs[4:8], outs[8:]


def update_kernel(me_ref, *refs):
    k = pl.program_id(0)
    state_ref, mask_ref, scale_ref, out_ref, held = refs[8:]

    def take(early, late):
        held[:HR] = early[...]
        held[HR:] = late[...]

    for i in range(4):
        pl.when(k == i)(lambda i=i: take(refs[i], refs[4 + i]))
    branch = jnp.swapaxes(held[...].astype(F32) * scale_ref[...][None], 0, 1)[:LC]
    mask = mask_ref[...].astype(F32)
    out_ref[...] = (mask[None] * (state_ref[...].astype(F32) + branch)).astype(BF)


def update(me, pieces, state, sea_mask, scale):
    whole = pl.BlockSpec((HR, CP, LANES), lambda i, me: (0, 0, 0), pipeline_mode=pl.Buffered(1))
    return pl.pallas_call(
        update_kernel,
        out_shape=jax.ShapeDtypeStruct((LC, ROWS, LANES), BF),
        grid_spec=pltpu.PrefetchScalarGridSpec(
            num_scalar_prefetch=1,
            grid=(4,),
            in_specs=[whole] * 8
            + [
                pl.BlockSpec((LC, QR, LANES), lambda i, me: (0, me[0] ^ i, 0)),
                pl.BlockSpec((QR, LANES), lambda i, me: (me[0] ^ i, 0)),
                pl.BlockSpec((CP, 1), lambda i, me: (0, 0)),
            ],
            out_specs=pl.BlockSpec((LC, QR, LANES), lambda i, me: (0, me[0] ^ i, 0)),
            scratch_shapes=[pltpu.VMEM((QR, CP, LANES), BF)],
        ),
        compiler_params=pltpu.CompilerParams(vmem_limit_bytes=VMEM),
        cost_estimate=cost(4.4),
        name="update",
    )(me, *pieces, state, sea_mask, scale)


def weights_kernel(one, two, pad, one_out, one_t, two_out, two_t):
    for source, out, turned in ((one, one_out, one_t), (two, two_out, two_t)):
        padded = dotg(pad[...], source[...], 0, 0)
        out[...] = padded.astype(BF)
        turned[...] = padded.T.astype(BF)


def padded_weights(one, two, pad):
    flat = jax.ShapeDtypeStruct((4 * CP, HID), BF)
    turned = jax.ShapeDtypeStruct((HID, 4 * CP), BF)
    return pl.pallas_call(
        weights_kernel,
        out_shape=[flat, turned, flat, turned],
        grid=(1,),
        in_specs=[full((C, HID)), full((C, HID)), full((C, 4 * CP))],
        out_specs=[full(x.shape) for x in (flat, turned, flat, turned)],
        compiler_params=pltpu.CompilerParams(vmem_limit_bytes=VMEM),
        cost_estimate=cost(5),
        name="padded_weights",
    )(one, two, pad)


def tap_patterns(kernel):
    lane = jnp.arange(4 * LANES)
    tile, pos = lane // LANES, lane % LANES
    away = jnp.where(pos % ROWS < ROWS // 2, pos % ROWS, pos % ROWS - ROWS)
    side = ((pos - away) // ROWS) % 2
    col = 2 * tile + side
    tap = jnp.where((jnp.abs(away) <= RIM) & (col < KW), (away + RIM) * KW + col, -1)
    pick = (jnp.arange(KW * KW)[:, None] == tap[None, :]).astype(BF)
    return jnp.dot(kernel.astype(BF), pick, preferred_element_type=F32).reshape(LC, 4, LANES)


def edge_picks():
    row = jnp.arange(8)[:, None]
    lane = jnp.arange(LANES)[None, :]
    head = ((row < RIM) & (lane == row)).astype(BF)
    tail = ((row < RIM) & (lane == LANES - RIM + row)).astype(BF)
    return head, tail


def edge_kernel(cells, pick, *refs):
    refs[-1][...] = dotg(pick[...], cells[...], 1, 1).astype(BF)


def edge(cells2d, pick, after=()):
    return pl.pallas_call(
        edge_kernel,
        out_shape=jax.ShapeDtypeStruct((8, cells2d.shape[0]), BF),
        grid=(1,),
        in_specs=[full(cells2d.shape), full(pick.shape)]
        + [pl.BlockSpec(memory_space=pl.ANY)] * len(after),
        out_specs=full((8, cells2d.shape[0])),
        compiler_params=pltpu.CompilerParams(vmem_limit_bytes=VMEM),
        cost_estimate=cost(1),
        name="edge",
    )(cells2d, pick, *after)


def piece_edges_kernel(pick, *refs):
    first, last = refs[8:]
    for i in range(8):
        cells = refs[i][...].reshape(HR * CP, LANES)
        both = dotg(pick[...], cells, 1, 1).astype(BF)
        first[i] = both[:8]
        last[i] = both[8:]


def piece_edges(picks, pieces):
    half = pl.BlockSpec((QR // 2, CP, LANES), lambda i: (0, 0, 0))
    whole = pl.BlockSpec((8, 8, HR * CP), lambda i: (0, 0, 0))
    out = jax.ShapeDtypeStruct((8, 8, HR * CP), BF)
    return pl.pallas_call(
        piece_edges_kernel,
        out_shape=[out, out],
        grid=(1,),
        in_specs=[pl.BlockSpec((16, LANES), lambda i: (0, 0))] + [half] * 8,
        out_specs=[whole] * 2,
        compiler_params=pltpu.CompilerParams(vmem_limit_bytes=VMEM),
        cost_estimate=cost(2),
        name="piece_edges",
    )(picks, *pieces)


def piece_rims_kernel(pick, first, last, out):
    for i in range(8):
        both = jnp.concatenate([first[i], last[i]], axis=0)
        out[i] = dotg(both, pick[...], 0, 0).astype(BF).reshape(HR, CP, LANES)


def piece_rims(picks, first, last):
    return pl.pallas_call(
        piece_rims_kernel,
        out_shape=jax.ShapeDtypeStruct((8, HR, CP, LANES), BF),
        grid=(1,),
        in_specs=[full((16, LANES)), full((8, 8, HR * CP)), full((8, 8, HR * CP))],
        out_specs=full((8, HR, CP, LANES)),
        compiler_params=pltpu.CompilerParams(vmem_limit_bytes=VMEM),
        cost_estimate=cost(2),
        name="piece_rims",
    )(picks, lon_shift(first, -1), lon_shift(last, 1))


def rims(first, last):
    both = jnp.concatenate([lon_shift(first, -1), lon_shift(last, 1)], 0)
    return dotg(both, jnp.concatenate(edge_picks(), 0), 0, 0).astype(BF)


PLANES = [[16 * half + i for i in range(16)] for half in range(2)]


def plane_exchange(pieces):
    return lax.all_to_all(pieces, "lon", 0, 0, axis_index_groups=PLANES)


def total_kernel(*refs):
    total = refs[0][0].astype(F32)
    for i in range(1, 16):
        total = total + refs[0][i].astype(F32)
    refs[-1][...] = total.astype(BF)


def plane_total(pieces, after):
    return pl.pallas_call(
        total_kernel,
        out_shape=jax.ShapeDtypeStruct((PIECE, LANES), BF),
        grid=(1,),
        in_specs=[full((16, PIECE, LANES))] + [pl.BlockSpec(memory_space=pl.ANY)] * len(after),
        out_specs=full((PIECE, LANES)),
        compiler_params=pltpu.CompilerParams(vmem_limit_bytes=VMEM),
        cost_estimate=cost(1.2),
        name="plane_total",
    )(pieces, *after)


def copies_kernel(part, out):
    for i in range(16):
        out[i] = part[...]


def plane_copies(part):
    return pl.pallas_call(
        copies_kernel,
        out_shape=jax.ShapeDtypeStruct((16, PIECE, LANES), BF),
        grid=(1,),
        in_specs=[full((PIECE, LANES))],
        out_specs=full((16, PIECE, LANES)),
        compiler_params=pltpu.CompilerParams(vmem_limit_bytes=VMEM),
        cost_estimate=cost(1),
        name="plane_copies",
    )(part)


def reduce_gradients(keep, send, late):
    mine = (keep.astype(F32) + ch_swap(send, 1).astype(F32)).astype(BF)
    mine = plane_exchange(mine.reshape(16, PIECE, LANES))
    wire = plane_total(mine, late)
    part = (
        (wire.astype(F32) + lon_swap(wire, 16).astype(F32))
        + (ch_swap(wire, 2).astype(F32) + both_swap(wire).astype(F32))
    ).astype(BF)
    return plane_exchange(plane_copies(part)).reshape(WIRE, LANES)


def finish_kernel(core_ref, own, other, pad, grad_in, grad_out, held):
    core = core_ref[0]
    for wire, slot in ((own, core), (other, 1 - core)):
        for t in range(3):
            held[slot, :, t * LANES : (t + 1) * LANES] = wire[t * HID : (t + 1) * HID, :]
        rest = wire[3 * HID : 3 * HID + 400, :]
        for q in range(4):
            held[slot, q * 400 : (q + 1) * 400, 3 * LANES :] = rest[:, q * 32 : (q + 1) * 32]
    factor = 1.0 / math.sqrt(ROWS * LANES * 32)
    grad_in[...] = dotg(pad[...], held[0], 1, 1) * factor
    grad_out[...] = dotg(pad[...], held[1], 1, 1) * factor


def finish(core, own, other, pad):
    return pl.pallas_call(
        finish_kernel,
        out_shape=[
            jax.ShapeDtypeStruct((C, HID), F32),
            jax.ShapeDtypeStruct((C, HID), F32),
        ],
        grid=(1,),
        in_specs=[
            pl.BlockSpec(memory_space=pltpu.SMEM),
            full((WIRE, LANES)),
            full((WIRE, LANES)),
            full((C, 4 * CP)),
        ],
        out_specs=[full((C, HID))] * 2,
        scratch_shapes=[pltpu.VMEM((2, HID, 4 * CP), BF)],
        compiler_params=pltpu.CompilerParams(vmem_limit_bytes=VMEM),
        cost_estimate=cost(6),
        name="finish",
    )(core, own, other, pad)


def both_swap(x):
    return lax.ppermute(x, ("lon", "ch"), [(i, i ^ (16 * 4 + 2)) for i in range(128)])


def body(
    ocean_state,
    sea_mask,
    kernel,
    conv_bias,
    norm_gain,
    norm_bias,
    weight_in,
    bias_in,
    weight_out,
    bias_out,
    layer_scale,
    cotangent,
):
    ch = lax.axis_index("ch")
    me = ch.reshape(1)
    core = (ch & 1).reshape(1)
    scale = jnp.pad(layer_scale, (0, CP - LC)).reshape(CP, 1)

    head, tail = edge_picks()
    state2d = ocean_state.reshape(LC * ROWS, LANES)
    sent = {}
    first = edge(state2d, head)
    sent[2] = branch_share(me, cotangent, sea_mask, scale, 2, (first,))
    last = edge(state2d, tail, (sent[2],))
    sent[3] = branch_share(me, cotangent, sea_mask, scale, 3, (last,))
    sent[1] = branch_share(me, cotangent, sea_mask, scale, 1, (sent[3],))
    sent[0] = branch_share(me, cotangent, sea_mask, scale, 0, (sent[1],))
    gs = [sent[0]] + [ch_swap(sent[k], k) for k in (1, 2, 3)]

    chan = jnp.arange(C)
    padded = jnp.arange(4 * CP)
    pad = ((chan // LC * CP + chan % LC)[:, None] == padded[None, :]).astype(BF)
    pad_own = (((chan // LC ^ ch) * CP + chan % LC)[:, None] == padded[None, :]).astype(BF)
    win, win_t, wout_t, wout = padded_weights(weight_in, weight_out.T, pad_own)
    vec = jnp.stack([norm_gain, norm_bias, bias_out], 1).reshape(4, LC, 3)
    vec = jnp.pad(vec, ((0, 0), (0, CP - LC), (0, 0)))
    vec = jnp.concatenate([lax.dynamic_index_in_dim(vec, ch ^ k, 0, False) for k in range(4)], 0)

    state_rim = rims(first, last).reshape(LC, ROWS, LANES)
    bias = jnp.broadcast_to(conv_bias[:, None, None], (LC, 1, LANES))
    conv = conv_forward(me, ocean_state, state_rim, tap_patterns(kernel), bias)
    xs = [
        [conv[4 * half]] + [ch_swap(conv[4 * half + k], k) for k in (1, 2, 3)] for half in (0, 1)
    ]

    weights = (win_t, win, wout, wout_t)
    bias_rows = bias_in.reshape(HID, 1)
    grad_a, branch_a, (hid_a, cells_a) = mlp(0, me, core, xs[0], gs, weights, vec, bias_rows)
    saved = (hid_a, cells_a.reshape(2, 4 * CP, 2 * CELLS))
    grad_b, branch_b, (keep, send) = mlp(
        1, me, core, xs[1], gs, weights, vec, bias_rows, saved, grad_a[:1]
    )
    grad_a = [grad_a[0]] + [ch_swap(grad_a[k], k) for k in (1, 2, 3)]
    branch_a = [branch_a[0]] + [ch_swap(branch_a[k], k) for k in (1, 2, 3)]
    keep, send, grad_a, branch_a = lax.optimization_barrier((keep, send, grad_a, branch_a))
    grad_b = [grad_b[0]] + [ch_swap(grad_b[k], k) for k in (1, 2, 3)]
    branch_b = [branch_b[0]] + [ch_swap(branch_b[k], k) for k in (1, 2, 3)]
    grads, branches = grad_a + grad_b, branch_a + branch_b

    picks = jnp.concatenate([head, tail], 0)
    grad_rims = piece_rims(picks, *piece_edges(picks, grads))
    own = reduce_gradients(keep, send, grads[5:] + branches[5:])

    grad_state = conv_backward(
        me,
        grads,
        grad_rims,
        tap_patterns(kernel[:, ::-1]),
        cotangent,
        sea_mask,
    )
    updated = update(me, branches, ocean_state, sea_mask, scale)
    own, grad_state, updated = lax.optimization_barrier((own, grad_state, updated))
    grad_in, grad_out = finish(core, own, ch_swap(own, 1), pad)
    return updated, grad_state, grad_in, grad_out.T


def solution(mesh):
    return jax.shard_map(
        body,
        mesh=mesh,
        in_specs=(
            P("ch", None, "lon"),
            P(None, "lon"),
            P("ch", None),
            P("ch"),
            P(),
            P(),
            P(),
            P(),
            P(),
            P(),
            P("ch"),
            P("ch", None, "lon"),
        ),
        out_specs=(P("ch", None, "lon"), P("ch", None, "lon"), P(), P()),
        check_vma=False,
    )
```

profile of v0, /device:TPU:1, one launch (start us, length us, event | category | flops | bytes accessed | tf_op | source)
XLA Modules:
  0.0 214.8 jit_solution(17061349097851095092)
XLA Ops:
  1.3 2.6 %edge.2.refs_0_ = bf16[8,6400]{1,0:T(8,128)(2,1)} custom-call(bf16[6400,128]{1,0:T(8,128)(2,1)} %bitcast.24, bf16[8,128]{1,0:T(8,128)(2,1)} %get-tuple-element.106.pick), custom_call_target="tpu_custom_call" | custom-call | bytes 3300000 | tf_op jit(solution)/shard_map/edge/pallas_call | solution.py:433
  4.0 9.5 %collective-permute-start = (bf16[8,6400]{1,0:T(8,128)(2,1)}, bf16[8,6400]{1,0:T(8,128)(2,1)S(1)}, u32[]{:S(2)}, u32[]{:S(2)}) collective-permute-start(bf16[8,6400]{1,0:T(8,128)(2,1)} %edge.2.refs_0_), channel_id=1, source_target_pairs={{0,124},{4,0},{8,4},{12,8},{16,12},{20,16},{24,20},{28,24},{32,28}... | collective-permute-start | bytes 307208 | tf_op jit(solution)/shard_map/ppermute | solution.py:48
  34.2 2.7 %convolution_convert_fusion = bf16[6400,128]{1,0:T(8,128)(2,1)} fusion(bf16[8,6400]{1,0:T(8,128)(2,1)} %collective-permute-done.1, bf16[8,6400]{1,0:T(8,128)(2,1)S(1)} %collective-permute-done, bf16[8,128]{1,0:T(8,128)(2,1)} %get-tuple-element.107.pick, bf16[8,128]{1,0:T(8,128)(2,1)} %get-tuple-element.106.pick), kind=kOutput, calls=%fused_computation | convolution fusion | flops 27451392 | bytes 1847296 | tf_op jit(solution)/shard_map/dot_general | solution.py:32
  37.7 11.9 %conv_forward.1 = (bf16[8,104,128]{2,1,0:T(8,128)(2,1)}, bf16[8,104,128]{2,1,0:T(8,128)(2,1)}, bf16[8,104,128]{2,1,0:T(8,128)(2,1)}, bf16[8,104,128]{2,1,0:T(8,1...) custom-call(s32[1]{0:T(128)} %bitcast.me_ref, ...), custom_call_target="tpu_custom_call" | custom-call | bytes 29700000 | tf_op jit(solution)/shard_map/conv_forward/pallas_call | solution.py:131
  52.7 4.8 %collective-permute-done.10.refs_3_ = bf16[8,104,128]{2,1,0:T(8,128)(2,1)} collective-permute-done((bf16[8,104,128]{2,1,0:T(8,128)(2,1)}, bf16[8,104,128]{2,1,0:T(8,128)(2,1)}, u32[]{:S(2)}, u32[]{:S(2)}) %collective-permute-start.10) | collective-permute-done | bytes 213024 | tf_op jit(solution)/shard_map/ppermute | solution.py:44
  58.7 5.5 %padded_weights.1 = (bf16[416,1600]{1,0:T(8,128)(2,1)}, bf16[1600,416]{1,0:T(8,128)(2,1)}, bf16[416,1600]{1,0:T(8,128)(2,1)}, bf16[1600,416]{1,0:T(8,128)(2,1)}) custom-call(bf16[400,1600]{1,0:T(8,128)(2,1)} %one.1, bf16[400,1600]{1,0:T(8,128)(2,1)} %bitcast.28, bf16[400,416]{1,0:T(8,128)(2,1)} %fusion.pad), custom_call_target="tpu_custom_call" | custom-call | bytes 16500000 | tf_op jit(solution)/shard_map/padded_weights/pallas_call | solution.py:397
  68.1 14.9 %mlp_a.1 = (bf16[8,104,128]{2,1,0:T(8,128)(2,1)}, bf16[8,104,128]{2,1,0:T(8,128)(2,1)}, bf16[8,104,128]{2,1,0:T(8,128)(2,1)}, bf16[8,104,128]{2,1,0:T(8,128)(2,1...) custom-call(s32[1]{0:T(128)} %bitcast.me_ref, ...), custom_call_target="tpu_custom_call" | custom-call | bytes 46200000 | tf_op jit(solution)/shard_map/mlp_a/pallas_call | solution.py:322
  87.4 22.1 %mlp_b.1 = (bf16[8,104,128]{2,1,0:T(8,128)(2,1)}, bf16[8,104,128]{2,1,0:T(8,128)(2,1)}, bf16[8,104,128]{2,1,0:T(8,128)(2,1)}, bf16[8,104,128]{2,1,0:T(8,128)(2,1...) custom-call(s32[1]{0:T(128)} %bitcast.me_ref, ...), custom_call_target="tpu_custom_call" | custom-call | bytes 72600000 | tf_op jit(solution)/shard_map/mlp_b/pallas_call | solution.py:322
  109.7 3.3 %collective-permute-done.17 = bf16[5248,128]{1,0:T(8,128)(2,1)S(1)} collective-permute-done((bf16[5248,128]{1,0:T(8,128)(2,1)}, bf16[5248,128]{1,0:T(8,128)(2,1)S(1)}, u32[]{:S(2)}, u32[]{:S(2)}) %collective-permute-start.17) | collective-permute-done | bytes 1343520 | tf_op jit(solution)/shard_map/ppermute | solution.py:44
  112.9 2.7 %add_convert_fusion = bf16[5248,128]{1,0:T(8,128)(2,1)} fusion(bf16[5248,128]{1,0:T(8,128)(2,1)S(1)} %collective-permute-done.17, bf16[5248,128]{1,0:T(8,128)(2,1)} %get-tuple-element.77), kind=kLoop, calls=%fused_computation.1 | loop fusion | flops 2686976 | bytes 4030464 | tf_op jit(solution)/shard_map/convert_element_type | solution.py:541
  115.8 7.6 %all-to-all-start = ((bf16[16,328,128]{2,1,0:T(8,128)(2,1)}), bf16[16,328,128]{2,1,0:T(8,128)(2,1)}, u32[]{:S(2)}, u32[]{:S(2)}) async-start(bf16[16,328,128]{2,1,0:T(8,128)(2,1)} %bitcast.8), calls=%async_computation | async-start | bytes 2686976 | tf_op jit(solution)/shard_map/all_to_all | solution.py:499
  127.9 3.0 %collective-permute-done.22.refs_5_.refs_6_ = bf16[8,104,128]{2,1,0:T(8,128)(2,1)S(1)} collective-permute-done((bf16[8,104,128]{2,1,0:T(8,128)(2,1)S(1)}, bf16[8,104,128]{2,1,0:T(8,128)(2,1)S(1)}, u32[]{:S(2)}, u32[]{:S(2)}) %collective-permute-start.22) | collective-permute-done | bytes 213024 | tf_op jit(solution)/shard_map/ppermute | solution.py:44
  130.8 5.5 %collective-permute-done.23.refs_6_.refs_7_ = bf16[8,104,128]{2,1,0:T(8,128)(2,1)S(1)} collective-permute-done((bf16[8,104,128]{2,1,0:T(8,128)(2,1)S(1)}, bf16[8,104,128]{2,1,0:T(8,128)(2,1)S(1)}, u32[]{:S(2)}, u32[]{:S(2)}) %collective-permute-start.23) | collective-permute-done | bytes 213024 | tf_op jit(solution)/shard_map/ppermute | solution.py:44
  136.4 3.6 %collective-permute-done.19.refs_2_.refs_6_ = bf16[8,104,128]{2,1,0:T(8,128)(2,1)S(1)} collective-permute-done((bf16[8,104,128]{2,1,0:T(8,128)(2,1)S(1)}, bf16[8,104,128]{2,1,0:T(8,128)(2,1)S(1)}, u32[]{:S(2)}, u32[]{:S(2)}) %collective-permute-start.19) | collective-permute-done | bytes 213024 | tf_op jit(solution)/shard_map/ppermute | solution.py:44
  140.0 5.0 %collective-permute-done.20.refs_3_.refs_7_ = bf16[8,104,128]{2,1,0:T(8,128)(2,1)S(1)} collective-permute-done((bf16[8,104,128]{2,1,0:T(8,128)(2,1)S(1)}, bf16[8,104,128]{2,1,0:T(8,128)(2,1)S(1)}, u32[]{:S(2)}, u32[]{:S(2)}) %collective-permute-start.20) | collective-permute-done | bytes 213024 | tf_op jit(solution)/shard_map/ppermute | solution.py:44
  158.9 6.5 %all-to-all-start.1 = ((bf16[16,328,128]{2,1,0:T(8,128)(2,1)}), bf16[16,328,128]{2,1,0:T(8,128)(2,1)}, u32[]{:S(2)}, u32[]{:S(2)}) async-start(bf16[16,328,128]{2,1,0:T(8,128)(2,1)} %plane_copies.1), calls=%async_computation.1 | async-start | bytes 2686976 | tf_op jit(solution)/shard_map/all_to_all | solution.py:499
  166.1 2.8 %piece_edges.1 = (bf16[8,8,832]{2,1,0:T(8,128)(2,1)}, bf16[8,8,832]{2,1,0:T(8,128)(2,1)}) custom-call(bf16[16,128]{1,0:T(8,128)(2,1)} %pad_maximum_fusion.1.pick, bf16[8,104,128]{2,1,0:T(8,128)(2,1)} %get-tuple-element.85.refs_16_.refs_0_, bf16[8,104,128]{2,1,0:T(8,128)(2,1)} %collective-permute-done.11.refs_1_, bf16[8,104,128]{2,1,0:T(8,128)(2,1)} %copy-done.8, ...), custom_call_target="tpu_custom_call" | custom-call | bytes 6600000 | tf_op jit(solution)/shard_map/piece_edges/pallas_call | solution.py:459
  168.9 7.2 %collective-permute-start.27 = (bf16[8,8,832]{2,1,0:T(8,128)(2,1)}, bf16[8,8,832]{2,1,0:T(8,128)(2,1)S(1)}, u32[]{:S(2)}, u32[]{:S(2)}) collective-permute-start(bf16[8,8,832]{2,1,0:T(8,128)(2,1)} %get-tuple-element.90), channel_id=1, source_target_pairs={{0,124},{4,0},{8,4},{12,8},{16,12},{20,16},{24,20},{28,24},{32,28}... | collective-permute-start | bytes 319496 | tf_op jit(solution)/shard_map/ppermute | solution.py:48
  177.0 5.1 %update.1 = bf16[100,64,128]{2,1,0:T(8,128)(2,1)} custom-call(s32[1]{0:T(128)} %bitcast.me_ref, bf16[8,104,128]{2,1,0:T(8,128)(2,1)} %get-tuple-element.92.refs_0_, bf16[8,104,128]{2,1,0:T(8,128)(2,1)} %copy-done.10, bf16[8,104,128]{2,1,0:T(8,128)(2,1)} %copy-done.11, bf16[8,104,128]{2,1,0:T(8,128)(2,1)} %collective-permute-done.16.refs_3_, ...), custom_call_target="tpu_custom_call" | custom-call | bytes 14520000 | tf_op jit(solution)/shard_map/update/pallas_call | solution.py:366
  182.6 3.1 %collective-permute-done.28.last = bf16[8,8,832]{2,1,0:T(8,128)(2,1)S(1)} collective-permute-done((bf16[8,8,832]{2,1,0:T(8,128)(2,1)}, bf16[8,8,832]{2,1,0:T(8,128)(2,1)S(1)}, u32[]{:S(2)}, u32[]{:S(2)}) %collective-permute-start.28) | collective-permute-done | bytes 106528 | tf_op jit(solution)/shard_map/ppermute | solution.py:48
  186.4 2.8 %piece_rims.1.refs_8_ = bf16[8,8,104,128]{3,2,1,0:T(8,128)(2,1)} custom-call(bf16[16,128]{1,0:T(8,128)(2,1)} %pad_maximum_fusion.1.pick, bf16[8,8,832]{2,1,0:T(8,128)(2,1)} %copy-done.13, bf16[8,8,832]{2,1,0:T(8,128)(2,1)} %copy-done.14), custom_call_target="tpu_custom_call" | custom-call | bytes 6600000 | tf_op jit(solution)/shard_map/piece_rims/pallas_call | solution.py:478
  189.2 13.2 %conv_backward.1 = bf16[100,64,128]{2,1,0:T(8,128)(2,1)} custom-call(s32[1]{0:T(128)} %bitcast.me_ref, bf16[8,104,128]{2,1,0:T(8,128)(2,1)} %get-tuple-element.85.refs_16_.refs_0_, bf16[8,104,128]{2,1,0:T(8,128)(2,1)} %collective-permute-done.11.refs_1_, bf16[8,104,128]{2,1,0:T(8,128)(2,1)} %copy-done.8, bf16[8,104,128]{2,1,0:T(8,128)(2,1)} %copy-done.9, ...), custom_call_target="tpu_custom_call" | custom-call | bytes 33000000 | tf_op jit(solution)/shard_map/conv_backward/pallas_call | solution.py:171
  202.4 3.5 %collective-permute-start.29 = (bf16[5248,128]{1,0:T(8,128)(2,1)}, bf16[5248,128]{1,0:T(8,128)(2,1)}, u32[]{:S(2)}, u32[]{:S(2)}) collective-permute-start(bf16[5248,128]{1,0:T(8,128)(2,1)} %bitcast.9.own), channel_id=1, source_target_pairs={{0,1},{1,0},{2,3},{3,2},{4,5},{5,4},{6,7},{7,6},{8,9},{9,8},{10,11... | collective-permute-start | bytes 4030472 | tf_op jit(solution)/shard_map/ppermute | solution.py:44
  208.9 5.8 %finish.1 = (f32[400,1600]{1,0:T(8,128)}, f32[400,1600]{1,0:T(8,128)}) custom-call(s32[1]{0:T(128)} %bitcast.1.core_ref, bf16[5248,128]{1,0:T(8,128)(2,1)} %bitcast.9.own, bf16[5248,128]{1,0:T(8,128)(2,1)} %collective-permute-done.29.other, bf16[400,416]{1,0:T(8,128)(2,1)} %fusion.1.pad), custom_call_target="tpu_custom_call" | custom-call | bytes 19800000 | tf_op jit(solution)/shard_map/finish/pallas_call | solution.py:565
  (151 shorter events, 58.9 us)
Async XLA Ops:
  4.0 30.2 %collective-permute-start = (bf16[8,6400]{1,0:T(8,128)(2,1)}, bf16[8,6400]{1,0:T(8,128)(2,1)S(1)}, u32[]{:S(2)}, u32[]{:S(2)}) collective-permute-start(bf16[8,6400]{1,0:T(8,128)(2,1)} %edge.2.refs_0_), channel_id=1, source_target_pairs={{0,124},{4,0},{8,4},{12,8},{16,12},{20,16},{24,20},{28,24},{32,28}... | collective-permute-start | bytes 307208 | tf_op jit(solution)/shard_map/ppermute | solution.py:48
  16.3 50.8 %collective-permute-start.6 = (bf16[16,104,128]{2,1,0:T(8,128)(2,1)}, bf16[16,104,128]{2,1,0:T(8,128)(2,1)S(1)}, u32[]{:S(2)}, u32[]{:S(2)}) collective-permute-start(bf16[16,104,128]{2,1,0:T(8,128)(2,1)} %branch_share.4.refs_0_), channel_id=1, source_target_pairs={{0,2},{1,3},{2,0},{3,1},{4,6},{5,7},{6,4},{7,5},{8,10},{9,11},{10,... | collective-permute-start | bytes 1277960 | tf_op jit(solution)/shard_map/ppermute | solution.py:44
  19.3 14.9 %collective-permute-start.1 = (bf16[8,6400]{1,0:T(8,128)(2,1)}, bf16[8,6400]{1,0:T(8,128)(2,1)}, u32[]{:S(2)}, u32[]{:S(2)}) collective-permute-start(bf16[8,6400]{1,0:T(8,128)(2,1)} %edge.3.refs_0_), channel_id=1, source_target_pairs={{0,4},{4,8},{8,12},{12,16},{16,20},{20,24},{24,28},{28,32},{32,36}... | collective-permute-start | bytes 307208 | tf_op jit(solution)/shard_map/ppermute | solution.py:48
  21.5 45.7 %collective-permute-start.7 = (bf16[16,104,128]{2,1,0:T(8,128)(2,1)}, bf16[16,104,128]{2,1,0:T(8,128)(2,1)S(1)}, u32[]{:S(2)}, u32[]{:S(2)}) collective-permute-start(bf16[16,104,128]{2,1,0:T(8,128)(2,1)} %branch_share.5.refs_0_), channel_id=1, source_target_pairs={{0,3},{1,2},{2,1},{3,0},{4,7},{5,6},{6,5},{7,4},{8,11},{9,10},{10,... | collective-permute-start | bytes 1277960 | tf_op jit(solution)/shard_map/ppermute | solution.py:44
  25.9 40.2 %collective-permute-start.5 = (bf16[16,104,128]{2,1,0:T(8,128)(2,1)}, bf16[16,104,128]{2,1,0:T(8,128)(2,1)}, u32[]{:S(2)}, u32[]{:S(2)}) collective-permute-start(bf16[16,104,128]{2,1,0:T(8,128)(2,1)} %branch_share.6.refs_0_), channel_id=1, source_target_pairs={{0,1},{1,0},{2,3},{3,2},{4,5},{5,4},{6,7},{7,6},{8,9},{9,8},{10,11... | collective-permute-start | bytes 1277960 | tf_op jit(solution)/shard_map/ppermute | solution.py:44
  49.6 7.9 %collective-permute-start.10 = (bf16[8,104,128]{2,1,0:T(8,128)(2,1)}, bf16[8,104,128]{2,1,0:T(8,128)(2,1)}, u32[]{:S(2)}, u32[]{:S(2)}) collective-permute-start(bf16[8,104,128]{2,1,0:T(8,128)(2,1)} %get-tuple-element.64), channel_id=1, source_target_pairs={{0,3},{1,2},{2,1},{3,0},{4,7},{5,6},{6,5},{7,4},{8,11},{9,10},{10,... | collective-permute-start | bytes 638984 | tf_op jit(solution)/shard_map/ppermute | solution.py:44
  52.6 11.7 %collective-permute-start.8 = (bf16[8,104,128]{2,1,0:T(8,128)(2,1)}, bf16[8,104,128]{2,1,0:T(8,128)(2,1)}, u32[]{:S(2)}, u32[]{:S(2)}) collective-permute-start(bf16[8,104,128]{2,1,0:T(8,128)(2,1)} %get-tuple-element.62), channel_id=1, source_target_pairs={{0,1},{1,0},{2,3},{3,2},{4,5},{5,4},{6,7},{7,6},{8,9},{9,8},{10,11... | collective-permute-start | bytes 638984 | tf_op jit(solution)/shard_map/ppermute | solution.py:44
  57.5 7.4 %collective-permute-start.9 = (bf16[8,104,128]{2,1,0:T(8,128)(2,1)}, bf16[8,104,128]{2,1,0:T(8,128)(2,1)}, u32[]{:S(2)}, u32[]{:S(2)}) collective-permute-start(bf16[8,104,128]{2,1,0:T(8,128)(2,1)} %get-tuple-element.63), channel_id=1, source_target_pairs={{0,2},{1,3},{2,0},{3,1},{4,6},{5,7},{6,4},{7,5},{8,10},{9,11},{10,... | collective-permute-start | bytes 638984 | tf_op jit(solution)/shard_map/ppermute | solution.py:44
  64.3 19.6 %collective-permute-start.2 = (bf16[8,104,128]{2,1,0:T(8,128)(2,1)}, bf16[8,104,128]{2,1,0:T(8,128)(2,1)}, u32[]{:S(2)}, u32[]{:S(2)}) collective-permute-start(bf16[8,104,128]{2,1,0:T(8,128)(2,1)} %get-tuple-element.54), channel_id=1, source_target_pairs={{0,1},{1,0},{2,3},{3,2},{4,5},{5,4},{6,7},{7,6},{8,9},{9,8},{10,11... | collective-permute-start | bytes 638984 | tf_op jit(solution)/shard_map/ppermute | solution.py:44
  64.9 20.3 %collective-permute-start.3 = (bf16[8,104,128]{2,1,0:T(8,128)(2,1)}, bf16[8,104,128]{2,1,0:T(8,128)(2,1)}, u32[]{:S(2)}, u32[]{:S(2)}) collective-permute-start(bf16[8,104,128]{2,1,0:T(8,128)(2,1)} %get-tuple-element.55), channel_id=1, source_target_pairs={{0,2},{1,3},{2,0},{3,1},{4,6},{5,7},{6,4},{7,5},{8,10},{9,11},{10,... | collective-permute-start | bytes 638984 | tf_op jit(solution)/shard_map/ppermute | solution.py:44
  66.1 19.1 %collective-permute-start.4 = (bf16[8,104,128]{2,1,0:T(8,128)(2,1)}, bf16[8,104,128]{2,1,0:T(8,128)(2,1)}, u32[]{:S(2)}, u32[]{:S(2)}) collective-permute-start(bf16[8,104,128]{2,1,0:T(8,128)(2,1)} %get-tuple-element.56), channel_id=1, source_target_pairs={{0,3},{1,2},{2,1},{3,0},{4,7},{5,6},{6,5},{7,4},{8,11},{9,10},{10,... | collective-permute-start | bytes 638984 | tf_op jit(solution)/shard_map/ppermute | solution.py:44
  83.1 26.4 %collective-permute-start.12 = (bf16[8,104,128]{2,1,0:T(8,128)(2,1)}, bf16[8,104,128]{2,1,0:T(8,128)(2,1)S(1)}, u32[]{:S(2)}, u32[]{:S(2)}) collective-permute-start(bf16[8,104,128]{2,1,0:T(8,128)(2,1)} %get-tuple-element.71), channel_id=1, source_target_pairs={{0,2},{1,3},{2,0},{3,1},{4,6},{5,7},{6,4},{7,5},{8,10},{9,11},{10,... | collective-permute-start | bytes 638984 | tf_op jit(solution)/shard_map/ppermute | solution.py:44
  83.9 25.6 %collective-permute-start.13 = (bf16[8,104,128]{2,1,0:T(8,128)(2,1)}, bf16[8,104,128]{2,1,0:T(8,128)(2,1)S(1)}, u32[]{:S(2)}, u32[]{:S(2)}) collective-permute-start(bf16[8,104,128]{2,1,0:T(8,128)(2,1)} %get-tuple-element.72), channel_id=1, source_target_pairs={{0,3},{1,2},{2,1},{3,0},{4,7},{5,6},{6,5},{7,4},{8,11},{9,10},{10,... | collective-permute-start | bytes 638984 | tf_op jit(solution)/shard_map/ppermute | solution.py:44
  85.2 24.3 %collective-permute-start.14 = (bf16[8,104,128]{2,1,0:T(8,128)(2,1)}, bf16[8,104,128]{2,1,0:T(8,128)(2,1)S(1)}, u32[]{:S(2)}, u32[]{:S(2)}) collective-permute-start(bf16[8,104,128]{2,1,0:T(8,128)(2,1)} %get-tuple-element.74), channel_id=1, source_target_pairs={{0,1},{1,0},{2,3},{3,2},{4,5},{5,4},{6,7},{7,6},{8,9},{9,8},{10,11... | collective-permute-start | bytes 638984 | tf_op jit(solution)/shard_map/ppermute | solution.py:44
  85.2 24.3 %collective-permute-start.15 = (bf16[8,104,128]{2,1,0:T(8,128)(2,1)}, bf16[8,104,128]{2,1,0:T(8,128)(2,1)S(1)}, u32[]{:S(2)}, u32[]{:S(2)}) collective-permute-start(bf16[8,104,128]{2,1,0:T(8,128)(2,1)} %get-tuple-element.75), channel_id=1, source_target_pairs={{0,2},{1,3},{2,0},{3,1},{4,6},{5,7},{6,4},{7,5},{8,10},{9,11},{10,... | collective-permute-start | bytes 638984 | tf_op jit(solution)/shard_map/ppermute | solution.py:44
  86.0 23.6 %collective-permute-start.16 = (bf16[8,104,128]{2,1,0:T(8,128)(2,1)}, bf16[8,104,128]{2,1,0:T(8,128)(2,1)}, u32[]{:S(2)}, u32[]{:S(2)}) collective-permute-start(bf16[8,104,128]{2,1,0:T(8,128)(2,1)} %get-tuple-element.76), channel_id=1, source_target_pairs={{0,3},{1,2},{2,1},{3,0},{4,7},{5,6},{6,5},{7,4},{8,11},{9,10},{10,... | collective-permute-start | bytes 638984 | tf_op jit(solution)/shard_map/ppermute | solution.py:44
  115.8 29.3 %all-to-all-start = ((bf16[16,328,128]{2,1,0:T(8,128)(2,1)}), bf16[16,328,128]{2,1,0:T(8,128)(2,1)}, u32[]{:S(2)}, u32[]{:S(2)}) async-start(bf16[16,328,128]{2,1,0:T(8,128)(2,1)} %bitcast.8), calls=%async_computation | async-start | bytes 2686976 | tf_op jit(solution)/shard_map/all_to_all | solution.py:499
  124.7 11.6 %collective-permute-start.23 = (bf16[8,104,128]{2,1,0:T(8,128)(2,1)S(1)}, bf16[8,104,128]{2,1,0:T(8,128)(2,1)S(1)}, u32[]{:S(2)}, u32[]{:S(2)}) collective-permute-start(bf16[8,104,128]{2,1,0:T(8,128)(2,1)S(1)} %copy-done.28), channel_id=1, source_target_pairs={{0,3},{1,2},{2,1},{3,0},{4,7},{5,6},{6,5},{7,4},{8,11},{9,10},{10,... | collective-permute-start | bytes 638984 | tf_op jit(solution)/shard_map/ppermute | solution.py:44
  125.7 10.7 %collective-permute-start.18 = (bf16[8,104,128]{2,1,0:T(8,128)(2,1)S(1)}, bf16[8,104,128]{2,1,0:T(8,128)(2,1)S(1)}, u32[]{:S(2)}, u32[]{:S(2)}) collective-permute-start(bf16[8,104,128]{2,1,0:T(8,128)(2,1)S(1)} %copy-done.27), channel_id=1, source_target_pairs={{0,1},{1,0},{2,3},{3,2},{4,5},{5,4},{6,7},{7,6},{8,9},{9,8},{10,11... | collective-permute-start | bytes 638984 | tf_op jit(solution)/shard_map/ppermute | solution.py:44
  125.8 14.2 %collective-permute-start.19 = (bf16[8,104,128]{2,1,0:T(8,128)(2,1)S(1)}, bf16[8,104,128]{2,1,0:T(8,128)(2,1)S(1)}, u32[]{:S(2)}, u32[]{:S(2)}) collective-permute-start(bf16[8,104,128]{2,1,0:T(8,128)(2,1)S(1)} %copy-done.26), channel_id=1, source_target_pairs={{0,2},{1,3},{2,0},{3,1},{4,6},{5,7},{6,4},{7,5},{8,10},{9,11},{10,... | collective-permute-start | bytes 638984 | tf_op jit(solution)/shard_map/ppermute | solution.py:44
  126.6 18.4 %collective-permute-start.20 = (bf16[8,104,128]{2,1,0:T(8,128)(2,1)S(1)}, bf16[8,104,128]{2,1,0:T(8,128)(2,1)S(1)}, u32[]{:S(2)}, u32[]{:S(2)}) collective-permute-start(bf16[8,104,128]{2,1,0:T(8,128)(2,1)S(1)} %copy-done.25), channel_id=1, source_target_pairs={{0,3},{1,2},{2,1},{3,0},{4,7},{5,6},{6,5},{7,4},{8,11},{9,10},{10,... | collective-permute-start | bytes 638984 | tf_op jit(solution)/shard_map/ppermute | solution.py:44
  158.9 43.4 %all-to-all-start.1 = ((bf16[16,328,128]{2,1,0:T(8,128)(2,1)}), bf16[16,328,128]{2,1,0:T(8,128)(2,1)}, u32[]{:S(2)}, u32[]{:S(2)}) async-start(bf16[16,328,128]{2,1,0:T(8,128)(2,1)} %plane_copies.1), calls=%async_computation.1 | async-start | bytes 2686976 | tf_op jit(solution)/shard_map/all_to_all | solution.py:499
  168.9 13.7 %collective-permute-start.27 = (bf16[8,8,832]{2,1,0:T(8,128)(2,1)}, bf16[8,8,832]{2,1,0:T(8,128)(2,1)S(1)}, u32[]{:S(2)}, u32[]{:S(2)}) collective-permute-start(bf16[8,8,832]{2,1,0:T(8,128)(2,1)} %get-tuple-element.90), channel_id=1, source_target_pairs={{0,124},{4,0},{8,4},{12,8},{16,12},{20,16},{24,20},{28,24},{32,28}... | collective-permute-start | bytes 319496 | tf_op jit(solution)/shard_map/ppermute | solution.py:48
  176.0 9.7 %collective-permute-start.28 = (bf16[8,8,832]{2,1,0:T(8,128)(2,1)}, bf16[8,8,832]{2,1,0:T(8,128)(2,1)S(1)}, u32[]{:S(2)}, u32[]{:S(2)}) collective-permute-start(bf16[8,8,832]{2,1,0:T(8,128)(2,1)} %get-tuple-element.91), channel_id=1, source_target_pairs={{0,4},{4,8},{8,12},{12,16},{16,20},{20,24},{24,28},{28,32},{32,36}... | collective-permute-start | bytes 319496 | tf_op jit(solution)/shard_map/ppermute | solution.py:48
  (40 other events, 291.5 us)
where the time goes:
time: 216 us; the launch traced here: 215 us
  Pallas kernels  102 us (47%)
  starting transfers between devices  53.1 us (25%)
  waiting for transfers between devices  35.2 us (16%)
  local copies, waits for them, and re-layouts  11.8 us (5%)
  other arithmetic  7.49 us (3%)
  matrix products  3.82 us (2%)
    pallas_call x2, Pallas kernels, mlp(): pl.pallas_call(functools.partial(mlp_kernel, half), out_shape=[jax.ShapeD...  37 us
    ppermute x24, waiting for transfers between devices, ch_swap(): return lax.ppermute(x, 'ch', [(i, i ^ k) for i in range(4)])  29.2 us
    ppermute x24, starting transfers between devices, ch_swap(): return lax.ppermute(x, 'ch', [(i, i ^ k) for i in range(4)])  19.1 us
    ppermute x4, starting transfers between devices, lon_shift(): return lax.ppermute(x, 'lon', [(i, (i + d) % 32) for i in range(32)])  16.7 us
    all_to_all x2, starting transfers between devices, plane_exchange(): return lax.all_to_all(pieces, 'lon', 0, 0, axis_index_groups=PLANES)  14.1 us
    pallas_call x1, Pallas kernels, conv_backward(): pl.pallas_call(backward_kernel, out_shape=jax.ShapeDtypeStruct((LC, ROWS,...  13.2 us
    pallas_call x1, Pallas kernels, conv_forward(): pl.pallas_call(forward_kernel, out_shape=[share] * 8, grid_spec=pltpu.Pre...  11.9 us
    pallas_call x4, Pallas kernels, branch_share(): pl.pallas_call(share_kernel, out_shape=jax.ShapeDtypeStruct((QR, CP, LANE...  8.62 us
  transfers between devices with their start and end apart: 32, of which 13 were waited for; matrix products, arithmetic and copies ran while one was open for 7% of the time, Pallas kernels for 42%

commit v1 on v0

--- a/solution.py
+++ b/solution.py
@@ -76,7 +76,7 @@
             + [pl.BlockSpec(memory_space=pl.ANY)] * len(after),
             out_specs=pl.BlockSpec((QR, CP, LANES), lambda i, me: (0, 0, 0)),
         ),
-        compiler_params=pltpu.CompilerParams(vmem_limit_bytes=VMEM),
+        compiler_params=pltpu.CompilerParams(vmem_limit_bytes=32 << 20),
         cost_estimate=cost(1.2),
         name="branch_share",
     )(me, cotangent, sea_mask, scale, *after)
@@ -143,7 +143,7 @@
             out_specs=[pl.BlockSpec((HR, GROUP, LANES), lambda i, me: (0, i, 0))] * 8,
             scratch_shapes=[pltpu.VMEM((4, QR, GROUP, LANES), F32)],
         ),
-        compiler_params=pltpu.CompilerParams(vmem_limit_bytes=VMEM),
+        compiler_params=pltpu.CompilerParams(vmem_limit_bytes=32 << 20),
         cost_estimate=cost(9),
         name="conv_forward",
     )(me, state, rim, pattern, bias)
@@ -184,7 +184,7 @@
             out_specs=pl.BlockSpec((GROUP, ROWS, LANES), lambda i, me: (i, 0, 0)),
             scratch_shapes=[pltpu.VMEM((4, QR, GROUP, LANES), F32)] * 2,
         ),
-        compiler_params=pltpu.CompilerParams(vmem_limit_bytes=VMEM),
+        compiler_params=pltpu.CompilerParams(vmem_limit_bytes=32 << 20),
         cost_estimate=cost(10),
         name="conv_backward",
     )(me, *pieces, rims, pattern, cotangent, sea_mask)
@@ -378,7 +378,7 @@
             out_specs=pl.BlockSpec((LC, QR, LANES), lambda i, me: (0, me[0] ^ i, 0)),
             scratch_shapes=[pltpu.VMEM((QR, CP, LANES), BF)],
         ),
-        compiler_params=pltpu.CompilerParams(vmem_limit_bytes=VMEM),
+        compiler_params=pltpu.CompilerParams(vmem_limit_bytes=32 << 20),
         cost_estimate=cost(4.4),
         name="update",
     )(me, *pieces, state, sea_mask, scale)
@@ -400,7 +400,7 @@
         grid=(1,),
         in_specs=[full((C, HID)), full((C, HID)), full((C, 4 * CP))],
         out_specs=[full(x.shape) for x in (flat, turned, flat, turned)],
-        compiler_params=pltpu.CompilerParams(vmem_limit_bytes=VMEM),
+        compiler_params=pltpu.CompilerParams(vmem_limit_bytes=32 << 20),
         cost_estimate=cost(5),
         name="padded_weights",
     )(one, two, pad)
@@ -437,7 +437,7 @@
         in_specs=[full(cells2d.shape), full(pick.shape)]
         + [pl.BlockSpec(memory_space=pl.ANY)] * len(after),
         out_specs=full((8, cells2d.shape[0])),
-        compiler_params=pltpu.CompilerParams(vmem_limit_bytes=VMEM),
+        compiler_params=pltpu.CompilerParams(vmem_limit_bytes=32 << 20),
         cost_estimate=cost(1),
         name="edge",
     )(cells2d, pick, *after)
@@ -462,7 +462,7 @@
         grid=(1,),
         in_specs=[pl.BlockSpec((16, LANES), lambda i: (0, 0))] + [half] * 8,
         out_specs=[whole] * 2,
-        compiler_params=pltpu.CompilerParams(vmem_limit_bytes=VMEM),
+        compiler_params=pltpu.CompilerParams(vmem_limit_bytes=32 << 20),
         cost_estimate=cost(2),
         name="piece_edges",
     )(picks, *pieces)
@@ -481,10 +481,10 @@
         grid=(1,),
         in_specs=[full((16, LANES)), full((8, 8, HR * CP)), full((8, 8, HR * CP))],
         out_specs=full((8, HR, CP, LANES)),
-        compiler_params=pltpu.CompilerParams(vmem_limit_bytes=VMEM),
+        compiler_params=pltpu.CompilerParams(vmem_limit_bytes=32 << 20),
         cost_estimate=cost(2),
         name="piece_rims",
-    )(picks, lon_shift(first, -1), lon_shift(last, 1))
+    )(picks, first, last)
 
 
 def rims(first, last):
@@ -513,7 +513,7 @@
         grid=(1,),
         in_specs=[full((16, PIECE, LANES))] + [pl.BlockSpec(memory_space=pl.ANY)] * len(after),
         out_specs=full((PIECE, LANES)),
-        compiler_params=pltpu.CompilerParams(vmem_limit_bytes=VMEM),
+        compiler_params=pltpu.CompilerParams(vmem_limit_bytes=32 << 20),
         cost_estimate=cost(1.2),
         name="plane_total",
     )(pieces, *after)
@@ -531,7 +531,7 @@
         grid=(1,),
         in_specs=[full((PIECE, LANES))],
         out_specs=full((16, PIECE, LANES)),
-        compiler_params=pltpu.CompilerParams(vmem_limit_bytes=VMEM),
+        compiler_params=pltpu.CompilerParams(vmem_limit_bytes=32 << 20),
         cost_estimate=cost(1),
         name="plane_copies",
     )(part)
@@ -577,7 +577,7 @@
         ],
         out_specs=[full((C, HID))] * 2,
         scratch_shapes=[pltpu.VMEM((2, HID, 4 * CP), BF)],
-        compiler_params=pltpu.CompilerParams(vmem_limit_bytes=VMEM),
+        compiler_params=pltpu.CompilerParams(vmem_limit_bytes=32 << 20),
         cost_estimate=cost(6),
         name="finish",
     )(core, own, other, pad)
@@ -644,12 +644,15 @@
     branch_a = [branch_a[0]] + [ch_swap(branch_a[k], k) for k in (1, 2, 3)]
     keep, send, grad_a, branch_a = lax.optimization_barrier((keep, send, grad_a, branch_a))
     grad_b = [grad_b[0]] + [ch_swap(grad_b[k], k) for k in (1, 2, 3)]
+    grads = grad_a + grad_b
+    picks = jnp.concatenate([head, tail], 0)
+    first, last = piece_edges(picks, grads)
+    first, last, branch_b = lax.optimization_barrier((first, last, branch_b))
     branch_b = [branch_b[0]] + [ch_swap(branch_b[k], k) for k in (1, 2, 3)]
-    grads, branches = grad_a + grad_b, branch_a + branch_b
-
-    picks = jnp.concatenate([head, tail], 0)
-    grad_rims = piece_rims(picks, *piece_edges(picks, grads))
-    own = reduce_gradients(keep, send, grads[5:] + branches[5:])
+    branches = branch_a + branch_b
+    from_right, from_left = lon_shift(first, -1), lon_shift(last, 1)
+    own = reduce_gradients(keep, send, [from_right, from_left] + branch_b[1:])
+    grad_rims = piece_rims(picks, from_right, from_left)
 
     grad_state = conv_backward(
         me,

time: 216 us -> 195 us (0.903)
  Pallas kernels: 102 us -> 75.2 us
  local copies, waits for them, and re-layouts: 11.8 us -> 26.9 us
  starting transfers between devices: 53.1 us -> 47.5 us
  other arithmetic: 7.49 us -> 3.28 us
    unnamed x66 -> x124, local copies, waits for them, and re-layouts: 3.5 us -> 21 us
    ppermute x4, waiting for transfers between devices: 3.62 us -> 14.2 us  [lon_shift(): return lax.ppermute(x, 'lon', [(i, (i + d) % 32) for i in range(32)])]
    ppermute x24, waiting for transfers between devices: 29.2 us -> 19.3 us  [ch_swap(): return lax.ppermute(x, 'ch', [(i, i ^ k) for i in range(4)])]
    all_to_all x2, starting transfers between devices: 14.1 us -> 7.56 us  [plane_exchange(): return lax.all_to_all(pieces, 'lon', 0, 0, axis_index_groups=PLANES)]
    pallas_call x4, Pallas kernels: 8.62 us -> 3.94 us  [branch_share(): pl.pallas_call(share_kernel, out_shape=jax.ShapeDtypeStruct((QR, CP, LANE...]
    pallas_call x1, Pallas kernels: 5.53 us -> 1.91 us  [padded_weights(): pl.pallas_call(weights_kernel, out_shape=[flat, turned, flat, turned], gr...]
    pallas_call x2, Pallas kernels: 5.26 us -> 1.73 us  [edge(): pl.pallas_call(edge_kernel, out_shape=jax.ShapeDtypeStruct((8, cells2d.sh...]
    pallas_call x1, Pallas kernels: 11.9 us -> 8.95 us  [conv_forward(): pl.pallas_call(forward_kernel, out_shape=[share] * 8, grid_spec=pltpu.Pre...]
  transfers between devices with their start and end apart: 32 -> 32, of which waited for: 13 -> 10; matrix products, arithmetic and copies ran while one was open for 7% -> 5% of each run, Pallas kernels for 42% -> 35%
where the time goes in v1:
time: 195 us
  Pallas kernels  75.2 us (39%)
  starting transfers between devices  47.5 us (24%)
  waiting for transfers between devices  37.1 us (19%)
  local copies, waits for them, and re-layouts  26.9 us (14%)
  matrix products  3.39 us (2%)
  other arithmetic  3.28 us (2%)
    pallas_call x2, Pallas kernels, mlp(): pl.pallas_call(functools.partial(mlp_kernel, half), out_shape=[jax.ShapeD...  37 us
    ppermute x24, starting transfers between devices, ch_swap(): return lax.ppermute(x, 'ch', [(i, i ^ k) for i in range(4)])  21.4 us
    unnamed x124, local copies, waits for them, and re-layouts  21 us
    ppermute x24, waiting for transfers between devices, ch_swap(): return lax.ppermute(x, 'ch', [(i, i ^ k) for i in range(4)])  19.3 us
    ppermute x4, starting transfers between devices, lon_shift(): return lax.ppermute(x, 'lon', [(i, (i + d) % 32) for i in range(32)])  15.7 us
    ppermute x4, waiting for transfers between devices, lon_shift(): return lax.ppermute(x, 'lon', [(i, (i + d) % 32) for i in range(32)])  14.2 us
    pallas_call x1, Pallas kernels, conv_backward(): pl.pallas_call(backward_kernel, out_shape=jax.ShapeDtypeStruct((LC, ROWS,...  10.2 us
    pallas_call x1, Pallas kernels, conv_forward(): pl.pallas_call(forward_kernel, out_shape=[share] * 8, grid_spec=pltpu.Pre...  8.95 us
  transfers between devices with their start and end apart: 32, of which 10 were waited for; matrix products, arithmetic and copies ran while one was open for 5% of the time, Pallas kernels for 35%

profile of v1, /device:TPU:1, one launch (start us, length us, event | category | flops | bytes accessed | tf_op | source)
XLA Modules:
  0.0 194.6 jit_solution(16352497905774843494)
XLA Ops:
  2.8 9.5 %collective-permute-start = (bf16[8,6400]{1,0:T(8,128)(2,1)S(1)}, bf16[8,6400]{1,0:T(8,128)(2,1)}, u32[]{:S(2)}, u32[]{:S(2)}) collective-permute-start(bf16[8,6400]{1,0:T(8,128)(2,1)S(1)} %edge.2.refs_0_), channel_id=1, source_target_pairs={{0,124},{4,0},{8,4},{12,8},{16,12},{20,16},{24,20},{28,24},{32,28}... | collective-permute-start | bytes 307208 | tf_op jit(solution)/shard_map/ppermute | solution.py:48
  17.8 2.4 %collective-permute-start.7 = (bf16[16,104,128]{2,1,0:T(8,128)(2,1)}, bf16[16,104,128]{2,1,0:T(8,128)(2,1)}, u32[]{:S(2)}, u32[]{:S(2)}) collective-permute-start(bf16[16,104,128]{2,1,0:T(8,128)(2,1)} %branch_share.5.refs_0_), channel_id=1, source_target_pairs={{0,3},{1,2},{2,1},{3,0},{4,7},{5,6},{6,5},{7,4},{8,11},{9,10},{10,... | collective-permute-start | bytes 1277960 | tf_op jit(solution)/shard_map/ppermute | solution.py:44
  24.8 2.8 %collective-permute-done.1 = bf16[8,6400]{1,0:T(8,128)(2,1)} collective-permute-done((bf16[8,6400]{1,0:T(8,128)(2,1)}, bf16[8,6400]{1,0:T(8,128)(2,1)}, u32[]{:S(2)}, u32[]{:S(2)}) %collective-permute-start.1) | collective-permute-done | bytes 102432 | tf_op jit(solution)/shard_map/ppermute | solution.py:48
  29.3 8.9 %conv_forward.1 = (bf16[8,104,128]{2,1,0:T(8,128)(2,1)S(1)}, bf16[8,104,128]{2,1,0:T(8,128)(2,1)S(1)}, bf16[8,104,128]{2,1,0:T(8,128)(2,1)S(1)}, bf16[8,104,128]...) custom-call(s32[1]{0:T(128)} %bitcast.me_ref, ...), custom_call_target="tpu_custom_call" | custom-call | bytes 29700000 | tf_op jit(solution)/shard_map/conv_forward/pallas_call | solution.py:131
  41.8 2.4 %collective-permute-start.10 = (bf16[8,104,128]{2,1,0:T(8,128)(2,1)}, bf16[8,104,128]{2,1,0:T(8,128)(2,1)S(1)}, u32[]{:S(2)}, u32[]{:S(2)}) collective-permute-start(bf16[8,104,128]{2,1,0:T(8,128)(2,1)} %get-tuple-element.70), channel_id=1, source_target_pairs={{0,3},{1,2},{2,1},{3,0},{4,7},{5,6},{6,5},{7,4},{8,11},{9,10},{10,... | collective-permute-start | bytes 638984 | tf_op jit(solution)/shard_map/ppermute | solution.py:44
  46.4 3.4 %collective-permute-done.10.refs_3_ = bf16[8,104,128]{2,1,0:T(8,128)(2,1)S(1)} collective-permute-done((bf16[8,104,128]{2,1,0:T(8,128)(2,1)}, bf16[8,104,128]{2,1,0:T(8,128)(2,1)S(1)}, u32[]{:S(2)}, u32[]{:S(2)}) %collective-permute-start.10) | collective-permute-done | bytes 213024 | tf_op jit(solution)/shard_map/ppermute | solution.py:44
  51.6 1.9 padded_weights.1
  62.0 14.9 %mlp_a.1 = (bf16[8,104,128]{2,1,0:T(8,128)(2,1)}, bf16[8,104,128]{2,1,0:T(8,128)(2,1)}, bf16[8,104,128]{2,1,0:T(8,128)(2,1)}, bf16[8,104,128]{2,1,0:T(8,128)(2,1...) custom-call(s32[1]{0:T(128)} %bitcast.me_ref, ...), custom_call_target="tpu_custom_call" | custom-call | bytes 46200000 | tf_op jit(solution)/shard_map/mlp_a/pallas_call | solution.py:322
  81.3 22.0 %mlp_b.1 = (bf16[8,104,128]{2,1,0:T(8,128)(2,1)}, bf16[8,104,128]{2,1,0:T(8,128)(2,1)}, bf16[8,104,128]{2,1,0:T(8,128)(2,1)}, bf16[8,104,128]{2,1,0:T(8,128)(2,1...) custom-call(s32[1]{0:T(128)} %bitcast.me_ref, ...), custom_call_target="tpu_custom_call" | custom-call | bytes 72600000 | tf_op jit(solution)/shard_map/mlp_b/pallas_call | solution.py:322
  104.8 3.3 %collective-permute-done.17 = bf16[5248,128]{1,0:T(8,128)(2,1)S(1)} collective-permute-done((bf16[5248,128]{1,0:T(8,128)(2,1)}, bf16[5248,128]{1,0:T(8,128)(2,1)S(1)}, u32[]{:S(2)}, u32[]{:S(2)}) %collective-permute-start.17) | collective-permute-done | bytes 1343520 | tf_op jit(solution)/shard_map/ppermute | solution.py:44
  108.1 2.7 %add_convert_fusion = bf16[5248,128]{1,0:T(8,128)(2,1)} fusion(bf16[5248,128]{1,0:T(8,128)(2,1)S(1)} %collective-permute-done.17, bf16[5248,128]{1,0:T(8,128)(2,1)} %get-tuple-element.83), kind=kLoop, calls=%fused_computation.1 | loop fusion | flops 2686976 | bytes 4030464 | tf_op jit(solution)/shard_map/convert_element_type | solution.py:541
  110.9 3.8 %all-to-all-start = ((bf16[16,328,128]{2,1,0:T(8,128)(2,1)}), bf16[16,328,128]{2,1,0:T(8,128)(2,1)S(1)}, u32[]{:S(2)}, u32[]{:S(2)}) async-start(bf16[16,328,128]{2,1,0:T(8,128)(2,1)} %bitcast.30), calls=%async_computation | async-start | bytes 2686976 | tf_op jit(solution)/shard_map/all_to_all | solution.py:499
  117.0 4.7 %collective-permute-done.19.refs_6_ = bf16[8,104,128]{2,1,0:T(8,128)(2,1)S(1)} collective-permute-done((bf16[8,104,128]{2,1,0:T(8,128)(2,1)}, bf16[8,104,128]{2,1,0:T(8,128)(2,1)S(1)}, u32[]{:S(2)}, u32[]{:S(2)}) %collective-permute-start.19) | collective-permute-done | bytes 213024 | tf_op jit(solution)/shard_map/ppermute | solution.py:44
  121.6 5.4 %collective-permute-done.20.refs_7_ = bf16[8,104,128]{2,1,0:T(8,128)(2,1)S(1)} collective-permute-done((bf16[8,104,128]{2,1,0:T(8,128)(2,1)S(1)}, bf16[8,104,128]{2,1,0:T(8,128)(2,1)S(1)}, u32[]{:S(2)}, u32[]{:S(2)}) %collective-permute-start.20) | collective-permute-done | bytes 213024 | tf_op jit(solution)/shard_map/ppermute | solution.py:44
  129.8 6.2 %collective-permute-start.21 = (bf16[8,8,832]{2,1,0:T(8,128)(2,1)S(1)}, bf16[8,8,832]{2,1,0:T(8,128)(2,1)S(1)}, u32[]{:S(2)}, u32[]{:S(2)}) collective-permute-start(bf16[8,8,832]{2,1,0:T(8,128)(2,1)S(1)} %get-tuple-element.99), channel_id=1, source_target_pairs={{0,124},{4,0},{8,4},{12,8},{16,12},{20,16},{24,20},{28,24},{32,28}... | collective-permute-start | bytes 319496 | tf_op jit(solution)/shard_map/ppermute | solution.py:48
  136.0 3.4 %collective-permute-done.21.refs_1_.first = bf16[8,8,832]{2,1,0:T(8,128)(2,1)S(1)} collective-permute-done((bf16[8,8,832]{2,1,0:T(8,128)(2,1)S(1)}, bf16[8,8,832]{2,1,0:T(8,128)(2,1)S(1)}, u32[]{:S(2)}, u32[]{:S(2)}) %collective-permute-start.21) | collective-permute-done | bytes 106528 | tf_op jit(solution)/shard_map/ppermute | solution.py:48
  139.5 7.9 %collective-permute-done.22.refs_2_.last = bf16[8,8,832]{2,1,0:T(8,128)(2,1)S(1)} collective-permute-done((bf16[8,8,832]{2,1,0:T(8,128)(2,1)S(1)}, bf16[8,8,832]{2,1,0:T(8,128)(2,1)S(1)}, u32[]{:S(2)}, u32[]{:S(2)}) %collective-permute-start.22) | collective-permute-done | bytes 106528 | tf_op jit(solution)/shard_map/ppermute | solution.py:48
  152.6 2.1 %collective-permute-done.28 = bf16[328,128]{1,0:T(8,128)(2,1)S(1)} collective-permute-done((bf16[328,128]{1,0:T(8,128)(2,1)S(1)}, bf16[328,128]{1,0:T(8,128)(2,1)S(1)}, u32[]{:S(2)}, u32[]{:S(2)}) %collective-permute-start.28) | collective-permute-done | bytes 84000 | tf_op jit(solution)/shard_map/ppermute | solution.py:587
  156.0 3.7 %all-to-all-start.1 = ((bf16[16,328,128]{2,1,0:T(8,128)(2,1)}), bf16[16,328,128]{2,1,0:T(8,128)(2,1)S(1)}, u32[]{:S(2)}, u32[]{:S(2)}) async-start(bf16[16,328,128]{2,1,0:T(8,128)(2,1)} %plane_copies.1), calls=%async_computation.1 | async-start | bytes 2686976 | tf_op jit(solution)/shard_map/all_to_all | solution.py:499
  170.7 10.2 %conv_backward.1 = bf16[100,64,128]{2,1,0:T(8,128)(2,1)} custom-call(s32[1]{0:T(128)} %bitcast.me_ref, bf16[8,104,128]{2,1,0:T(8,128)(2,1)S(1)} %copy-done.10, bf16[8,104,128]{2,1,0:T(8,128)(2,1)S(1)} %copy-done.16, bf16[8,104,128]{2,1,0:T(8,128)(2,1)S(1)} %copy-done.19, bf16[8,104,128]{2,1,0:T(8,128)(2,1)S(1)} %copy-done.22, ...), custom_call_target="tpu_custom_call" | custom-call | bytes 33000000 | tf_op jit(solution)/shard_map/conv_backward/pallas_call | solution.py:171
  181.0 4.3 %update.1 = bf16[100,64,128]{2,1,0:T(8,128)(2,1)} custom-call(s32[1]{0:T(128)} %bitcast.me_ref, bf16[8,104,128]{2,1,0:T(8,128)(2,1)S(1)} %copy-done.40, bf16[8,104,128]{2,1,0:T(8,128)(2,1)} %collective-permute-done.14.refs_1_, bf16[8,104,128]{2,1,0:T(8,128)(2,1)} %collective-permute-done.15.refs_2_, bf16[8,104,128]{2,1,0:T(8,128)(2,1)} %collective-permute-done.16.refs_3_, ...), custom_call_target="tpu_custom_call" | custom-call | bytes 14520000 | tf_op jit(solution)/shard_map/update/pallas_call | solution.py:366
  185.3 2.1 %collective-permute-start.29 = (bf16[5248,128]{1,0:T(8,128)(2,1)S(1)}, bf16[5248,128]{1,0:T(8,128)(2,1)S(1)}, u32[]{:S(2)}, u32[]{:S(2)}) collective-permute-start(bf16[5248,128]{1,0:T(8,128)(2,1)S(1)} %bitcast.27), channel_id=1, source_target_pairs={{0,1},{1,0},{2,3},{3,2},{4,5},{5,4},{6,7},{7,6},{8,9},{9,8},{10,11... | collective-permute-start | bytes 4030472 | tf_op jit(solution)/shard_map/ppermute | solution.py:44
  187.5 2.6 %collective-permute-done.29.other = bf16[5248,128]{1,0:T(8,128)(2,1)S(1)} collective-permute-done((bf16[5248,128]{1,0:T(8,128)(2,1)S(1)}, bf16[5248,128]{1,0:T(8,128)(2,1)S(1)}, u32[]{:S(2)}, u32[]{:S(2)}) %collective-permute-start.29) | collective-permute-done | bytes 1343520 | tf_op jit(solution)/shard_map/ppermute | solution.py:44
  190.1 4.5 %finish.1 = (f32[400,1600]{1,0:T(8,128)}, f32[400,1600]{1,0:T(8,128)}) custom-call(s32[1]{0:T(128)} %bitcast.1.core_ref, bf16[5248,128]{1,0:T(8,128)(2,1)S(1)} %bitcast.28, bf16[5248,128]{1,0:T(8,128)(2,1)S(1)} %collective-permute-done.29.other, bf16[400,416]{1,0:T(8,128)(2,1)S(1)} %fusion.1.pad), custom_call_target="tpu_custom_call" | custom-call | bytes 19800000 | tf_op jit(solution)/shard_map/finish/pallas_call | solution.py:565
  (209 shorter events, 58.2 us)
Async XLA Ops:
  2.8 24.8 %collective-permute-start = (bf16[8,6400]{1,0:T(8,128)(2,1)S(1)}, bf16[8,6400]{1,0:T(8,128)(2,1)}, u32[]{:S(2)}, u32[]{:S(2)}) collective-permute-start(bf16[8,6400]{1,0:T(8,128)(2,1)S(1)} %edge.2.refs_0_), channel_id=1, source_target_pairs={{0,124},{4,0},{8,4},{12,8},{16,12},{20,16},{24,20},{28,24},{32,28}... | collective-permute-start | bytes 307208 | tf_op jit(solution)/shard_map/ppermute | solution.py:48
  15.0 46.9 %collective-permute-start.6 = (bf16[16,104,128]{2,1,0:T(8,128)(2,1)}, bf16[16,104,128]{2,1,0:T(8,128)(2,1)}, u32[]{:S(2)}, u32[]{:S(2)}) collective-permute-start(bf16[16,104,128]{2,1,0:T(8,128)(2,1)} %branch_share.4.refs_0_), channel_id=1, source_target_pairs={{0,2},{1,3},{2,0},{3,1},{4,6},{5,7},{6,4},{7,5},{8,10},{9,11},{10,... | collective-permute-start | bytes 1277960 | tf_op jit(solution)/shard_map/ppermute | solution.py:44
  16.6 11.0 %collective-permute-start.1 = (bf16[8,6400]{1,0:T(8,128)(2,1)}, bf16[8,6400]{1,0:T(8,128)(2,1)}, u32[]{:S(2)}, u32[]{:S(2)}) collective-permute-start(bf16[8,6400]{1,0:T(8,128)(2,1)} %edge.3.refs_0_), channel_id=1, source_target_pairs={{0,4},{4,8},{8,12},{12,16},{16,20},{20,24},{24,28},{28,32},{32,36}... | collective-permute-start | bytes 307208 | tf_op jit(solution)/shard_map/ppermute | solution.py:48
  17.8 44.2 %collective-permute-start.7 = (bf16[16,104,128]{2,1,0:T(8,128)(2,1)}, bf16[16,104,128]{2,1,0:T(8,128)(2,1)}, u32[]{:S(2)}, u32[]{:S(2)}) collective-permute-start(bf16[16,104,128]{2,1,0:T(8,128)(2,1)} %branch_share.5.refs_0_), channel_id=1, source_target_pairs={{0,3},{1,2},{2,1},{3,0},{4,7},{5,6},{6,5},{7,4},{8,11},{9,10},{10,... | collective-permute-start | bytes 1277960 | tf_op jit(solution)/shard_map/ppermute | solution.py:44
  21.3 38.8 %collective-permute-start.5 = (bf16[16,104,128]{2,1,0:T(8,128)(2,1)}, bf16[16,104,128]{2,1,0:T(8,128)(2,1)}, u32[]{:S(2)}, u32[]{:S(2)}) collective-permute-start(bf16[16,104,128]{2,1,0:T(8,128)(2,1)} %branch_share.6.refs_0_), channel_id=1, source_target_pairs={{0,1},{1,0},{2,3},{3,2},{4,5},{5,4},{6,7},{7,6},{8,9},{9,8},{10,11... | collective-permute-start | bytes 1277960 | tf_op jit(solution)/shard_map/ppermute | solution.py:44
  41.8 8.0 %collective-permute-start.10 = (bf16[8,104,128]{2,1,0:T(8,128)(2,1)}, bf16[8,104,128]{2,1,0:T(8,128)(2,1)S(1)}, u32[]{:S(2)}, u32[]{:S(2)}) collective-permute-start(bf16[8,104,128]{2,1,0:T(8,128)(2,1)} %get-tuple-element.70), channel_id=1, source_target_pairs={{0,3},{1,2},{2,1},{3,0},{4,7},{5,6},{6,5},{7,4},{8,11},{9,10},{10,... | collective-permute-start | bytes 638984 | tf_op jit(solution)/shard_map/ppermute | solution.py:44
  46.3 11.8 %collective-permute-start.8 = (bf16[8,104,128]{2,1,0:T(8,128)(2,1)}, bf16[8,104,128]{2,1,0:T(8,128)(2,1)S(1)}, u32[]{:S(2)}, u32[]{:S(2)}) collective-permute-start(bf16[8,104,128]{2,1,0:T(8,128)(2,1)} %copy-done.47), channel_id=1, source_target_pairs={{0,1},{1,0},{2,3},{3,2},{4,5},{5,4},{6,7},{7,6},{8,9},{9,8},{10,11... | collective-permute-start | bytes 638984 | tf_op jit(solution)/shard_map/ppermute | solution.py:44
  49.8 9.3 %collective-permute-start.9 = (bf16[8,104,128]{2,1,0:T(8,128)(2,1)}, bf16[8,104,128]{2,1,0:T(8,128)(2,1)S(1)}, u32[]{:S(2)}, u32[]{:S(2)}) collective-permute-start(bf16[8,104,128]{2,1,0:T(8,128)(2,1)} %copy-done.46), channel_id=1, source_target_pairs={{0,2},{1,3},{2,0},{3,1},{4,6},{5,7},{6,4},{7,5},{8,10},{9,11},{10,... | collective-permute-start | bytes 638984 | tf_op jit(solution)/shard_map/ppermute | solution.py:44
  58.2 19.3 %collective-permute-start.2 = (bf16[8,104,128]{2,1,0:T(8,128)(2,1)S(1)}, bf16[8,104,128]{2,1,0:T(8,128)(2,1)}, u32[]{:S(2)}, u32[]{:S(2)}) collective-permute-start(bf16[8,104,128]{2,1,0:T(8,128)(2,1)S(1)} %copy-done.45), channel_id=1, source_target_pairs={{0,1},{1,0},{2,3},{3,2},{4,5},{5,4},{6,7},{7,6},{8,9},{9,8},{10,11... | collective-permute-start | bytes 638984 | tf_op jit(solution)/shard_map/ppermute | solution.py:44
  59.7 19.4 %collective-permute-start.3 = (bf16[8,104,128]{2,1,0:T(8,128)(2,1)}, bf16[8,104,128]{2,1,0:T(8,128)(2,1)}, u32[]{:S(2)}, u32[]{:S(2)}) collective-permute-start(bf16[8,104,128]{2,1,0:T(8,128)(2,1)} %get-tuple-element.61), channel_id=1, source_target_pairs={{0,2},{1,3},{2,0},{3,1},{4,6},{5,7},{6,4},{7,5},{8,10},{9,11},{10,... | collective-permute-start | bytes 638984 | tf_op jit(solution)/shard_map/ppermute | solution.py:44
  60.1 19.0 %collective-permute-start.4 = (bf16[8,104,128]{2,1,0:T(8,128)(2,1)}, bf16[8,104,128]{2,1,0:T(8,128)(2,1)}, u32[]{:S(2)}, u32[]{:S(2)}) collective-permute-start(bf16[8,104,128]{2,1,0:T(8,128)(2,1)} %get-tuple-element.62), channel_id=1, source_target_pairs={{0,3},{1,2},{2,1},{3,0},{4,7},{5,6},{6,5},{7,4},{8,11},{9,10},{10,... | collective-permute-start | bytes 638984 | tf_op jit(solution)/shard_map/ppermute | solution.py:44
  77.0 26.3 %collective-permute-start.12 = (bf16[8,104,128]{2,1,0:T(8,128)(2,1)}, bf16[8,104,128]{2,1,0:T(8,128)(2,1)S(1)}, u32[]{:S(2)}, u32[]{:S(2)}) collective-permute-start(bf16[8,104,128]{2,1,0:T(8,128)(2,1)} %get-tuple-element.77), channel_id=1, source_target_pairs={{0,2},{1,3},{2,0},{3,1},{4,6},{5,7},{6,4},{7,5},{8,10},{9,11},{10,... | collective-permute-start | bytes 638984 | tf_op jit(solution)/shard_map/ppermute | solution.py:44
  77.5 26.6 %collective-permute-start.13 = (bf16[8,104,128]{2,1,0:T(8,128)(2,1)}, bf16[8,104,128]{2,1,0:T(8,128)(2,1)S(1)}, u32[]{:S(2)}, u32[]{:S(2)}) collective-permute-start(bf16[8,104,128]{2,1,0:T(8,128)(2,1)} %get-tuple-element.78), channel_id=1, source_target_pairs={{0,3},{1,2},{2,1},{3,0},{4,7},{5,6},{6,5},{7,4},{8,11},{9,10},{10,... | collective-permute-start | bytes 638984 | tf_op jit(solution)/shard_map/ppermute | solution.py:44
  79.1 25.6 %collective-permute-start.14 = (bf16[8,104,128]{2,1,0:T(8,128)(2,1)}, bf16[8,104,128]{2,1,0:T(8,128)(2,1)}, u32[]{:S(2)}, u32[]{:S(2)}) collective-permute-start(bf16[8,104,128]{2,1,0:T(8,128)(2,1)} %get-tuple-element.80), channel_id=1, source_target_pairs={{0,1},{1,0},{2,3},{3,2},{4,5},{5,4},{6,7},{7,6},{8,9},{9,8},{10,11... | collective-permute-start | bytes 638984 | tf_op jit(solution)/shard_map/ppermute | solution.py:44
  79.1 25.6 %collective-permute-start.15 = (bf16[8,104,128]{2,1,0:T(8,128)(2,1)}, bf16[8,104,128]{2,1,0:T(8,128)(2,1)}, u32[]{:S(2)}, u32[]{:S(2)}) collective-permute-start(bf16[8,104,128]{2,1,0:T(8,128)(2,1)} %get-tuple-element.81), channel_id=1, source_target_pairs={{0,2},{1,3},{2,0},{3,1},{4,6},{5,7},{6,4},{7,5},{8,10},{9,11},{10,... | collective-permute-start | bytes 638984 | tf_op jit(solution)/shard_map/ppermute | solution.py:44
  79.6 25.1 %collective-permute-start.16 = (bf16[8,104,128]{2,1,0:T(8,128)(2,1)}, bf16[8,104,128]{2,1,0:T(8,128)(2,1)}, u32[]{:S(2)}, u32[]{:S(2)}) collective-permute-start(bf16[8,104,128]{2,1,0:T(8,128)(2,1)} %get-tuple-element.82), channel_id=1, source_target_pairs={{0,3},{1,2},{2,1},{3,0},{4,7},{5,6},{6,5},{7,4},{8,11},{9,10},{10,... | collective-permute-start | bytes 638984 | tf_op jit(solution)/shard_map/ppermute | solution.py:44
  110.9 36.6 %all-to-all-start = ((bf16[16,328,128]{2,1,0:T(8,128)(2,1)}), bf16[16,328,128]{2,1,0:T(8,128)(2,1)S(1)}, u32[]{:S(2)}, u32[]{:S(2)}) async-start(bf16[16,328,128]{2,1,0:T(8,128)(2,1)} %bitcast.30), calls=%async_computation | async-start | bytes 2686976 | tf_op jit(solution)/shard_map/all_to_all | solution.py:499
  115.4 11.6 %collective-permute-start.20 = (bf16[8,104,128]{2,1,0:T(8,128)(2,1)S(1)}, bf16[8,104,128]{2,1,0:T(8,128)(2,1)S(1)}, u32[]{:S(2)}, u32[]{:S(2)}) collective-permute-start(bf16[8,104,128]{2,1,0:T(8,128)(2,1)S(1)} %copy-done.60), channel_id=1, source_target_pairs={{0,3},{1,2},{2,1},{3,0},{4,7},{5,6},{6,5},{7,4},{8,11},{9,10},{10,... | collective-permute-start | bytes 638984 | tf_op jit(solution)/shard_map/ppermute | solution.py:44
  127.6 19.8 %collective-permute-start.23 = (bf16[8,104,128]{2,1,0:T(8,128)(2,1)S(1)}, bf16[8,104,128]{2,1,0:T(8,128)(2,1)S(1)}, u32[]{:S(2)}, u32[]{:S(2)}) collective-permute-start(bf16[8,104,128]{2,1,0:T(8,128)(2,1)S(1)} %copy-done.59), channel_id=1, source_target_pairs={{0,1},{1,0},{2,3},{3,2},{4,5},{5,4},{6,7},{7,6},{8,9},{9,8},{10,11... | collective-permute-start | bytes 638984 | tf_op jit(solution)/shard_map/ppermute | solution.py:44
  127.7 19.7 %collective-permute-start.24 = (bf16[8,104,128]{2,1,0:T(8,128)(2,1)S(1)}, bf16[8,104,128]{2,1,0:T(8,128)(2,1)S(1)}, u32[]{:S(2)}, u32[]{:S(2)}) collective-permute-start(bf16[8,104,128]{2,1,0:T(8,128)(2,1)S(1)} %copy-done.58), channel_id=1, source_target_pairs={{0,2},{1,3},{2,0},{3,1},{4,6},{5,7},{6,4},{7,5},{8,10},{9,11},{10,... | collective-permute-start | bytes 638984 | tf_op jit(solution)/shard_map/ppermute | solution.py:44
  128.2 19.2 %collective-permute-start.25 = (bf16[8,104,128]{2,1,0:T(8,128)(2,1)S(1)}, bf16[8,104,128]{2,1,0:T(8,128)(2,1)S(1)}, u32[]{:S(2)}, u32[]{:S(2)}) collective-permute-start(bf16[8,104,128]{2,1,0:T(8,128)(2,1)S(1)} %copy-done.57), channel_id=1, source_target_pairs={{0,3},{1,2},{2,1},{3,0},{4,7},{5,6},{6,5},{7,4},{8,11},{9,10},{10,... | collective-permute-start | bytes 638984 | tf_op jit(solution)/shard_map/ppermute | solution.py:44
  129.8 9.6 %collective-permute-start.21 = (bf16[8,8,832]{2,1,0:T(8,128)(2,1)S(1)}, bf16[8,8,832]{2,1,0:T(8,128)(2,1)S(1)}, u32[]{:S(2)}, u32[]{:S(2)}) collective-permute-start(bf16[8,8,832]{2,1,0:T(8,128)(2,1)S(1)} %get-tuple-element.99), channel_id=1, source_target_pairs={{0,124},{4,0},{8,4},{12,8},{16,12},{20,16},{24,20},{28,24},{32,28}... | collective-permute-start | bytes 319496 | tf_op jit(solution)/shard_map/ppermute | solution.py:48
  136.0 11.4 %collective-permute-start.22 = (bf16[8,8,832]{2,1,0:T(8,128)(2,1)S(1)}, bf16[8,8,832]{2,1,0:T(8,128)(2,1)S(1)}, u32[]{:S(2)}, u32[]{:S(2)}) collective-permute-start(bf16[8,8,832]{2,1,0:T(8,128)(2,1)S(1)} %get-tuple-element.100), channel_id=1, source_target_pairs={{0,4},{4,8},{8,12},{12,16},{16,20},{20,24},{24,28},{28,32},{32,36}... | collective-permute-start | bytes 319496 | tf_op jit(solution)/shard_map/ppermute | solution.py:48
  156.0 29.3 %all-to-all-start.1 = ((bf16[16,328,128]{2,1,0:T(8,128)(2,1)}), bf16[16,328,128]{2,1,0:T(8,128)(2,1)S(1)}, u32[]{:S(2)}, u32[]{:S(2)}) async-start(bf16[16,328,128]{2,1,0:T(8,128)(2,1)} %plane_copies.1), calls=%async_computation.1 | async-start | bytes 2686976 | tf_op jit(solution)/shard_map/all_to_all | solution.py:499
  (69 other events, 498.2 us)

commit v2 on v1

--- a/solution.py
+++ b/solution.py
@@ -127,7 +127,7 @@
 
 
 def conv_forward(me, state, rim, pattern, bias):
-    share = jax.ShapeDtypeStruct((HR, CP, LANES), BF)
+    share = pltpu.HBM((HR, CP, LANES), BF)
     return pl.pallas_call(
         forward_kernel,
         out_shape=[share] * 8,
@@ -167,14 +167,15 @@
         out_ref[c] = (cot_ref[c].astype(F32) * mask + total).astype(BF)
 
 
-def conv_backward(me, pieces, rims, pattern, cotangent, sea_mask):
+def conv_backward(me, early, late, rims, pattern, cotangent, sea_mask):
     return pl.pallas_call(
         backward_kernel,
         out_shape=jax.ShapeDtypeStruct((LC, ROWS, LANES), BF),
         grid_spec=pltpu.PrefetchScalarGridSpec(
             num_scalar_prefetch=1,
             grid=(CP // GROUP,),
-            in_specs=[pl.BlockSpec((HR, GROUP, LANES), lambda i, me: (0, i, 0))] * 8
+            in_specs=[pl.BlockSpec((None, HR, GROUP, LANES), lambda i, me: (0, 0, i, 0))] * 4
+            + [pl.BlockSpec((HR, GROUP, LANES), lambda i, me: (0, i, 0))] * 4
             + [
                 pl.BlockSpec((8, HR, GROUP, LANES), lambda i, me: (0, 0, i, 0)),
                 pl.BlockSpec((GROUP, 4, LANES), lambda i, me: (i, 0, 0)),
@@ -187,7 +188,7 @@
         compiler_params=pltpu.CompilerParams(vmem_limit_bytes=32 << 20),
         cost_estimate=cost(10),
         name="conv_backward",
-    )(me, *pieces, rims, pattern, cotangent, sea_mask)
+    )(me, *early, *late, rims, pattern, cotangent, sea_mask)
 
 
 SUB = 4
@@ -209,8 +210,8 @@
             pltpu.make_async_copy(cells_in, cells_a, sems.at[1]),
         )
     else:
-        grad_out, branch_out = refs[14:18], refs[18:22]
-        hidden, cells = refs[22:]
+        both_out = refs[14:18]
+        hidden, cells = refs[18:]
     step = pl.program_id(0)
     me = me_ref[0]
     if half:
@@ -268,8 +269,14 @@
     for k in range(4):
         for r in range(SUB):
             here = slice(r * LANES, (r + 1) * LANES)
-            grad_out[k][r] = x_grad[k * CP : (k + 1) * CP, here].astype(BF)
-            branch_out[k][r] = branch[k * CP : (k + 1) * CP, here].astype(BF)
+            grad_piece = x_grad[k * CP : (k + 1) * CP, here].astype(BF)
+            branch_piece = branch[k * CP : (k + 1) * CP, here].astype(BF)
+            if half:
+                grad_out[k][r] = grad_piece
+                branch_out[k][r] = branch_piece
+            else:
+                both_out[k][0, r] = grad_piece
+                both_out[k][1, r] = branch_piece
     if not half:
         return
 
@@ -319,9 +326,14 @@
             pl.BlockSpec((2, 4, CP, CELLS), lambda i, me, core: (0, 0, 0, i)),
         ]
         scratch = []
+    count = 8 if half else 4
+    result = (HR, CP, LANES) if half else (2, HR, CP, LANES)
+    place = piece
+    if not half:
+        place = pl.BlockSpec((2, SUB, CP, LANES), lambda i, me, core: (0, i, 0, 0))
     outs = pl.pallas_call(
         functools.partial(mlp_kernel, half),
-        out_shape=[jax.ShapeDtypeStruct((HR, CP, LANES), BF)] * 8 + shapes,
+        out_shape=[jax.ShapeDtypeStruct(result, BF)] * count + shapes,
         grid_spec=pltpu.PrefetchScalarGridSpec(
             num_scalar_prefetch=2,
             grid=(2,),
@@ -336,14 +348,14 @@
                 whole((HID, 1)),
             ]
             + [any_space] * (len(saved) + len(after)),
-            out_specs=[piece] * 8 + specs,
+            out_specs=[place] * count + specs,
             scratch_shapes=scratch,
         ),
         compiler_params=pltpu.CompilerParams(vmem_limit_bytes=VMEM),
         cost_estimate=cost(22 if half else 14),
         name="mlp_b" if half else "mlp_a",
     )(me, core, *xs, *gs, *weights, vec, bias_in, *saved, *after)
-    return outs[:4], outs[4:8], outs[8:]
+    return outs[:4], outs[4:count], outs[count:]
 
 
 def update_kernel(me_ref, *refs):
@@ -361,7 +373,7 @@
     out_ref[...] = (mask[None] * (state_ref[...].astype(F32) + branch)).astype(BF)
 
 
-def update(me, pieces, state, sea_mask, scale):
+def update(me, early, late, state, sea_mask, scale):
     whole = pl.BlockSpec((HR, CP, LANES), lambda i, me: (0, 0, 0), pipeline_mode=pl.Buffered(1))
     return pl.pallas_call(
         update_kernel,
@@ -369,7 +381,15 @@
         grid_spec=pltpu.PrefetchScalarGridSpec(
             num_scalar_prefetch=1,
             grid=(4,),
-            in_specs=[whole] * 8
+            in_specs=[
+                pl.BlockSpec(
+                    (None, HR, CP, LANES),
+                    lambda i, me: (1, 0, 0, 0),
+                    pipeline_mode=pl.Buffered(1),
+                )
+            ]
+            * 4
+            + [whole] * 4
             + [
                 pl.BlockSpec((LC, QR, LANES), lambda i, me: (0, me[0] ^ i, 0)),
                 pl.BlockSpec((QR, LANES), lambda i, me: (me[0] ^ i, 0)),
@@ -378,10 +398,10 @@
             out_specs=pl.BlockSpec((LC, QR, LANES), lambda i, me: (0, me[0] ^ i, 0)),
             scratch_shapes=[pltpu.VMEM((QR, CP, LANES), BF)],
         ),
-        compiler_params=pltpu.CompilerParams(vmem_limit_bytes=32 << 20),
+        compiler_params=pltpu.CompilerParams(vmem_limit_bytes=VMEM),
         cost_estimate=cost(4.4),
         name="update",
-    )(me, *pieces, state, sea_mask, scale)
+    )(me, *early, *late, state, sea_mask, scale)
 
 
 def weights_kernel(one, two, pad, one_out, one_t, two_out, two_t):
@@ -392,8 +412,8 @@
 
 
 def padded_weights(one, two, pad):
-    flat = jax.ShapeDtypeStruct((4 * CP, HID), BF)
-    turned = jax.ShapeDtypeStruct((HID, 4 * CP), BF)
+    flat = pltpu.HBM((4 * CP, HID), BF)
+    turned = pltpu.HBM((HID, 4 * CP), BF)
     return pl.pallas_call(
         weights_kernel,
         out_shape=[flat, turned, flat, turned],
@@ -452,7 +472,7 @@
         last[i] = both[8:]
 
 
-def piece_edges(picks, pieces):
+def piece_edges(picks, early, late):
     half = pl.BlockSpec((QR // 2, CP, LANES), lambda i: (0, 0, 0))
     whole = pl.BlockSpec((8, 8, HR * CP), lambda i: (0, 0, 0))
     out = jax.ShapeDtypeStruct((8, 8, HR * CP), BF)
@@ -460,12 +480,14 @@
         piece_edges_kernel,
         out_shape=[out, out],
         grid=(1,),
-        in_specs=[pl.BlockSpec((16, LANES), lambda i: (0, 0))] + [half] * 8,
+        in_specs=[pl.BlockSpec((16, LANES), lambda i: (0, 0))]
+        + [pl.BlockSpec((None, HR, CP, LANES), lambda i: (0, 0, 0, 0))] * 4
+        + [half] * 4,
         out_specs=[whole] * 2,
         compiler_params=pltpu.CompilerParams(vmem_limit_bytes=32 << 20),
         cost_estimate=cost(2),
         name="piece_edges",
-    )(picks, *pieces)
+    )(picks, *early, *late)
 
 
 def piece_rims_kernel(pick, first, last, out):
@@ -519,25 +541,26 @@
     )(pieces, *after)
 
 
-def copies_kernel(part, out):
+def copies_kernel(part, *refs):
+    out = refs[-1]
     for i in range(16):
         out[i] = part[...]
 
 
-def plane_copies(part):
+def plane_copies(part, after):
     return pl.pallas_call(
         copies_kernel,
         out_shape=jax.ShapeDtypeStruct((16, PIECE, LANES), BF),
         grid=(1,),
-        in_specs=[full((PIECE, LANES))],
+        in_specs=[full((PIECE, LANES))] + [pl.BlockSpec(memory_space=pl.ANY)] * len(after),
         out_specs=full((16, PIECE, LANES)),
         compiler_params=pltpu.CompilerParams(vmem_limit_bytes=32 << 20),
         cost_estimate=cost(1),
         name="plane_copies",
-    )(part)
-
-
-def reduce_gradients(keep, send, late):
+    )(part, *after)
+
+
+def reduce_gradients(keep, send, late, last):
     mine = (keep.astype(F32) + ch_swap(send, 1).astype(F32)).astype(BF)
     mine = plane_exchange(mine.reshape(16, PIECE, LANES))
     wire = plane_total(mine, late)
@@ -545,7 +568,7 @@
         (wire.astype(F32) + lon_swap(wire, 16).astype(F32))
         + (ch_swap(wire, 2).astype(F32) + both_swap(wire).astype(F32))
     ).astype(BF)
-    return plane_exchange(plane_copies(part)).reshape(WIRE, LANES)
+    return plane_exchange(plane_copies(part, last)).reshape(WIRE, LANES)
 
 
 def finish_kernel(core_ref, own, other, pad, grad_in, grad_out, held):
@@ -629,41 +652,40 @@
     state_rim = rims(first, last).reshape(LC, ROWS, LANES)
     bias = jnp.broadcast_to(conv_bias[:, None, None], (LC, 1, LANES))
     conv = conv_forward(me, ocean_state, state_rim, tap_patterns(kernel), bias)
+    weights, gs, second = lax.optimization_barrier(((win_t, win, wout, wout_t), gs, conv[4:]))
     xs = [
-        [conv[4 * half]] + [ch_swap(conv[4 * half + k], k) for k in (1, 2, 3)] for half in (0, 1)
+        [half[0]] + [ch_swap(half[k], k) for k in (1, 2, 3)] for half in (conv[:4], second)
     ]
 
-    weights = (win_t, win, wout, wout_t)
     bias_rows = bias_in.reshape(HID, 1)
-    grad_a, branch_a, (hid_a, cells_a) = mlp(0, me, core, xs[0], gs, weights, vec, bias_rows)
+    early, _, (hid_a, cells_a) = mlp(0, me, core, xs[0], gs, weights, vec, bias_rows)
+    early, second = lax.optimization_barrier((early, xs[1]))
     saved = (hid_a, cells_a.reshape(2, 4 * CP, 2 * CELLS))
     grad_b, branch_b, (keep, send) = mlp(
-        1, me, core, xs[1], gs, weights, vec, bias_rows, saved, grad_a[:1]
+        1, me, core, second, gs, weights, vec, bias_rows, saved, early[:1]
     )
-    grad_a = [grad_a[0]] + [ch_swap(grad_a[k], k) for k in (1, 2, 3)]
-    branch_a = [branch_a[0]] + [ch_swap(branch_a[k], k) for k in (1, 2, 3)]
-    keep, send, grad_a, branch_a = lax.optimization_barrier((keep, send, grad_a, branch_a))
+    early = [early[0]] + [ch_swap(early[k], k) for k in (1, 2, 3)]
+    keep, send, early = lax.optimization_barrier((keep, send, early))
     grad_b = [grad_b[0]] + [ch_swap(grad_b[k], k) for k in (1, 2, 3)]
-    grads = grad_a + grad_b
+    branch_b = [branch_b[0]] + [ch_swap(branch_b[k], k) for k in (1, 2, 3)]
+    grad_b, branch_b = lax.optimization_barrier((grad_b, branch_b))
+    updated = update(me, early, branch_b, ocean_state, sea_mask, scale)
     picks = jnp.concatenate([head, tail], 0)
-    first, last = piece_edges(picks, grads)
-    first, last, branch_b = lax.optimization_barrier((first, last, branch_b))
-    branch_b = [branch_b[0]] + [ch_swap(branch_b[k], k) for k in (1, 2, 3)]
-    branches = branch_a + branch_b
+    first, last = piece_edges(picks, early, grad_b)
     from_right, from_left = lon_shift(first, -1), lon_shift(last, 1)
-    own = reduce_gradients(keep, send, [from_right, from_left] + branch_b[1:])
+    own = reduce_gradients(keep, send, branch_b[1:], (updated,))
     grad_rims = piece_rims(picks, from_right, from_left)
 
     grad_state = conv_backward(
         me,
-        grads,
+        early,
+        grad_b,
         grad_rims,
         tap_patterns(kernel[:, ::-1]),
         cotangent,
         sea_mask,
     )
-    updated = update(me, branches, ocean_state, sea_mask, scale)
-    own, grad_state, updated = lax.optimization_barrier((own, grad_state, updated))
+    own, grad_state = lax.optimization_barrier((own, grad_state))
     grad_in, grad_out = finish(core, own, ch_swap(own, 1), pad)
     return updated, grad_state, grad_in, grad_out.T
 

time: 195 us -> 202 us (1.036)
  Pallas kernels: 75.2 us -> 80.9 us
  starting transfers between devices: 47.5 us -> 50.8 us
  local copies, waits for them, and re-layouts: 26.9 us -> 23.9 us
  waiting for transfers between devices: 37.1 us -> 35 us
    ppermute x24 -> x21, waiting for transfers between devices: 19.3 us -> 27.7 us  [ch_swap(): return lax.ppermute(x, 'ch', [(i, i ^ k) for i in range(4)])]
    ppermute x4, waiting for transfers between devices: 14.2 us -> 7.21 us  [lon_shift(): return lax.ppermute(x, 'lon', [(i, (i + d) % 32) for i in range(32)])]
    all_to_all x2, starting transfers between devices: 7.56 us -> 13.6 us  [plane_exchange(): return lax.all_to_all(pieces, 'lon', 0, 0, axis_index_groups=PLANES)]
    ppermute x24 -> x21, starting transfers between devices: 21.4 us -> 16.9 us  [ch_swap(): return lax.ppermute(x, 'ch', [(i, i ^ k) for i in range(4)])]
    unnamed x124 -> x112, local copies, waits for them, and re-layouts: 21 us -> 17.4 us
    ppermute x1, waiting for transfers between devices: 2.12 us -> 0.01 us  [both_swap(): lax.ppermute(x, ('lon', 'ch'), [(i, i ^ 16 * 4 + 2) for i in range(128)])]
  transfers between devices with their start and end apart: 32 -> 29, of which waited for: 10 -> 11; matrix products, arithmetic and copies ran while one was open for 5% -> 6% of each run, Pallas kernels for 35% -> 37%
where the time goes in v2:
time: 202 us; the launch traced here: 200 us
  Pallas kernels  80.9 us (40%)
  starting transfers between devices  50.8 us (25%)
  waiting for transfers between devices  35 us (17%)
  local copies, waits for them, and re-layouts  23.9 us (12%)
  other arithmetic  4.93 us (2%)
  matrix products  3.39 us (2%)
    pallas_call x2, Pallas kernels, mlp(): pl.pallas_call(functools.partial(mlp_kernel, half), out_shape=[jax.ShapeD...  37.1 us
    ppermute x21, waiting for transfers between devices, ch_swap(): return lax.ppermute(x, 'ch', [(i, i ^ k) for i in range(4)])  27.7 us
    unnamed x112, local copies, waits for them, and re-layouts  17.4 us
    ppermute x21, starting transfers between devices, ch_swap(): return lax.ppermute(x, 'ch', [(i, i ^ k) for i in range(4)])  16.9 us
    ppermute x4, starting transfers between devices, lon_shift(): return lax.ppermute(x, 'lon', [(i, (i + d) % 32) for i in range(32)])  16.4 us
    all_to_all x2, starting transfers between devices, plane_exchange(): return lax.all_to_all(pieces, 'lon', 0, 0, axis_index_groups=PLANES)  13.6 us
    pallas_call x1, Pallas kernels, conv_backward(): pl.pallas_call(backward_kernel, out_shape=jax.ShapeDtypeStruct((LC, ROWS,...  10.6 us
    pallas_call x1, Pallas kernels, conv_forward(): pl.pallas_call(forward_kernel, out_shape=[share] * 8, grid_spec=pltpu.Pre...  8.89 us
  transfers between devices with their start and end apart: 29, of which 11 were waited for; matrix products, arithmetic and copies ran while one was open for 6% of the time, Pallas kernels for 37%

profile of v2, /device:TPU:1, one launch (start us, length us, event | category | flops | bytes accessed | tf_op | source)
XLA Modules:
  0.0 200.1 jit_solution(11240022069845442588)
XLA Ops:
  2.8 9.5 %collective-permute-start = (bf16[8,6400]{1,0:T(8,128)(2,1)S(1)}, bf16[8,6400]{1,0:T(8,128)(2,1)}, u32[]{:S(2)}, u32[]{:S(2)}) collective-permute-start(bf16[8,6400]{1,0:T(8,128)(2,1)S(1)} %edge.2.refs_0_), channel_id=1, source_target_pairs={{0,124},{4,0},{8,4},{12,8},{16,12},{20,16},{24,20},{28,24},{32,28}... | collective-permute-start | bytes 307208 | tf_op jit(solution)/shard_map/ppermute | solution.py:48
  17.8 2.4 %collective-permute-start.7 = (bf16[16,104,128]{2,1,0:T(8,128)(2,1)}, bf16[16,104,128]{2,1,0:T(8,128)(2,1)}, u32[]{:S(2)}, u32[]{:S(2)}) collective-permute-start(bf16[16,104,128]{2,1,0:T(8,128)(2,1)} %branch_share.5.refs_0_), channel_id=1, source_target_pairs={{0,3},{1,2},{2,1},{3,0},{4,7},{5,6},{6,5},{7,4},{8,11},{9,10},{10,... | collective-permute-start | bytes 1277960 | tf_op jit(solution)/shard_map/ppermute | solution.py:44
  29.3 3.7 %padded_weights.1 = (bf16[416,1600]{1,0:T(8,128)(2,1)}, bf16[1600,416]{1,0:T(8,128)(2,1)}, bf16[416,1600]{1,0:T(8,128)(2,1)}, bf16[1600,416]{1,0:T(8,128)(2,1)}) custom-call(bf16[400,1600]{1,0:T(8,128)(2,1)S(1)} %copy-done.15, bf16[400,1600]{1,0:T(8,128)(2,1)S(1)} %bitcast.29, bf16[400,416]{1,0:T(8,128)(2,1)S(1)} %copy-done.14), custom_call_target="tpu_custom_call" | custom-call | bytes 16500000 | tf_op jit(solution)/shard_map/padded_weights/pallas_call | solution.py:417
  34.9 8.9 %conv_forward.1 = (bf16[8,104,128]{2,1,0:T(8,128)(2,1)}, bf16[8,104,128]{2,1,0:T(8,128)(2,1)}, bf16[8,104,128]{2,1,0:T(8,128)(2,1)}, bf16[8,104,128]{2,1,0:T(8,1...) custom-call(s32[1]{0:T(128)} %bitcast.me_ref, ...), custom_call_target="tpu_custom_call" | custom-call | bytes 29700000 | tf_op jit(solution)/shard_map/conv_forward/pallas_call | solution.py:131
  51.5 5.4 %collective-permute-done.4.refs_3_ = bf16[8,104,128]{2,1,0:T(8,128)(2,1)} collective-permute-done((bf16[8,104,128]{2,1,0:T(8,128)(2,1)}, bf16[8,104,128]{2,1,0:T(8,128)(2,1)}, u32[]{:S(2)}, u32[]{:S(2)}) %collective-permute-start.4) | collective-permute-done | bytes 213024 | tf_op jit(solution)/shard_map/ppermute | solution.py:44
  56.9 15.0 %mlp_a.1 = (bf16[2,8,104,128]{3,2,1,0:T(8,128)(2,1)}, bf16[2,8,104,128]{3,2,1,0:T(8,128)(2,1)}, bf16[2,8,104,128]{3,2,1,0:T(8,128)(2,1)}, bf16[2,8,104,128]{3,2,...) custom-call(s32[1]{0:T(128)} %bitcast.me_ref, s32[1]{0:T(128)} %bitcast.1.core_ref, ...), custom_call_target="tpu_custom_call" | custom-call | bytes 46200000 | tf_op jit(solution)/shard_map/mlp_a/pallas_call | solution.py:334
  75.0 22.0 %mlp_b.1 = (bf16[8,104,128]{2,1,0:T(8,128)(2,1)}, bf16[8,104,128]{2,1,0:T(8,128)(2,1)}, bf16[8,104,128]{2,1,0:T(8,128)(2,1)}, bf16[8,104,128]{2,1,0:T(8,128)(2,1...) custom-call(s32[1]{0:T(128)} %bitcast.me_ref, ...), custom_call_target="tpu_custom_call" | custom-call | bytes 72600000 | tf_op jit(solution)/shard_map/mlp_b/pallas_call | solution.py:334
  97.1 3.3 %collective-permute-done.20 = bf16[5248,128]{1,0:T(8,128)(2,1)S(1)} collective-permute-done((bf16[5248,128]{1,0:T(8,128)(2,1)}, bf16[5248,128]{1,0:T(8,128)(2,1)S(1)}, u32[]{:S(2)}, u32[]{:S(2)}) %collective-permute-start.20) | collective-permute-done | bytes 1343520 | tf_op jit(solution)/shard_map/ppermute | solution.py:44
  100.4 2.7 %add_convert_fusion = bf16[5248,128]{1,0:T(8,128)(2,1)} fusion(bf16[5248,128]{1,0:T(8,128)(2,1)S(1)} %collective-permute-done.20, bf16[5248,128]{1,0:T(8,128)(2,1)} %get-tuple-element.128), kind=kLoop, calls=%fused_computation.1 | loop fusion | flops 2686976 | bytes 4030464 | tf_op jit(solution)/shard_map/convert_element_type | solution.py:564
  103.2 6.9 %all-to-all-start = ((bf16[16,328,128]{2,1,0:T(8,128)(2,1)}), bf16[16,328,128]{2,1,0:T(8,128)(2,1)S(1)}, u32[]{:S(2)}, u32[]{:S(2)}) async-start(bf16[16,328,128]{2,1,0:T(8,128)(2,1)} %bitcast.30), calls=%async_computation | async-start | bytes 2686976 | tf_op jit(solution)/shard_map/all_to_all | solution.py:521
  118.1 4.8 %collective-permute-done.16.refs_7_ = bf16[8,104,128]{2,1,0:T(8,128)(2,1)S(1)} collective-permute-done((bf16[8,104,128]{2,1,0:T(8,128)(2,1)S(1)}, bf16[8,104,128]{2,1,0:T(8,128)(2,1)S(1)}, u32[]{:S(2)}, u32[]{:S(2)}) %collective-permute-start.16) | collective-permute-done | bytes 213024 | tf_op jit(solution)/shard_map/ppermute | solution.py:44
  123.7 2.9 %collective-permute-done.18.refs_6_.refs_2_ = bf16[8,104,128]{2,1,0:T(8,128)(2,1)S(1)} collective-permute-done((bf16[8,104,128]{2,1,0:T(8,128)(2,1)S(1)}, bf16[8,104,128]{2,1,0:T(8,128)(2,1)S(1)}, u32[]{:S(2)}, u32[]{:S(2)}) %collective-permute-start.18) | collective-permute-done | bytes 213024 | tf_op jit(solution)/shard_map/ppermute | solution.py:44
  126.6 5.0 %collective-permute-done.19.refs_7_.refs_3_ = bf16[8,104,128]{2,1,0:T(8,128)(2,1)S(1)} collective-permute-done((bf16[8,104,128]{2,1,0:T(8,128)(2,1)S(1)}, bf16[8,104,128]{2,1,0:T(8,128)(2,1)S(1)}, u32[]{:S(2)}, u32[]{:S(2)}) %collective-permute-start.19) | collective-permute-done | bytes 213024 | tf_op jit(solution)/shard_map/ppermute | solution.py:44
  131.9 3.0 %collective-permute-start.21 = (bf16[328,128]{1,0:T(8,128)(2,1)S(1)}, bf16[328,128]{1,0:T(8,128)(2,1)S(1)}, u32[]{:S(2)}, u32[]{:S(2)}) collective-permute-start(bf16[328,128]{1,0:T(8,128)(2,1)S(1)} %plane_total.1), channel_id=1, source_target_pairs={{0,64},{4,68},{8,72},{12,76},{16,80},{20,84},{24,88},{28,92},{32,9... | collective-permute-start | bytes 251912 | tf_op jit(solution)/shard_map/ppermute | solution.py:52
  135.8 5.1 %update.1.refs_0_ = bf16[100,64,128]{2,1,0:T(8,128)(2,1)} custom-call(s32[1]{0:T(128)} %bitcast.me_ref, bf16[2,8,104,128]{3,2,1,0:T(8,128)(2,1)} %get-tuple-element.112.refs_16_.refs_0_, bf16[2,8,104,128]{3,2,1,0:T(8,128)(2,1)} %copy-done.6, bf16[2,8,104,128]{3,2,1,0:T(8,128)(2,1)} %copy-done.9, bf16[2,8,104,128]{3,2,1,0:T(8,128)(2,1)} %collective-permute-done.13.refs_3_, ...), custom_call_target="tpu_custom_call" | custom-call | bytes 14520000 | tf_op jit(solution)/shard_map/update/pallas_call | solution.py:378
  144.7 6.7 %all-to-all-start.1 = ((bf16[16,328,128]{2,1,0:T(8,128)(2,1)}), bf16[16,328,128]{2,1,0:T(8,128)(2,1)S(1)}, u32[]{:S(2)}, u32[]{:S(2)}) async-start(bf16[16,328,128]{2,1,0:T(8,128)(2,1)} %plane_copies.1), calls=%async_computation.1 | async-start | bytes 2686976 | tf_op jit(solution)/shard_map/all_to_all | solution.py:521
  153.0 2.2 %piece_edges.1 = (bf16[8,8,832]{2,1,0:T(8,128)(2,1)}, bf16[8,8,832]{2,1,0:T(8,128)(2,1)}) custom-call(bf16[16,128]{1,0:T(8,128)(2,1)S(1)} %pad_maximum_fusion.1.pick, bf16[2,8,104,128]{3,2,1,0:T(8,128)(2,1)S(1)} %copy-done.4, bf16[2,8,104,128]{3,2,1,0:T(8,128)(2,1)S(1)} %copy-done.7, bf16[2,8,104,128]{3,2,1,0:T(8,128)(2,1)S(1)} %copy-done.10, ...), custom_call_target="tpu_custom_call" | custom-call | bytes 6600000 | tf_op jit(solution)/shard_map/piece_edges/pallas_call | solution.py:479
  155.2 6.9 %collective-permute-start.24 = (bf16[8,8,832]{2,1,0:T(8,128)(2,1)}, bf16[8,8,832]{2,1,0:T(8,128)(2,1)S(1)}, u32[]{:S(2)}, u32[]{:S(2)}) collective-permute-start(bf16[8,8,832]{2,1,0:T(8,128)(2,1)} %get-tuple-element.134), channel_id=1, source_target_pairs={{0,124},{4,0},{8,4},{12,8},{16,12},{20,16},{24,20},{28,24},{32,28}... | collective-permute-start | bytes 319496 | tf_op jit(solution)/shard_map/ppermute | solution.py:48
  164.6 4.7 %collective-permute-done.24.first = bf16[8,8,832]{2,1,0:T(8,128)(2,1)S(1)} collective-permute-done((bf16[8,8,832]{2,1,0:T(8,128)(2,1)}, bf16[8,8,832]{2,1,0:T(8,128)(2,1)S(1)}, u32[]{:S(2)}, u32[]{:S(2)}) %collective-permute-start.24) | collective-permute-done | bytes 106528 | tf_op jit(solution)/shard_map/ppermute | solution.py:48
  169.3 2.5 %collective-permute-done.25.last = bf16[8,8,832]{2,1,0:T(8,128)(2,1)} collective-permute-done((bf16[8,8,832]{2,1,0:T(8,128)(2,1)}, bf16[8,8,832]{2,1,0:T(8,128)(2,1)}, u32[]{:S(2)}, u32[]{:S(2)}) %collective-permute-start.25) | collective-permute-done | bytes 106528 | tf_op jit(solution)/shard_map/ppermute | solution.py:48
  178.8 10.6 %conv_backward.1 = bf16[100,64,128]{2,1,0:T(8,128)(2,1)} custom-call(s32[1]{0:T(128)} %bitcast.me_ref, bf16[2,8,104,128]{3,2,1,0:T(8,128)(2,1)S(1)} %copy-done.4, bf16[2,8,104,128]{3,2,1,0:T(8,128)(2,1)S(1)} %copy-done.8, bf16[2,8,104,128]{3,2,1,0:T(8,128)(2,1)S(1)} %copy-done.11, bf16[2,8,104,128]{3,2,1,0:T(8,128)(2,1)} %collective-permute-done.13.refs_3_, ...), custom_call_target="tpu_custom_call" | custom-call | bytes 33000000 | tf_op jit(solution)/shard_map/conv_backward/pallas_call | solution.py:171
  189.4 3.4 %collective-permute-start.26 = (bf16[5248,128]{1,0:T(8,128)(2,1)S(1)}, bf16[5248,128]{1,0:T(8,128)(2,1)S(1)}, u32[]{:S(2)}, u32[]{:S(2)}) collective-permute-start(bf16[5248,128]{1,0:T(8,128)(2,1)S(1)} %bitcast.27), channel_id=1, source_target_pairs={{0,1},{1,0},{2,3},{3,2},{4,5},{5,4},{6,7},{7,6},{8,9},{9,8},{10,11... | collective-permute-start | bytes 4030472 | tf_op jit(solution)/shard_map/ppermute | solution.py:44
  193.0 2.6 %collective-permute-done.26.other = bf16[5248,128]{1,0:T(8,128)(2,1)S(1)} collective-permute-done((bf16[5248,128]{1,0:T(8,128)(2,1)S(1)}, bf16[5248,128]{1,0:T(8,128)(2,1)S(1)}, u32[]{:S(2)}, u32[]{:S(2)}) %collective-permute-start.26) | collective-permute-done | bytes 1343520 | tf_op jit(solution)/shard_map/ppermute | solution.py:44
  195.5 4.5 %finish.1 = (f32[400,1600]{1,0:T(8,128)}, f32[400,1600]{1,0:T(8,128)}) custom-call(s32[1]{0:T(128)} %bitcast.1.core_ref, bf16[5248,128]{1,0:T(8,128)(2,1)S(1)} %bitcast.28, bf16[5248,128]{1,0:T(8,128)(2,1)S(1)} %collective-permute-done.26.other, bf16[400,416]{1,0:T(8,128)(2,1)S(1)} %fusion.1.pad), custom_call_target="tpu_custom_call" | custom-call | bytes 19800000 | tf_op jit(solution)/shard_map/finish/pallas_call | solution.py:588
  (191 shorter events, 53.9 us)
Async XLA Ops:
  2.8 30.3 %collective-permute-start = (bf16[8,6400]{1,0:T(8,128)(2,1)S(1)}, bf16[8,6400]{1,0:T(8,128)(2,1)}, u32[]{:S(2)}, u32[]{:S(2)}) collective-permute-start(bf16[8,6400]{1,0:T(8,128)(2,1)S(1)} %edge.2.refs_0_), channel_id=1, source_target_pairs={{0,124},{4,0},{8,4},{12,8},{16,12},{20,16},{24,20},{28,24},{32,28}... | collective-permute-start | bytes 307208 | tf_op jit(solution)/shard_map/ppermute | solution.py:48
  15.1 31.0 %collective-permute-start.6 = (bf16[16,104,128]{2,1,0:T(8,128)(2,1)}, bf16[16,104,128]{2,1,0:T(8,128)(2,1)}, u32[]{:S(2)}, u32[]{:S(2)}) collective-permute-start(bf16[16,104,128]{2,1,0:T(8,128)(2,1)} %branch_share.4.refs_0_), channel_id=1, source_target_pairs={{0,2},{1,3},{2,0},{3,1},{4,6},{5,7},{6,4},{7,5},{8,10},{9,11},{10,... | collective-permute-start | bytes 1277960 | tf_op jit(solution)/shard_map/ppermute | solution.py:44
  16.6 16.5 %collective-permute-start.1 = (bf16[8,6400]{1,0:T(8,128)(2,1)}, bf16[8,6400]{1,0:T(8,128)(2,1)}, u32[]{:S(2)}, u32[]{:S(2)}) collective-permute-start(bf16[8,6400]{1,0:T(8,128)(2,1)} %edge.3.refs_0_), channel_id=1, source_target_pairs={{0,4},{4,8},{8,12},{12,16},{16,20},{20,24},{24,28},{28,32},{32,36}... | collective-permute-start | bytes 307208 | tf_op jit(solution)/shard_map/ppermute | solution.py:48
  17.8 28.3 %collective-permute-start.7 = (bf16[16,104,128]{2,1,0:T(8,128)(2,1)}, bf16[16,104,128]{2,1,0:T(8,128)(2,1)}, u32[]{:S(2)}, u32[]{:S(2)}) collective-permute-start(bf16[16,104,128]{2,1,0:T(8,128)(2,1)} %branch_share.5.refs_0_), channel_id=1, source_target_pairs={{0,3},{1,2},{2,1},{3,0},{4,7},{5,6},{6,5},{7,4},{8,11},{9,10},{10,... | collective-permute-start | bytes 1277960 | tf_op jit(solution)/shard_map/ppermute | solution.py:44
  21.3 23.4 %collective-permute-start.5 = (bf16[16,104,128]{2,1,0:T(8,128)(2,1)}, bf16[16,104,128]{2,1,0:T(8,128)(2,1)}, u32[]{:S(2)}, u32[]{:S(2)}) collective-permute-start(bf16[16,104,128]{2,1,0:T(8,128)(2,1)} %branch_share.6.refs_0_), channel_id=1, source_target_pairs={{0,1},{1,0},{2,3},{3,2},{4,5},{5,4},{6,7},{7,6},{8,9},{9,8},{10,11... | collective-permute-start | bytes 1277960 | tf_op jit(solution)/shard_map/ppermute | solution.py:44
  44.3 7.1 %collective-permute-start.3 = (bf16[8,104,128]{2,1,0:T(8,128)(2,1)}, bf16[8,104,128]{2,1,0:T(8,128)(2,1)}, u32[]{:S(2)}, u32[]{:S(2)}) collective-permute-start(bf16[8,104,128]{2,1,0:T(8,128)(2,1)} %get-tuple-element.74), channel_id=1, source_target_pairs={{0,2},{1,3},{2,0},{3,1},{4,6},{5,7},{6,4},{7,5},{8,10},{9,11},{10,... | collective-permute-start | bytes 638984 | tf_op jit(solution)/shard_map/ppermute | solution.py:44
  44.7 12.2 %collective-permute-start.4 = (bf16[8,104,128]{2,1,0:T(8,128)(2,1)}, bf16[8,104,128]{2,1,0:T(8,128)(2,1)}, u32[]{:S(2)}, u32[]{:S(2)}) collective-permute-start(bf16[8,104,128]{2,1,0:T(8,128)(2,1)} %get-tuple-element.75), channel_id=1, source_target_pairs={{0,3},{1,2},{2,1},{3,0},{4,7},{5,6},{6,5},{7,4},{8,11},{9,10},{10,... | collective-permute-start | bytes 638984 | tf_op jit(solution)/shard_map/ppermute | solution.py:44
  46.1 25.8 %collective-permute-start.10 = (bf16[8,104,128]{2,1,0:T(8,128)(2,1)}, bf16[8,104,128]{2,1,0:T(8,128)(2,1)S(1)}, u32[]{:S(2)}, u32[]{:S(2)}) collective-permute-start(bf16[8,104,128]{2,1,0:T(8,128)(2,1)} %get-tuple-element.99), channel_id=1, source_target_pairs={{0,3},{1,2},{2,1},{3,0},{4,7},{5,6},{6,5},{7,4},{8,11},{9,10},{10,... | collective-permute-start | bytes 638984 | tf_op jit(solution)/shard_map/ppermute | solution.py:44
  46.5 25.5 %collective-permute-start.8 = (bf16[8,104,128]{2,1,0:T(8,128)(2,1)}, bf16[8,104,128]{2,1,0:T(8,128)(2,1)S(1)}, u32[]{:S(2)}, u32[]{:S(2)}) collective-permute-start(bf16[8,104,128]{2,1,0:T(8,128)(2,1)} %get-tuple-element.97), channel_id=1, source_target_pairs={{0,1},{1,0},{2,3},{3,2},{4,5},{5,4},{6,7},{7,6},{8,9},{9,8},{10,11... | collective-permute-start | bytes 638984 | tf_op jit(solution)/shard_map/ppermute | solution.py:44
  46.8 25.2 %collective-permute-start.9 = (bf16[8,104,128]{2,1,0:T(8,128)(2,1)}, bf16[8,104,128]{2,1,0:T(8,128)(2,1)S(1)}, u32[]{:S(2)}, u32[]{:S(2)}) collective-permute-start(bf16[8,104,128]{2,1,0:T(8,128)(2,1)} %get-tuple-element.98), channel_id=1, source_target_pairs={{0,2},{1,3},{2,0},{3,1},{4,6},{5,7},{6,4},{7,5},{8,10},{9,11},{10,... | collective-permute-start | bytes 638984 | tf_op jit(solution)/shard_map/ppermute | solution.py:44
  72.8 24.2 %collective-permute-start.11 = (bf16[2,8,104,128]{3,2,1,0:T(8,128)(2,1)}, bf16[2,8,104,128]{3,2,1,0:T(8,128)(2,1)S(1)}, u32[]{:S(2)}, u32[]{:S(2)}) collective-permute-start(bf16[2,8,104,128]{3,2,1,0:T(8,128)(2,1)} %get-tuple-element.109), channel_id=1, source_target_pairs={{0,1},{1,0},{2,3},{3,2},{4,5},{5,4},{6,7},{7,6},{8,9},{9,8},{10,11... | collective-permute-start | bytes 1277960 | tf_op jit(solution)/shard_map/ppermute | solution.py:44
  72.8 24.2 %collective-permute-start.12 = (bf16[2,8,104,128]{3,2,1,0:T(8,128)(2,1)}, bf16[2,8,104,128]{3,2,1,0:T(8,128)(2,1)S(1)}, u32[]{:S(2)}, u32[]{:S(2)}) collective-permute-start(bf16[2,8,104,128]{3,2,1,0:T(8,128)(2,1)} %get-tuple-element.110), channel_id=1, source_target_pairs={{0,2},{1,3},{2,0},{3,1},{4,6},{5,7},{6,4},{7,5},{8,10},{9,11},{10,... | collective-permute-start | bytes 1277960 | tf_op jit(solution)/shard_map/ppermute | solution.py:44
  73.1 23.9 %collective-permute-start.13 = (bf16[2,8,104,128]{3,2,1,0:T(8,128)(2,1)}, bf16[2,8,104,128]{3,2,1,0:T(8,128)(2,1)}, u32[]{:S(2)}, u32[]{:S(2)}) collective-permute-start(bf16[2,8,104,128]{3,2,1,0:T(8,128)(2,1)} %get-tuple-element.111), channel_id=1, source_target_pairs={{0,3},{1,2},{2,1},{3,0},{4,7},{5,6},{6,5},{7,4},{8,11},{9,10},{10,... | collective-permute-start | bytes 1277960 | tf_op jit(solution)/shard_map/ppermute | solution.py:44
  103.2 28.5 %all-to-all-start = ((bf16[16,328,128]{2,1,0:T(8,128)(2,1)}), bf16[16,328,128]{2,1,0:T(8,128)(2,1)S(1)}, u32[]{:S(2)}, u32[]{:S(2)}) async-start(bf16[16,328,128]{2,1,0:T(8,128)(2,1)} %bitcast.30), calls=%async_computation | async-start | bytes 2686976 | tf_op jit(solution)/shard_map/all_to_all | solution.py:521
  110.6 6.8 %collective-permute-start.15 = (bf16[8,104,128]{2,1,0:T(8,128)(2,1)S(1)}, bf16[8,104,128]{2,1,0:T(8,128)(2,1)S(1)}, u32[]{:S(2)}, u32[]{:S(2)}) collective-permute-start(bf16[8,104,128]{2,1,0:T(8,128)(2,1)S(1)} %copy-done.53), channel_id=1, source_target_pairs={{0,2},{1,3},{2,0},{3,1},{4,6},{5,7},{6,4},{7,5},{8,10},{9,11},{10,... | collective-permute-start | bytes 638984 | tf_op jit(solution)/shard_map/ppermute | solution.py:44
  112.1 10.9 %collective-permute-start.16 = (bf16[8,104,128]{2,1,0:T(8,128)(2,1)S(1)}, bf16[8,104,128]{2,1,0:T(8,128)(2,1)S(1)}, u32[]{:S(2)}, u32[]{:S(2)}) collective-permute-start(bf16[8,104,128]{2,1,0:T(8,128)(2,1)S(1)} %copy-done.52), channel_id=1, source_target_pairs={{0,3},{1,2},{2,1},{3,0},{4,7},{5,6},{6,5},{7,4},{8,11},{9,10},{10,... | collective-permute-start | bytes 638984 | tf_op jit(solution)/shard_map/ppermute | solution.py:44
  112.4 11.3 %collective-permute-start.17 = (bf16[8,104,128]{2,1,0:T(8,128)(2,1)S(1)}, bf16[8,104,128]{2,1,0:T(8,128)(2,1)S(1)}, u32[]{:S(2)}, u32[]{:S(2)}) collective-permute-start(bf16[8,104,128]{2,1,0:T(8,128)(2,1)S(1)} %copy-done.51), channel_id=1, source_target_pairs={{0,1},{1,0},{2,3},{3,2},{4,5},{5,4},{6,7},{7,6},{8,9},{9,8},{10,11... | collective-permute-start | bytes 638984 | tf_op jit(solution)/shard_map/ppermute | solution.py:44
  112.8 13.8 %collective-permute-start.18 = (bf16[8,104,128]{2,1,0:T(8,128)(2,1)S(1)}, bf16[8,104,128]{2,1,0:T(8,128)(2,1)S(1)}, u32[]{:S(2)}, u32[]{:S(2)}) collective-permute-start(bf16[8,104,128]{2,1,0:T(8,128)(2,1)S(1)} %copy-done.50), channel_id=1, source_target_pairs={{0,2},{1,3},{2,0},{3,1},{4,6},{5,7},{6,4},{7,5},{8,10},{9,11},{10,... | collective-permute-start | bytes 638984 | tf_op jit(solution)/shard_map/ppermute | solution.py:44
  114.7 17.0 %collective-permute-start.19 = (bf16[8,104,128]{2,1,0:T(8,128)(2,1)S(1)}, bf16[8,104,128]{2,1,0:T(8,128)(2,1)S(1)}, u32[]{:S(2)}, u32[]{:S(2)}) collective-permute-start(bf16[8,104,128]{2,1,0:T(8,128)(2,1)S(1)} %copy-done.49), channel_id=1, source_target_pairs={{0,3},{1,2},{2,1},{3,0},{4,7},{5,6},{6,5},{7,4},{8,11},{9,10},{10,... | collective-permute-start | bytes 638984 | tf_op jit(solution)/shard_map/ppermute | solution.py:44
  131.9 9.1 %collective-permute-start.21 = (bf16[328,128]{1,0:T(8,128)(2,1)S(1)}, bf16[328,128]{1,0:T(8,128)(2,1)S(1)}, u32[]{:S(2)}, u32[]{:S(2)}) collective-permute-start(bf16[328,128]{1,0:T(8,128)(2,1)S(1)} %plane_total.1), channel_id=1, source_target_pairs={{0,64},{4,68},{8,72},{12,76},{16,80},{20,84},{24,88},{28,92},{32,9... | collective-permute-start | bytes 251912 | tf_op jit(solution)/shard_map/ppermute | solution.py:52
  144.7 44.7 %all-to-all-start.1 = ((bf16[16,328,128]{2,1,0:T(8,128)(2,1)}), bf16[16,328,128]{2,1,0:T(8,128)(2,1)S(1)}, u32[]{:S(2)}, u32[]{:S(2)}) async-start(bf16[16,328,128]{2,1,0:T(8,128)(2,1)} %plane_copies.1), calls=%async_computation.1 | async-start | bytes 2686976 | tf_op jit(solution)/shard_map/all_to_all | solution.py:521
  155.2 14.1 %collective-permute-start.24 = (bf16[8,8,832]{2,1,0:T(8,128)(2,1)}, bf16[8,8,832]{2,1,0:T(8,128)(2,1)S(1)}, u32[]{:S(2)}, u32[]{:S(2)}) collective-permute-start(bf16[8,8,832]{2,1,0:T(8,128)(2,1)} %get-tuple-element.134), channel_id=1, source_target_pairs={{0,124},{4,0},{8,4},{12,8},{16,12},{20,16},{24,20},{28,24},{32,28}... | collective-permute-start | bytes 319496 | tf_op jit(solution)/shard_map/ppermute | solution.py:48
  162.0 9.8 %collective-permute-start.25 = (bf16[8,8,832]{2,1,0:T(8,128)(2,1)}, bf16[8,8,832]{2,1,0:T(8,128)(2,1)}, u32[]{:S(2)}, u32[]{:S(2)}) collective-permute-start(bf16[8,8,832]{2,1,0:T(8,128)(2,1)} %get-tuple-element.135), channel_id=1, source_target_pairs={{0,4},{4,8},{8,12},{12,16},{16,20},{20,24},{24,28},{28,32},{32,36}... | collective-permute-start | bytes 319496 | tf_op jit(solution)/shard_map/ppermute | solution.py:48
  189.4 6.1 %collective-permute-start.26 = (bf16[5248,128]{1,0:T(8,128)(2,1)S(1)}, bf16[5248,128]{1,0:T(8,128)(2,1)S(1)}, u32[]{:S(2)}, u32[]{:S(2)}) collective-permute-start(bf16[5248,128]{1,0:T(8,128)(2,1)S(1)} %bitcast.27), channel_id=1, source_target_pairs={{0,1},{1,0},{2,3},{3,2},{4,5},{5,4},{6,7},{7,6},{8,9},{9,8},{10,11... | collective-permute-start | bytes 4030472 | tf_op jit(solution)/shard_map/ppermute | solution.py:44
  (60 other events, 337.2 us)

commit v3 on v2

--- a/solution.py
+++ b/solution.py
@@ -185,7 +185,7 @@
             out_specs=pl.BlockSpec((GROUP, ROWS, LANES), lambda i, me: (i, 0, 0)),
             scratch_shapes=[pltpu.VMEM((4, QR, GROUP, LANES), F32)] * 2,
         ),
-        compiler_params=pltpu.CompilerParams(vmem_limit_bytes=32 << 20),
+        compiler_params=pltpu.CompilerParams(vmem_limit_bytes=VMEM),
         cost_estimate=cost(10),
         name="conv_backward",
     )(me, *early, *late, rims, pattern, cotangent, sea_mask)
@@ -404,26 +404,28 @@
     )(me, *early, *late, state, sea_mask, scale)
 
 
-def weights_kernel(one, two, pad, one_out, one_t, two_out, two_t):
+def weights_kernel(one, two, pad, *refs):
+    one_out, one_t, two_out, two_t = refs[-4:]
     for source, out, turned in ((one, one_out, one_t), (two, two_out, two_t)):
         padded = dotg(pad[...], source[...], 0, 0)
         out[...] = padded.astype(BF)
         turned[...] = padded.T.astype(BF)
 
 
-def padded_weights(one, two, pad):
+def padded_weights(one, two, pad, after):
     flat = pltpu.HBM((4 * CP, HID), BF)
     turned = pltpu.HBM((HID, 4 * CP), BF)
     return pl.pallas_call(
         weights_kernel,
         out_shape=[flat, turned, flat, turned],
         grid=(1,),
-        in_specs=[full((C, HID)), full((C, HID)), full((C, 4 * CP))],
+        in_specs=[full((C, HID)), full((C, HID)), full((C, 4 * CP))]
+        + [pl.BlockSpec(memory_space=pl.ANY)] * len(after),
         out_specs=[full(x.shape) for x in (flat, turned, flat, turned)],
         compiler_params=pltpu.CompilerParams(vmem_limit_bytes=32 << 20),
         cost_estimate=cost(5),
         name="padded_weights",
-    )(one, two, pad)
+    )(one, two, pad, *after)
 
 
 def tap_patterns(kernel):
@@ -475,7 +477,7 @@
 def piece_edges(picks, early, late):
     half = pl.BlockSpec((QR // 2, CP, LANES), lambda i: (0, 0, 0))
     whole = pl.BlockSpec((8, 8, HR * CP), lambda i: (0, 0, 0))
-    out = jax.ShapeDtypeStruct((8, 8, HR * CP), BF)
+    out = pltpu.HBM((8, 8, HR * CP), BF)
     return pl.pallas_call(
         piece_edges_kernel,
         out_shape=[out, out],
@@ -560,15 +562,18 @@
     )(part, *after)
 
 
-def reduce_gradients(keep, send, late, last):
+def reduce_gradients(keep, send, late, first, last):
     mine = (keep.astype(F32) + ch_swap(send, 1).astype(F32)).astype(BF)
     mine = plane_exchange(mine.reshape(16, PIECE, LANES))
+    mine, first, last = lax.optimization_barrier((mine, first, last))
+    from_right, from_left = lon_shift(first, -1), lon_shift(last, 1)
     wire = plane_total(mine, late)
     part = (
         (wire.astype(F32) + lon_swap(wire, 16).astype(F32))
         + (ch_swap(wire, 2).astype(F32) + both_swap(wire).astype(F32))
     ).astype(BF)
-    return plane_exchange(plane_copies(part, last)).reshape(WIRE, LANES)
+    copies = plane_copies(part, (from_right, from_left))
+    return plane_exchange(copies).reshape(WIRE, LANES), from_right, from_left
 
 
 def finish_kernel(core_ref, own, other, pad, grad_in, grad_out, held):
@@ -644,7 +649,6 @@
     padded = jnp.arange(4 * CP)
     pad = ((chan // LC * CP + chan % LC)[:, None] == padded[None, :]).astype(BF)
     pad_own = (((chan // LC ^ ch) * CP + chan % LC)[:, None] == padded[None, :]).astype(BF)
-    win, win_t, wout_t, wout = padded_weights(weight_in, weight_out.T, pad_own)
     vec = jnp.stack([norm_gain, norm_bias, bias_out], 1).reshape(4, LC, 3)
     vec = jnp.pad(vec, ((0, 0), (0, CP - LC), (0, 0)))
     vec = jnp.concatenate([lax.dynamic_index_in_dim(vec, ch ^ k, 0, False) for k in range(4)], 0)
@@ -652,6 +656,7 @@
     state_rim = rims(first, last).reshape(LC, ROWS, LANES)
     bias = jnp.broadcast_to(conv_bias[:, None, None], (LC, 1, LANES))
     conv = conv_forward(me, ocean_state, state_rim, tap_patterns(kernel), bias)
+    win, win_t, wout_t, wout = padded_weights(weight_in, weight_out.T, pad_own, conv[:1])
     weights, gs, second = lax.optimization_barrier(((win_t, win, wout, wout_t), gs, conv[4:]))
     xs = [
         [half[0]] + [ch_swap(half[k], k) for k in (1, 2, 3)] for half in (conv[:4], second)
@@ -672,8 +677,9 @@
     updated = update(me, early, branch_b, ocean_state, sea_mask, scale)
     picks = jnp.concatenate([head, tail], 0)
     first, last = piece_edges(picks, early, grad_b)
-    from_right, from_left = lon_shift(first, -1), lon_shift(last, 1)
-    own = reduce_gradients(keep, send, branch_b[1:], (updated,))
+    own, from_right, from_left = reduce_gradients(
+        keep, send, branch_b[1:], first, last
+    )
     grad_rims = piece_rims(picks, from_right, from_left)
 
     grad_state = conv_backward(
@@ -685,7 +691,7 @@
         cotangent,
         sea_mask,
     )
-    own, grad_state = lax.optimization_barrier((own, grad_state))
+    own, grad_state, updated = lax.optimization_barrier((own, grad_state, updated))
     grad_in, grad_out = finish(core, own, ch_swap(own, 1), pad)
     return updated, grad_state, grad_in, grad_out.T
 

time: 202 us -> 191 us (0.946)
  local copies, waits for them, and re-layouts: 23.9 us -> 16.5 us
  starting transfers between devices: 50.8 us -> 45.2 us
  Pallas kernels: 80.9 us -> 83.9 us
    unnamed x112 -> x76, local copies, waits for them, and re-layouts: 17.4 us -> 11.5 us
    all_to_all x2, starting transfers between devices: 13.6 us -> 8.86 us  [plane_exchange(): return lax.all_to_all(pieces, 'lon', 0, 0, axis_index_groups=PLANES)]
    ppermute x4, waiting for transfers between devices: 7.21 us -> 11.1 us  [lon_shift(): return lax.ppermute(x, 'lon', [(i, (i + d) % 32) for i in range(32)])]
    pallas_call x1, Pallas kernels: 10.6 us -> 13.2 us  [conv_backward(): pl.pallas_call(backward_kernel, out_shape=jax.ShapeDtypeStruct((LC, ROWS,...]
    ppermute x21, waiting for transfers between devices: 27.7 us -> 25.2 us  [ch_swap(): return lax.ppermute(x, 'ch', [(i, i ^ k) for i in range(4)])]
  transfers between devices with their start and end apart: 29 -> 29, of which waited for: 11 -> 10; matrix products, arithmetic and copies ran while one was open for 6% -> 5% of each run, Pallas kernels for 37% -> 40%
where the time goes in v3:
time: 191 us; the launch traced here: 190 us
  Pallas kernels  83.9 us (44%)
  starting transfers between devices  45.2 us (24%)
  waiting for transfers between devices  36.4 us (19%)
  local copies, waits for them, and re-layouts  16.5 us (9%)
  other arithmetic  4.04 us (2%)
  matrix products  2.7 us (1%)
    pallas_call x2, Pallas kernels, mlp(): pl.pallas_call(functools.partial(mlp_kernel, half), out_shape=[jax.ShapeD...  37.1 us
    ppermute x21, waiting for transfers between devices, ch_swap(): return lax.ppermute(x, 'ch', [(i, i ^ k) for i in range(4)])  25.2 us
    ppermute x21, starting transfers between devices, ch_swap(): return lax.ppermute(x, 'ch', [(i, i ^ k) for i in range(4)])  18.5 us
    ppermute x4, starting transfers between devices, lon_shift(): return lax.ppermute(x, 'lon', [(i, (i + d) % 32) for i in range(32)])  15.4 us
    pallas_call x1, Pallas kernels, conv_backward(): pl.pallas_call(backward_kernel, out_shape=jax.ShapeDtypeStruct((LC, ROWS,...  13.2 us
    unnamed x76, local copies, waits for them, and re-layouts  11.5 us
    ppermute x4, waiting for transfers between devices, lon_shift(): return lax.ppermute(x, 'lon', [(i, (i + d) % 32) for i in range(32)])  11.1 us
    pallas_call x1, Pallas kernels, conv_forward(): pl.pallas_call(forward_kernel, out_shape=[share] * 8, grid_spec=pltpu.Pre...  8.9 us
  transfers between devices with their start and end apart: 29, of which 10 were waited for; matrix products, arithmetic and copies ran while one was open for 5% of the time, Pallas kernels for 40%

profile of v3, /device:TPU:1, one launch (start us, length us, event | category | flops | bytes accessed | tf_op | source)
XLA Modules:
  0.0 189.7 jit_solution(8560774104713425884)
XLA Ops:
  2.8 9.5 %collective-permute-start = (bf16[8,6400]{1,0:T(8,128)(2,1)S(1)}, bf16[8,6400]{1,0:T(8,128)(2,1)}, u32[]{:S(2)}, u32[]{:S(2)}) collective-permute-start(bf16[8,6400]{1,0:T(8,128)(2,1)S(1)} %edge.2.refs_0_), channel_id=1, source_target_pairs={{0,124},{4,0},{8,4},{12,8},{16,12},{20,16},{24,20},{28,24},{32,28}... | collective-permute-start | bytes 307208 | tf_op jit(solution)/shard_map/ppermute | solution.py:48
  17.8 2.4 %collective-permute-start.7 = (bf16[16,104,128]{2,1,0:T(8,128)(2,1)}, bf16[16,104,128]{2,1,0:T(8,128)(2,1)}, u32[]{:S(2)}, u32[]{:S(2)}) collective-permute-start(bf16[16,104,128]{2,1,0:T(8,128)(2,1)} %branch_share.5.refs_0_), channel_id=1, source_target_pairs={{0,3},{1,2},{2,1},{3,0},{4,7},{5,6},{6,5},{7,4},{8,11},{9,10},{10,... | collective-permute-start | bytes 1277960 | tf_op jit(solution)/shard_map/ppermute | solution.py:44
  29.4 8.9 %conv_forward.1 = (bf16[8,104,128]{2,1,0:T(8,128)(2,1)}, bf16[8,104,128]{2,1,0:T(8,128)(2,1)}, bf16[8,104,128]{2,1,0:T(8,128)(2,1)}, bf16[8,104,128]{2,1,0:T(8,1...) custom-call(s32[1]{0:T(128)} %bitcast.me_ref, ...), custom_call_target="tpu_custom_call" | custom-call | bytes 29700000 | tf_op jit(solution)/shard_map/conv_forward/pallas_call | solution.py:131
  38.3 2.2 %collective-permute-start.2 = (bf16[8,104,128]{2,1,0:T(8,128)(2,1)}, bf16[8,104,128]{2,1,0:T(8,128)(2,1)S(1)}, u32[]{:S(2)}, u32[]{:S(2)}) collective-permute-start(bf16[8,104,128]{2,1,0:T(8,128)(2,1)} %get-tuple-element.77), channel_id=1, source_target_pairs={{0,1},{1,0},{2,3},{3,2},{4,5},{5,4},{6,7},{7,6},{8,9},{9,8},{10,11... | collective-permute-start | bytes 638984 | tf_op jit(solution)/shard_map/ppermute | solution.py:44
  41.9 3.7 %padded_weights.1 = (bf16[416,1600]{1,0:T(8,128)(2,1)}, bf16[1600,416]{1,0:T(8,128)(2,1)}, bf16[416,1600]{1,0:T(8,128)(2,1)}, bf16[1600,416]{1,0:T(8,128)(2,1)}) custom-call(bf16[400,1600]{1,0:T(8,128)(2,1)S(1)} %copy-done.11, bf16[400,1600]{1,0:T(8,128)(2,1)S(1)} %bitcast.27, bf16[400,416]{1,0:T(8,128)(2,1)S(1)} %copy-done.10, ...), custom_call_target="tpu_custom_call" | custom-call | bytes 16500000 | tf_op jit(solution)/shard_map/padded_weights/pallas_call | solution.py:418
  51.0 2.5 %collective-permute-done.4.refs_3_ = bf16[8,104,128]{2,1,0:T(8,128)(2,1)} collective-permute-done((bf16[8,104,128]{2,1,0:T(8,128)(2,1)S(1)}, bf16[8,104,128]{2,1,0:T(8,128)(2,1)}, u32[]{:S(2)}, u32[]{:S(2)}) %collective-permute-start.4) | collective-permute-done | bytes 213024 | tf_op jit(solution)/shard_map/ppermute | solution.py:44
  53.5 15.0 %mlp_a.1 = (bf16[2,8,104,128]{3,2,1,0:T(8,128)(2,1)}, bf16[2,8,104,128]{3,2,1,0:T(8,128)(2,1)}, bf16[2,8,104,128]{3,2,1,0:T(8,128)(2,1)}, bf16[2,8,104,128]{3,2,...) custom-call(s32[1]{0:T(128)} %bitcast.me_ref, s32[1]{0:T(128)} %bitcast.1.core_ref, ...), custom_call_target="tpu_custom_call" | custom-call | bytes 46200000 | tf_op jit(solution)/shard_map/mlp_a/pallas_call | solution.py:334
  71.5 22.1 %mlp_b.1 = (bf16[8,104,128]{2,1,0:T(8,128)(2,1)}, bf16[8,104,128]{2,1,0:T(8,128)(2,1)}, bf16[8,104,128]{2,1,0:T(8,128)(2,1)}, bf16[8,104,128]{2,1,0:T(8,128)(2,1...) custom-call(s32[1]{0:T(128)} %bitcast.me_ref, ...), custom_call_target="tpu_custom_call" | custom-call | bytes 72600000 | tf_op jit(solution)/shard_map/mlp_b/pallas_call | solution.py:334
  94.5 3.3 %collective-permute-done.14 = bf16[5248,128]{1,0:T(8,128)(2,1)S(1)} collective-permute-done((bf16[5248,128]{1,0:T(8,128)(2,1)}, bf16[5248,128]{1,0:T(8,128)(2,1)S(1)}, u32[]{:S(2)}, u32[]{:S(2)}) %collective-permute-start.14) | collective-permute-done | bytes 1343520 | tf_op jit(solution)/shard_map/ppermute | solution.py:44
  97.7 2.7 %add_convert_fusion = bf16[5248,128]{1,0:T(8,128)(2,1)} fusion(bf16[5248,128]{1,0:T(8,128)(2,1)S(1)} %collective-permute-done.14, bf16[5248,128]{1,0:T(8,128)(2,1)} %get-tuple-element.116), kind=kLoop, calls=%fused_computation.1 | loop fusion | flops 2686976 | bytes 4030464 | tf_op jit(solution)/shard_map/convert_element_type | solution.py:566
  100.5 4.5 %all-to-all-start = ((bf16[16,328,128]{2,1,0:T(8,128)(2,1)}), bf16[16,328,128]{2,1,0:T(8,128)(2,1)S(1)}, u32[]{:S(2)}, u32[]{:S(2)}) async-start(bf16[16,328,128]{2,1,0:T(8,128)(2,1)} %bitcast.28), calls=%async_computation | async-start | bytes 2686976 | tf_op jit(solution)/shard_map/all_to_all | solution.py:523
  109.4 3.1 %collective-permute-done.16.refs_6_ = bf16[8,104,128]{2,1,0:T(8,128)(2,1)S(1)} collective-permute-done((bf16[8,104,128]{2,1,0:T(8,128)(2,1)}, bf16[8,104,128]{2,1,0:T(8,128)(2,1)S(1)}, u32[]{:S(2)}, u32[]{:S(2)}) %collective-permute-start.16) | collective-permute-done | bytes 213024 | tf_op jit(solution)/shard_map/ppermute | solution.py:44
  112.5 5.5 %collective-permute-done.17.refs_7_ = bf16[8,104,128]{2,1,0:T(8,128)(2,1)S(1)} collective-permute-done((bf16[8,104,128]{2,1,0:T(8,128)(2,1)}, bf16[8,104,128]{2,1,0:T(8,128)(2,1)S(1)}, u32[]{:S(2)}, u32[]{:S(2)}) %collective-permute-start.17) | collective-permute-done | bytes 213024 | tf_op jit(solution)/shard_map/ppermute | solution.py:44
  118.0 3.6 %collective-permute-done.19.refs_2_.refs_6_ = bf16[8,104,128]{2,1,0:T(8,128)(2,1)S(1)} collective-permute-done((bf16[8,104,128]{2,1,0:T(8,128)(2,1)}, bf16[8,104,128]{2,1,0:T(8,128)(2,1)S(1)}, u32[]{:S(2)}, u32[]{:S(2)}) %collective-permute-start.19) | collective-permute-done | bytes 213024 | tf_op jit(solution)/shard_map/ppermute | solution.py:44
  122.3 4.4 %collective-permute-done.20.refs_3_.refs_7_ = bf16[8,104,128]{2,1,0:T(8,128)(2,1)S(1)} collective-permute-done((bf16[8,104,128]{2,1,0:T(8,128)(2,1)}, bf16[8,104,128]{2,1,0:T(8,128)(2,1)S(1)}, u32[]{:S(2)}, u32[]{:S(2)}) %collective-permute-start.20) | collective-permute-done | bytes 213024 | tf_op jit(solution)/shard_map/ppermute | solution.py:44
  127.4 2.2 %piece_edges.1 = (bf16[8,8,832]{2,1,0:T(8,128)(2,1)}, bf16[8,8,832]{2,1,0:T(8,128)(2,1)}) custom-call(bf16[16,128]{1,0:T(8,128)(2,1)S(1)} %pad_maximum_fusion.1.pick, bf16[2,8,104,128]{3,2,1,0:T(8,128)(2,1)S(1)} %copy-done.4, bf16[2,8,104,128]{3,2,1,0:T(8,128)(2,1)S(1)} %collective-permute-done.11.refs_1_, bf16[2,8,104,128]{3,2,1,0:T(8,128)(2,1)S(1)} %copy-done.7, ...), custom_call_target="tpu_custom_call" | custom-call | bytes 6600000 | tf_op jit(solution)/shard_map/piece_edges/pallas_call | solution.py:481
  136.4 5.8 %collective-permute-start.24 = (bf16[8,8,832]{2,1,0:T(8,128)(2,1)S(1)}, bf16[8,8,832]{2,1,0:T(8,128)(2,1)S(1)}, u32[]{:S(2)}, u32[]{:S(2)}) collective-permute-start(bf16[8,8,832]{2,1,0:T(8,128)(2,1)S(1)} %copy-done.36), channel_id=1, source_target_pairs={{0,124},{4,0},{8,4},{12,8},{16,12},{20,16},{24,20},{28,24},{32,28}... | collective-permute-start | bytes 319496 | tf_op jit(solution)/shard_map/ppermute | solution.py:48
  144.0 7.6 %collective-permute-done.25.refs_1_.last = bf16[8,8,832]{2,1,0:T(8,128)(2,1)S(1)} collective-permute-done((bf16[8,8,832]{2,1,0:T(8,128)(2,1)S(1)}, bf16[8,8,832]{2,1,0:T(8,128)(2,1)S(1)}, u32[]{:S(2)}, u32[]{:S(2)}) %collective-permute-start.25) | collective-permute-done | bytes 106528 | tf_op jit(solution)/shard_map/ppermute | solution.py:48
  152.8 4.4 %all-to-all-start.1 = ((bf16[16,328,128]{2,1,0:T(8,128)(2,1)}), bf16[16,328,128]{2,1,0:T(8,128)(2,1)}, u32[]{:S(2)}, u32[]{:S(2)}) async-start(bf16[16,328,128]{2,1,0:T(8,128)(2,1)} %plane_copies.1), calls=%async_computation.1 | async-start | bytes 2686976 | tf_op jit(solution)/shard_map/all_to_all | solution.py:523
  158.2 5.1 %update.1 = bf16[100,64,128]{2,1,0:T(8,128)(2,1)} custom-call(s32[1]{0:T(128)} %bitcast.me_ref, bf16[2,8,104,128]{3,2,1,0:T(8,128)(2,1)} %get-tuple-element.118.refs_16_.refs_0_, bf16[2,8,104,128]{3,2,1,0:T(8,128)(2,1)} %copy-done.5, bf16[2,8,104,128]{3,2,1,0:T(8,128)(2,1)} %copy-done.6, bf16[2,8,104,128]{3,2,1,0:T(8,128)(2,1)} %collective-permute-done.13.refs_3_, ...), custom_call_target="tpu_custom_call" | custom-call | bytes 14520000 | tf_op jit(solution)/shard_map/update/pallas_call | solution.py:378
  165.1 13.2 %conv_backward.1 = bf16[100,64,128]{2,1,0:T(8,128)(2,1)} custom-call(s32[1]{0:T(128)} %bitcast.me_ref, bf16[2,8,104,128]{3,2,1,0:T(8,128)(2,1)} %get-tuple-element.118.refs_16_.refs_0_, bf16[2,8,104,128]{3,2,1,0:T(8,128)(2,1)} %copy-done.5, bf16[2,8,104,128]{3,2,1,0:T(8,128)(2,1)} %copy-done.6, bf16[2,8,104,128]{3,2,1,0:T(8,128)(2,1)} %collective-permute-done.13.refs_3_, ...), custom_call_target="tpu_custom_call" | custom-call | bytes 33000000 | tf_op jit(solution)/shard_map/conv_backward/pallas_call | solution.py:171
  178.3 2.6 %collective-permute-start.26 = (bf16[5248,128]{1,0:T(8,128)(2,1)}, bf16[5248,128]{1,0:T(8,128)(2,1)S(1)}, u32[]{:S(2)}, u32[]{:S(2)}) collective-permute-start(bf16[5248,128]{1,0:T(8,128)(2,1)} %bitcast.9.own), channel_id=1, source_target_pairs={{0,1},{1,0},{2,3},{3,2},{4,5},{5,4},{6,7},{7,6},{8,9},{9,8},{10,11... | collective-permute-start | bytes 4030472 | tf_op jit(solution)/shard_map/ppermute | solution.py:44
  181.1 2.8 %collective-permute-done.26.other = bf16[5248,128]{1,0:T(8,128)(2,1)S(1)} collective-permute-done((bf16[5248,128]{1,0:T(8,128)(2,1)}, bf16[5248,128]{1,0:T(8,128)(2,1)S(1)}, u32[]{:S(2)}, u32[]{:S(2)}) %collective-permute-start.26) | collective-permute-done | bytes 1343520 | tf_op jit(solution)/shard_map/ppermute | solution.py:44
  183.8 5.9 %finish.1 = (f32[400,1600]{1,0:T(8,128)}, f32[400,1600]{1,0:T(8,128)}) custom-call(s32[1]{0:T(128)} %bitcast.1.core_ref, bf16[5248,128]{1,0:T(8,128)(2,1)} %bitcast.9.own, bf16[5248,128]{1,0:T(8,128)(2,1)S(1)} %collective-permute-done.26.other, bf16[400,416]{1,0:T(8,128)(2,1)S(1)} %fusion.1.pad), custom_call_target="tpu_custom_call" | custom-call | bytes 19800000 | tf_op jit(solution)/shard_map/finish/pallas_call | solution.py:593
  (155 shorter events, 45.7 us)
Async XLA Ops:
  2.8 24.8 %collective-permute-start = (bf16[8,6400]{1,0:T(8,128)(2,1)S(1)}, bf16[8,6400]{1,0:T(8,128)(2,1)}, u32[]{:S(2)}, u32[]{:S(2)}) collective-permute-start(bf16[8,6400]{1,0:T(8,128)(2,1)S(1)} %edge.2.refs_0_), channel_id=1, source_target_pairs={{0,124},{4,0},{8,4},{12,8},{16,12},{20,16},{24,20},{28,24},{32,28}... | collective-permute-start | bytes 307208 | tf_op jit(solution)/shard_map/ppermute | solution.py:48
  15.1 31.9 %collective-permute-start.6 = (bf16[16,104,128]{2,1,0:T(8,128)(2,1)}, bf16[16,104,128]{2,1,0:T(8,128)(2,1)}, u32[]{:S(2)}, u32[]{:S(2)}) collective-permute-start(bf16[16,104,128]{2,1,0:T(8,128)(2,1)} %branch_share.4.refs_0_), channel_id=1, source_target_pairs={{0,2},{1,3},{2,0},{3,1},{4,6},{5,7},{6,4},{7,5},{8,10},{9,11},{10,... | collective-permute-start | bytes 1277960 | tf_op jit(solution)/shard_map/ppermute | solution.py:44
  16.6 11.0 %collective-permute-start.1 = (bf16[8,6400]{1,0:T(8,128)(2,1)}, bf16[8,6400]{1,0:T(8,128)(2,1)}, u32[]{:S(2)}, u32[]{:S(2)}) collective-permute-start(bf16[8,6400]{1,0:T(8,128)(2,1)} %edge.3.refs_0_), channel_id=1, source_target_pairs={{0,4},{4,8},{8,12},{12,16},{16,20},{20,24},{24,28},{28,32},{32,36}... | collective-permute-start | bytes 307208 | tf_op jit(solution)/shard_map/ppermute | solution.py:48
  17.8 29.1 %collective-permute-start.7 = (bf16[16,104,128]{2,1,0:T(8,128)(2,1)}, bf16[16,104,128]{2,1,0:T(8,128)(2,1)}, u32[]{:S(2)}, u32[]{:S(2)}) collective-permute-start(bf16[16,104,128]{2,1,0:T(8,128)(2,1)} %branch_share.5.refs_0_), channel_id=1, source_target_pairs={{0,3},{1,2},{2,1},{3,0},{4,7},{5,6},{6,5},{7,4},{8,11},{9,10},{10,... | collective-permute-start | bytes 1277960 | tf_op jit(solution)/shard_map/ppermute | solution.py:44
  21.4 24.3 %collective-permute-start.5 = (bf16[16,104,128]{2,1,0:T(8,128)(2,1)}, bf16[16,104,128]{2,1,0:T(8,128)(2,1)}, u32[]{:S(2)}, u32[]{:S(2)}) collective-permute-start(bf16[16,104,128]{2,1,0:T(8,128)(2,1)} %branch_share.6.refs_0_), channel_id=1, source_target_pairs={{0,1},{1,0},{2,3},{3,2},{4,5},{5,4},{6,7},{7,6},{8,9},{9,8},{10,11... | collective-permute-start | bytes 1277960 | tf_op jit(solution)/shard_map/ppermute | solution.py:44
  38.3 9.5 %collective-permute-start.2 = (bf16[8,104,128]{2,1,0:T(8,128)(2,1)}, bf16[8,104,128]{2,1,0:T(8,128)(2,1)S(1)}, u32[]{:S(2)}, u32[]{:S(2)}) collective-permute-start(bf16[8,104,128]{2,1,0:T(8,128)(2,1)} %get-tuple-element.77), channel_id=1, source_target_pairs={{0,1},{1,0},{2,3},{3,2},{4,5},{5,4},{6,7},{7,6},{8,9},{9,8},{10,11... | collective-permute-start | bytes 638984 | tf_op jit(solution)/shard_map/ppermute | solution.py:44
  40.5 10.4 %collective-permute-start.3 = (bf16[8,104,128]{2,1,0:T(8,128)(2,1)}, bf16[8,104,128]{2,1,0:T(8,128)(2,1)}, u32[]{:S(2)}, u32[]{:S(2)}) collective-permute-start(bf16[8,104,128]{2,1,0:T(8,128)(2,1)} %get-tuple-element.78), channel_id=1, source_target_pairs={{0,2},{1,3},{2,0},{3,1},{4,6},{5,7},{6,4},{7,5},{8,10},{9,11},{10,... | collective-permute-start | bytes 638984 | tf_op jit(solution)/shard_map/ppermute | solution.py:44
  45.6 7.8 %collective-permute-start.4 = (bf16[8,104,128]{2,1,0:T(8,128)(2,1)S(1)}, bf16[8,104,128]{2,1,0:T(8,128)(2,1)}, u32[]{:S(2)}, u32[]{:S(2)}) collective-permute-start(bf16[8,104,128]{2,1,0:T(8,128)(2,1)S(1)} %copy-done.34), channel_id=1, source_target_pairs={{0,3},{1,2},{2,1},{3,0},{4,7},{5,6},{6,5},{7,4},{8,11},{9,10},{10,... | collective-permute-start | bytes 638984 | tf_op jit(solution)/shard_map/ppermute | solution.py:44
  47.0 21.6 %collective-permute-start.10 = (bf16[8,104,128]{2,1,0:T(8,128)(2,1)}, bf16[8,104,128]{2,1,0:T(8,128)(2,1)S(1)}, u32[]{:S(2)}, u32[]{:S(2)}) collective-permute-start(bf16[8,104,128]{2,1,0:T(8,128)(2,1)} %get-tuple-element.103), channel_id=1, source_target_pairs={{0,3},{1,2},{2,1},{3,0},{4,7},{5,6},{6,5},{7,4},{8,11},{9,10},{10,... | collective-permute-start | bytes 638984 | tf_op jit(solution)/shard_map/ppermute | solution.py:44
  47.4 21.2 %collective-permute-start.8 = (bf16[8,104,128]{2,1,0:T(8,128)(2,1)}, bf16[8,104,128]{2,1,0:T(8,128)(2,1)S(1)}, u32[]{:S(2)}, u32[]{:S(2)}) collective-permute-start(bf16[8,104,128]{2,1,0:T(8,128)(2,1)} %get-tuple-element.101), channel_id=1, source_target_pairs={{0,1},{1,0},{2,3},{3,2},{4,5},{5,4},{6,7},{7,6},{8,9},{9,8},{10,11... | collective-permute-start | bytes 638984 | tf_op jit(solution)/shard_map/ppermute | solution.py:44
  47.7 20.8 %collective-permute-start.9 = (bf16[8,104,128]{2,1,0:T(8,128)(2,1)}, bf16[8,104,128]{2,1,0:T(8,128)(2,1)S(1)}, u32[]{:S(2)}, u32[]{:S(2)}) collective-permute-start(bf16[8,104,128]{2,1,0:T(8,128)(2,1)} %get-tuple-element.102), channel_id=1, source_target_pairs={{0,2},{1,3},{2,0},{3,1},{4,6},{5,7},{6,4},{7,5},{8,10},{9,11},{10,... | collective-permute-start | bytes 638984 | tf_op jit(solution)/shard_map/ppermute | solution.py:44
  69.3 24.2 %collective-permute-start.11 = (bf16[2,8,104,128]{3,2,1,0:T(8,128)(2,1)}, bf16[2,8,104,128]{3,2,1,0:T(8,128)(2,1)S(1)}, u32[]{:S(2)}, u32[]{:S(2)}) collective-permute-start(bf16[2,8,104,128]{3,2,1,0:T(8,128)(2,1)} %get-tuple-element.113), channel_id=1, source_target_pairs={{0,1},{1,0},{2,3},{3,2},{4,5},{5,4},{6,7},{7,6},{8,9},{9,8},{10,11... | collective-permute-start | bytes 1277960 | tf_op jit(solution)/shard_map/ppermute | solution.py:44
  69.4 24.2 %collective-permute-start.12 = (bf16[2,8,104,128]{3,2,1,0:T(8,128)(2,1)}, bf16[2,8,104,128]{3,2,1,0:T(8,128)(2,1)S(1)}, u32[]{:S(2)}, u32[]{:S(2)}) collective-permute-start(bf16[2,8,104,128]{3,2,1,0:T(8,128)(2,1)} %get-tuple-element.114), channel_id=1, source_target_pairs={{0,2},{1,3},{2,0},{3,1},{4,6},{5,7},{6,4},{7,5},{8,10},{9,11},{10,... | collective-permute-start | bytes 1277960 | tf_op jit(solution)/shard_map/ppermute | solution.py:44
  70.5 24.0 %collective-permute-start.13 = (bf16[2,8,104,128]{3,2,1,0:T(8,128)(2,1)}, bf16[2,8,104,128]{3,2,1,0:T(8,128)(2,1)}, u32[]{:S(2)}, u32[]{:S(2)}) collective-permute-start(bf16[2,8,104,128]{3,2,1,0:T(8,128)(2,1)} %get-tuple-element.115), channel_id=1, source_target_pairs={{0,3},{1,2},{2,1},{3,0},{4,7},{5,6},{6,5},{7,4},{8,11},{9,10},{10,... | collective-permute-start | bytes 1277960 | tf_op jit(solution)/shard_map/ppermute | solution.py:44
  100.5 30.5 %all-to-all-start = ((bf16[16,328,128]{2,1,0:T(8,128)(2,1)}), bf16[16,328,128]{2,1,0:T(8,128)(2,1)S(1)}, u32[]{:S(2)}, u32[]{:S(2)}) async-start(bf16[16,328,128]{2,1,0:T(8,128)(2,1)} %bitcast.28), calls=%async_computation | async-start | bytes 2686976 | tf_op jit(solution)/shard_map/all_to_all | solution.py:523
  105.6 12.4 %collective-permute-start.17 = (bf16[8,104,128]{2,1,0:T(8,128)(2,1)}, bf16[8,104,128]{2,1,0:T(8,128)(2,1)S(1)}, u32[]{:S(2)}, u32[]{:S(2)}) collective-permute-start(bf16[8,104,128]{2,1,0:T(8,128)(2,1)} %get-tuple-element.125), channel_id=1, source_target_pairs={{0,3},{1,2},{2,1},{3,0},{4,7},{5,6},{6,5},{7,4},{8,11},{9,10},{10,... | collective-permute-start | bytes 638984 | tf_op jit(solution)/shard_map/ppermute | solution.py:44
  107.2 10.8 %collective-permute-start.18 = (bf16[8,104,128]{2,1,0:T(8,128)(2,1)}, bf16[8,104,128]{2,1,0:T(8,128)(2,1)S(1)}, u32[]{:S(2)}, u32[]{:S(2)}) collective-permute-start(bf16[8,104,128]{2,1,0:T(8,128)(2,1)} %get-tuple-element.127), channel_id=1, source_target_pairs={{0,1},{1,0},{2,3},{3,2},{4,5},{5,4},{6,7},{7,6},{8,9},{9,8},{10,11... | collective-permute-start | bytes 638984 | tf_op jit(solution)/shard_map/ppermute | solution.py:44
  107.4 14.3 %collective-permute-start.19 = (bf16[8,104,128]{2,1,0:T(8,128)(2,1)}, bf16[8,104,128]{2,1,0:T(8,128)(2,1)S(1)}, u32[]{:S(2)}, u32[]{:S(2)}) collective-permute-start(bf16[8,104,128]{2,1,0:T(8,128)(2,1)} %get-tuple-element.128), channel_id=1, source_target_pairs={{0,2},{1,3},{2,0},{3,1},{4,6},{5,7},{6,4},{7,5},{8,10},{9,11},{10,... | collective-permute-start | bytes 638984 | tf_op jit(solution)/shard_map/ppermute | solution.py:44
  107.7 19.0 %collective-permute-start.20 = (bf16[8,104,128]{2,1,0:T(8,128)(2,1)}, bf16[8,104,128]{2,1,0:T(8,128)(2,1)S(1)}, u32[]{:S(2)}, u32[]{:S(2)}) collective-permute-start(bf16[8,104,128]{2,1,0:T(8,128)(2,1)} %get-tuple-element.129), channel_id=1, source_target_pairs={{0,3},{1,2},{2,1},{3,0},{4,7},{5,6},{6,5},{7,4},{8,11},{9,10},{10,... | collective-permute-start | bytes 638984 | tf_op jit(solution)/shard_map/ppermute | solution.py:44
  133.0 9.2 %collective-permute-start.21 = (bf16[328,128]{1,0:T(8,128)(2,1)S(1)}, bf16[328,128]{1,0:T(8,128)(2,1)S(1)}, u32[]{:S(2)}, u32[]{:S(2)}) collective-permute-start(bf16[328,128]{1,0:T(8,128)(2,1)S(1)} %plane_total.1), channel_id=1, source_target_pairs={{0,64},{4,68},{8,72},{12,76},{16,80},{20,84},{24,88},{28,92},{32,9... | collective-permute-start | bytes 251912 | tf_op jit(solution)/shard_map/ppermute | solution.py:52
  134.6 7.6 %collective-permute-start.22 = (bf16[328,128]{1,0:T(8,128)(2,1)S(1)}, bf16[328,128]{1,0:T(8,128)(2,1)S(1)}, u32[]{:S(2)}, u32[]{:S(2)}) collective-permute-start(bf16[328,128]{1,0:T(8,128)(2,1)S(1)} %plane_total.1), channel_id=1, source_target_pairs={{0,2},{1,3},{2,0},{3,1},{4,6},{5,7},{6,4},{7,5},{8,10},{9,11},{10,... | collective-permute-start | bytes 251912 | tf_op jit(solution)/shard_map/ppermute | solution.py:44
  136.4 7.6 %collective-permute-start.24 = (bf16[8,8,832]{2,1,0:T(8,128)(2,1)S(1)}, bf16[8,8,832]{2,1,0:T(8,128)(2,1)S(1)}, u32[]{:S(2)}, u32[]{:S(2)}) collective-permute-start(bf16[8,8,832]{2,1,0:T(8,128)(2,1)S(1)} %copy-done.36), channel_id=1, source_target_pairs={{0,124},{4,0},{8,4},{12,8},{16,12},{20,16},{24,20},{28,24},{32,28}... | collective-permute-start | bytes 319496 | tf_op jit(solution)/shard_map/ppermute | solution.py:48
  142.2 9.4 %collective-permute-start.25 = (bf16[8,8,832]{2,1,0:T(8,128)(2,1)S(1)}, bf16[8,8,832]{2,1,0:T(8,128)(2,1)S(1)}, u32[]{:S(2)}, u32[]{:S(2)}) collective-permute-start(bf16[8,8,832]{2,1,0:T(8,128)(2,1)S(1)} %copy-done.35), channel_id=1, source_target_pairs={{0,4},{4,8},{8,12},{12,16},{16,20},{20,24},{24,28},{28,32},{32,36}... | collective-permute-start | bytes 319496 | tf_op jit(solution)/shard_map/ppermute | solution.py:48
  152.8 25.5 %all-to-all-start.1 = ((bf16[16,328,128]{2,1,0:T(8,128)(2,1)}), bf16[16,328,128]{2,1,0:T(8,128)(2,1)}, u32[]{:S(2)}, u32[]{:S(2)}) async-start(bf16[16,328,128]{2,1,0:T(8,128)(2,1)} %plane_copies.1), calls=%async_computation.1 | async-start | bytes 2686976 | tf_op jit(solution)/shard_map/all_to_all | solution.py:523
  (42 other events, 316.8 us)

commit v4 on v3

--- a/solution.py
+++ b/solution.py
@@ -562,18 +562,15 @@
     )(part, *after)
 
 
-def reduce_gradients(keep, send, late, first, last):
-    mine = (keep.astype(F32) + ch_swap(send, 1).astype(F32)).astype(BF)
+def reduce_gradients(mine, late, from_right, from_left):
     mine = plane_exchange(mine.reshape(16, PIECE, LANES))
-    mine, first, last = lax.optimization_barrier((mine, first, last))
-    from_right, from_left = lon_shift(first, -1), lon_shift(last, 1)
+    mine, from_right, from_left = lax.optimization_barrier((mine, from_right, from_left))
     wire = plane_total(mine, late)
     part = (
         (wire.astype(F32) + lon_swap(wire, 16).astype(F32))
         + (ch_swap(wire, 2).astype(F32) + both_swap(wire).astype(F32))
     ).astype(BF)
-    copies = plane_copies(part, (from_right, from_left))
-    return plane_exchange(copies).reshape(WIRE, LANES), from_right, from_left
+    return plane_exchange(plane_copies(part, ())).reshape(WIRE, LANES), from_right, from_left
 
 
 def finish_kernel(core_ref, own, other, pad, grad_in, grad_out, held):
@@ -672,14 +669,14 @@
     early = [early[0]] + [ch_swap(early[k], k) for k in (1, 2, 3)]
     keep, send, early = lax.optimization_barrier((keep, send, early))
     grad_b = [grad_b[0]] + [ch_swap(grad_b[k], k) for k in (1, 2, 3)]
+    mine = (keep.astype(F32) + ch_swap(send, 1).astype(F32)).astype(BF)
+    mine, grad_b, branch_b = lax.optimization_barrier((mine, grad_b, branch_b))
     branch_b = [branch_b[0]] + [ch_swap(branch_b[k], k) for k in (1, 2, 3)]
-    grad_b, branch_b = lax.optimization_barrier((grad_b, branch_b))
     updated = update(me, early, branch_b, ocean_state, sea_mask, scale)
     picks = jnp.concatenate([head, tail], 0)
     first, last = piece_edges(picks, early, grad_b)
-    own, from_right, from_left = reduce_gradients(
-        keep, send, branch_b[1:], first, last
-    )
+    from_right, from_left = lon_shift(first, -1), lon_shift(last, 1)
+    own, from_right, from_left = reduce_gradients(mine, branch_b[1:], from_right, from_left)
     grad_rims = piece_rims(picks, from_right, from_left)
 
     grad_state = conv_backward(

time: 191 us -> 181 us (0.948)
  waiting for transfers between devices: 36.4 us -> 27.4 us
  local copies, waits for them, and re-layouts: 16.5 us -> 13.5 us
  starting transfers between devices: 45.2 us -> 47.9 us
    ppermute x21, waiting for transfers between devices: 25.2 us -> 13.2 us  [ch_swap(): return lax.ppermute(x, 'ch', [(i, i ^ k) for i in range(4)])]
    unnamed x76 -> x64, local copies, waits for them, and re-layouts: 11.5 us -> 8.55 us
  transfers between devices with their start and end apart: 29 -> 29, of which waited for: 10 -> 11; matrix products, arithmetic and copies ran while one was open for 5% -> 6% of each run, Pallas kernels for 40% -> 42%
where the time goes in v4:
time: 181 us; the launch traced here: 180 us
  Pallas kernels  84 us (46%)
  starting transfers between devices  47.9 us (26%)
  waiting for transfers between devices  27.4 us (15%)
  local copies, waits for them, and re-layouts  13.5 us (7%)
  other arithmetic  4.04 us (2%)
  matrix products  2.7 us (1%)
    pallas_call x2, Pallas kernels, mlp(): pl.pallas_call(functools.partial(mlp_kernel, half), out_shape=[jax.ShapeD...  37.1 us
    ppermute x21, starting transfers between devices, ch_swap(): return lax.ppermute(x, 'ch', [(i, i ^ k) for i in range(4)])  18.5 us
    ppermute x4, starting transfers between devices, lon_shift(): return lax.ppermute(x, 'lon', [(i, (i + d) % 32) for i in range(32)])  15.4 us
    ppermute x21, waiting for transfers between devices, ch_swap(): return lax.ppermute(x, 'ch', [(i, i ^ k) for i in range(4)])  13.2 us
    pallas_call x1, Pallas kernels, conv_backward(): pl.pallas_call(backward_kernel, out_shape=jax.ShapeDtypeStruct((LC, ROWS,...  13.2 us
    ppermute x4, waiting for transfers between devices, lon_shift(): return lax.ppermute(x, 'lon', [(i, (i + d) % 32) for i in range(32)])  12.1 us
    all_to_all x2, starting transfers between devices, plane_exchange(): return lax.all_to_all(pieces, 'lon', 0, 0, axis_index_groups=PLANES)  9.95 us
    pallas_call x1, Pallas kernels, conv_forward(): pl.pallas_call(forward_kernel, out_shape=[share] * 8, grid_spec=pltpu.Pre...  8.96 us
  transfers between devices with their start and end apart: 29, of which 11 were waited for; matrix products, arithmetic and copies ran while one was open for 6% of the time, Pallas kernels for 42%

profile of v4, /device:TPU:1, one launch (start us, length us, event | category | flops | bytes accessed | tf_op | source)
XLA Modules:
  0.0 180.5 jit_solution(13890155985669668648)
XLA Ops:
  2.8 9.5 %collective-permute-start = (bf16[8,6400]{1,0:T(8,128)(2,1)S(1)}, bf16[8,6400]{1,0:T(8,128)(2,1)}, u32[]{:S(2)}, u32[]{:S(2)}) collective-permute-start(bf16[8,6400]{1,0:T(8,128)(2,1)S(1)} %edge.2.refs_0_), channel_id=1, source_target_pairs={{0,124},{4,0},{8,4},{12,8},{16,12},{20,16},{24,20},{28,24},{32,28}... | collective-permute-start | bytes 307208 | tf_op jit(solution)/shard_map/ppermute | solution.py:48
  17.8 2.4 %collective-permute-start.7 = (bf16[16,104,128]{2,1,0:T(8,128)(2,1)}, bf16[16,104,128]{2,1,0:T(8,128)(2,1)}, u32[]{:S(2)}, u32[]{:S(2)}) collective-permute-start(bf16[16,104,128]{2,1,0:T(8,128)(2,1)} %branch_share.5.refs_0_), channel_id=1, source_target_pairs={{0,3},{1,2},{2,1},{3,0},{4,7},{5,6},{6,5},{7,4},{8,11},{9,10},{10,... | collective-permute-start | bytes 1277960 | tf_op jit(solution)/shard_map/ppermute | solution.py:44
  25.7 1.9 %collective-permute-done.1 = bf16[8,6400]{1,0:T(8,128)(2,1)} collective-permute-done((bf16[8,6400]{1,0:T(8,128)(2,1)}, bf16[8,6400]{1,0:T(8,128)(2,1)}, u32[]{:S(2)}, u32[]{:S(2)}) %collective-permute-start.1) | collective-permute-done | bytes 102432 | tf_op jit(solution)/shard_map/ppermute | solution.py:48
  29.4 9.0 %conv_forward.1 = (bf16[8,104,128]{2,1,0:T(8,128)(2,1)}, bf16[8,104,128]{2,1,0:T(8,128)(2,1)}, bf16[8,104,128]{2,1,0:T(8,128)(2,1)}, bf16[8,104,128]{2,1,0:T(8,1...) custom-call(s32[1]{0:T(128)} %bitcast.me_ref, ...), custom_call_target="tpu_custom_call" | custom-call | bytes 29700000 | tf_op jit(solution)/shard_map/conv_forward/pallas_call | solution.py:131
  38.4 2.2 %collective-permute-start.2 = (bf16[8,104,128]{2,1,0:T(8,128)(2,1)}, bf16[8,104,128]{2,1,0:T(8,128)(2,1)S(1)}, u32[]{:S(2)}, u32[]{:S(2)}) collective-permute-start(bf16[8,104,128]{2,1,0:T(8,128)(2,1)} %get-tuple-element.78), channel_id=1, source_target_pairs={{0,1},{1,0},{2,3},{3,2},{4,5},{5,4},{6,7},{7,6},{8,9},{9,8},{10,11... | collective-permute-start | bytes 638984 | tf_op jit(solution)/shard_map/ppermute | solution.py:44
  41.9 3.7 %padded_weights.1 = (bf16[416,1600]{1,0:T(8,128)(2,1)}, bf16[1600,416]{1,0:T(8,128)(2,1)}, bf16[416,1600]{1,0:T(8,128)(2,1)}, bf16[1600,416]{1,0:T(8,128)(2,1)}) custom-call(bf16[400,1600]{1,0:T(8,128)(2,1)S(1)} %copy-done.11, bf16[400,1600]{1,0:T(8,128)(2,1)S(1)} %bitcast.27, bf16[400,416]{1,0:T(8,128)(2,1)S(1)} %copy-done.10, ...), custom_call_target="tpu_custom_call" | custom-call | bytes 16500000 | tf_op jit(solution)/shard_map/padded_weights/pallas_call | solution.py:418
  51.0 2.5 %collective-permute-done.4.refs_3_ = bf16[8,104,128]{2,1,0:T(8,128)(2,1)} collective-permute-done((bf16[8,104,128]{2,1,0:T(8,128)(2,1)S(1)}, bf16[8,104,128]{2,1,0:T(8,128)(2,1)}, u32[]{:S(2)}, u32[]{:S(2)}) %collective-permute-start.4) | collective-permute-done | bytes 213024 | tf_op jit(solution)/shard_map/ppermute | solution.py:44
  53.5 15.0 %mlp_a.1 = (bf16[2,8,104,128]{3,2,1,0:T(8,128)(2,1)}, bf16[2,8,104,128]{3,2,1,0:T(8,128)(2,1)}, bf16[2,8,104,128]{3,2,1,0:T(8,128)(2,1)}, bf16[2,8,104,128]{3,2,...) custom-call(s32[1]{0:T(128)} %bitcast.me_ref, s32[1]{0:T(128)} %bitcast.1.core_ref, ...), custom_call_target="tpu_custom_call" | custom-call | bytes 46200000 | tf_op jit(solution)/shard_map/mlp_a/pallas_call | solution.py:334
  71.6 22.1 %mlp_b.1 = (bf16[8,104,128]{2,1,0:T(8,128)(2,1)}, bf16[8,104,128]{2,1,0:T(8,128)(2,1)}, bf16[8,104,128]{2,1,0:T(8,128)(2,1)}, bf16[8,104,128]{2,1,0:T(8,128)(2,1...) custom-call(s32[1]{0:T(128)} %bitcast.me_ref, ...), custom_call_target="tpu_custom_call" | custom-call | bytes 72600000 | tf_op jit(solution)/shard_map/mlp_b/pallas_call | solution.py:334
  97.8 2.7 %add_convert_fusion = bf16[5248,128]{1,0:T(8,128)(2,1)} fusion(bf16[5248,128]{1,0:T(8,128)(2,1)S(1)} %collective-permute-done.14, bf16[5248,128]{1,0:T(8,128)(2,1)} %get-tuple-element.117), kind=kLoop, calls=%fused_computation.1 | loop fusion | flops 2686976 | bytes 4030464 | tf_op jit(solution)/shard_map/convert_element_type | solution.py:672
  102.2 4.7 %collective-permute-done.17.refs_7_ = bf16[8,104,128]{2,1,0:T(8,128)(2,1)S(1)} collective-permute-done((bf16[8,104,128]{2,1,0:T(8,128)(2,1)}, bf16[8,104,128]{2,1,0:T(8,128)(2,1)S(1)}, u32[]{:S(2)}, u32[]{:S(2)}) %collective-permute-start.17) | collective-permute-done | bytes 213024 | tf_op jit(solution)/shard_map/ppermute | solution.py:44
  107.5 4.3 %all-to-all-start = ((bf16[16,328,128]{2,1,0:T(8,128)(2,1)}), bf16[16,328,128]{2,1,0:T(8,128)(2,1)S(1)}, u32[]{:S(2)}, u32[]{:S(2)}) async-start(bf16[16,328,128]{2,1,0:T(8,128)(2,1)} %bitcast.28), calls=%async_computation | async-start | bytes 2686976 | tf_op jit(solution)/shard_map/all_to_all | solution.py:523
  115.4 2.2 %piece_edges.1 = (bf16[8,8,832]{2,1,0:T(8,128)(2,1)}, bf16[8,8,832]{2,1,0:T(8,128)(2,1)}) custom-call(bf16[16,128]{1,0:T(8,128)(2,1)S(1)} %pad_maximum_fusion.1.pick, bf16[2,8,104,128]{3,2,1,0:T(8,128)(2,1)S(1)} %copy-done.4, bf16[2,8,104,128]{3,2,1,0:T(8,128)(2,1)S(1)} %collective-permute-done.11.refs_1_, bf16[2,8,104,128]{3,2,1,0:T(8,128)(2,1)S(1)} %copy-done.7, ...), custom_call_target="tpu_custom_call" | custom-call | bytes 6600000 | tf_op jit(solution)/shard_map/piece_edges/pallas_call | solution.py:481
  117.6 5.8 %collective-permute-start.18 = (bf16[8,8,832]{2,1,0:T(8,128)(2,1)}, bf16[8,8,832]{2,1,0:T(8,128)(2,1)S(1)}, u32[]{:S(2)}, u32[]{:S(2)}) collective-permute-start(bf16[8,8,832]{2,1,0:T(8,128)(2,1)} %get-tuple-element.136), channel_id=1, source_target_pairs={{0,124},{4,0},{8,4},{12,8},{16,12},{20,16},{24,20},{28,24},{32,28}... | collective-permute-start | bytes 319496 | tf_op jit(solution)/shard_map/ppermute | solution.py:48
  123.5 7.4 %collective-permute-done.18.first = bf16[8,8,832]{2,1,0:T(8,128)(2,1)S(1)} collective-permute-done((bf16[8,8,832]{2,1,0:T(8,128)(2,1)}, bf16[8,8,832]{2,1,0:T(8,128)(2,1)S(1)}, u32[]{:S(2)}, u32[]{:S(2)}) %collective-permute-start.18) | collective-permute-done | bytes 106528 | tf_op jit(solution)/shard_map/ppermute | solution.py:48
  130.8 2.9 %collective-permute-done.19.last = bf16[8,8,832]{2,1,0:T(8,128)(2,1)S(1)} collective-permute-done((bf16[8,8,832]{2,1,0:T(8,128)(2,1)}, bf16[8,8,832]{2,1,0:T(8,128)(2,1)S(1)}, u32[]{:S(2)}, u32[]{:S(2)}) %collective-permute-start.19) | collective-permute-done | bytes 106528 | tf_op jit(solution)/shard_map/ppermute | solution.py:48
  133.9 2.1 %collective-permute-start.23 = (bf16[328,128]{1,0:T(8,128)(2,1)S(1)}, bf16[328,128]{1,0:T(8,128)(2,1)S(1)}, u32[]{:S(2)}, u32[]{:S(2)}) collective-permute-start(bf16[328,128]{1,0:T(8,128)(2,1)S(1)} %plane_total.1), channel_id=1, source_target_pairs={{0,64},{4,68},{8,72},{12,76},{16,80},{20,84},{24,88},{28,92},{32,9... | collective-permute-start | bytes 251912 | tf_op jit(solution)/shard_map/ppermute | solution.py:52
  136.1 1.9 %collective-permute-start.25 = (bf16[328,128]{1,0:T(8,128)(2,1)S(1)}, bf16[328,128]{1,0:T(8,128)(2,1)S(1)}, u32[]{:S(2)}, u32[]{:S(2)}) collective-permute-start(bf16[328,128]{1,0:T(8,128)(2,1)S(1)} %plane_total.1), channel_id=1, source_target_pairs={{0,66},{1,67},{2,64},{3,65},{4,70},{5,71},{6,68},{7,69},{8,74},{9,... | collective-permute-start | bytes 251912 | tf_op jit(solution)/shard_map/ppermute | solution.py:612
  141.9 5.6 %all-to-all-start.1 = ((bf16[16,328,128]{2,1,0:T(8,128)(2,1)}), bf16[16,328,128]{2,1,0:T(8,128)(2,1)}, u32[]{:S(2)}, u32[]{:S(2)}) async-start(bf16[16,328,128]{2,1,0:T(8,128)(2,1)} %plane_copies.1), calls=%async_computation.1 | async-start | bytes 2686976 | tf_op jit(solution)/shard_map/all_to_all | solution.py:523
  148.6 5.1 %update.1 = bf16[100,64,128]{2,1,0:T(8,128)(2,1)} custom-call(s32[1]{0:T(128)} %bitcast.me_ref, bf16[2,8,104,128]{3,2,1,0:T(8,128)(2,1)} %get-tuple-element.128.refs_16_.refs_0_, bf16[2,8,104,128]{3,2,1,0:T(8,128)(2,1)} %copy-done.5, bf16[2,8,104,128]{3,2,1,0:T(8,128)(2,1)} %copy-done.6, bf16[2,8,104,128]{3,2,1,0:T(8,128)(2,1)} %collective-permute-done.13.refs_3_, ...), custom_call_target="tpu_custom_call" | custom-call | bytes 14520000 | tf_op jit(solution)/shard_map/update/pallas_call | solution.py:378
  155.5 13.2 %conv_backward.1 = bf16[100,64,128]{2,1,0:T(8,128)(2,1)} custom-call(s32[1]{0:T(128)} %bitcast.me_ref, bf16[2,8,104,128]{3,2,1,0:T(8,128)(2,1)} %get-tuple-element.128.refs_16_.refs_0_, bf16[2,8,104,128]{3,2,1,0:T(8,128)(2,1)} %copy-done.5, bf16[2,8,104,128]{3,2,1,0:T(8,128)(2,1)} %copy-done.6, bf16[2,8,104,128]{3,2,1,0:T(8,128)(2,1)} %collective-permute-done.13.refs_3_, ...), custom_call_target="tpu_custom_call" | custom-call | bytes 33000000 | tf_op jit(solution)/shard_map/conv_backward/pallas_call | solution.py:171
  168.7 3.0 %collective-permute-start.26 = (bf16[5248,128]{1,0:T(8,128)(2,1)}, bf16[5248,128]{1,0:T(8,128)(2,1)S(1)}, u32[]{:S(2)}, u32[]{:S(2)}) collective-permute-start(bf16[5248,128]{1,0:T(8,128)(2,1)} %bitcast.9.own), channel_id=1, source_target_pairs={{0,1},{1,0},{2,3},{3,2},{4,5},{5,4},{6,7},{7,6},{8,9},{9,8},{10,11... | collective-permute-start | bytes 4030472 | tf_op jit(solution)/shard_map/ppermute | solution.py:44
  171.8 2.8 %collective-permute-done.26.other = bf16[5248,128]{1,0:T(8,128)(2,1)S(1)} collective-permute-done((bf16[5248,128]{1,0:T(8,128)(2,1)}, bf16[5248,128]{1,0:T(8,128)(2,1)S(1)}, u32[]{:S(2)}, u32[]{:S(2)}) %collective-permute-start.26) | collective-permute-done | bytes 1343520 | tf_op jit(solution)/shard_map/ppermute | solution.py:44
  174.6 5.9 %finish.1 = (f32[400,1600]{1,0:T(8,128)}, f32[400,1600]{1,0:T(8,128)}) custom-call(s32[1]{0:T(128)} %bitcast.1.core_ref, bf16[5248,128]{1,0:T(8,128)(2,1)} %bitcast.9.own, bf16[5248,128]{1,0:T(8,128)(2,1)S(1)} %collective-permute-done.26.other, bf16[400,416]{1,0:T(8,128)(2,1)S(1)} %fusion.1.pad), custom_call_target="tpu_custom_call" | custom-call | bytes 19800000 | tf_op jit(solution)/shard_map/finish/pallas_call | solution.py:590
  (143 shorter events, 41.6 us)
Async XLA Ops:
  2.8 24.8 %collective-permute-start = (bf16[8,6400]{1,0:T(8,128)(2,1)S(1)}, bf16[8,6400]{1,0:T(8,128)(2,1)}, u32[]{:S(2)}, u32[]{:S(2)}) collective-permute-start(bf16[8,6400]{1,0:T(8,128)(2,1)S(1)} %edge.2.refs_0_), channel_id=1, source_target_pairs={{0,124},{4,0},{8,4},{12,8},{16,12},{20,16},{24,20},{28,24},{32,28}... | collective-permute-start | bytes 307208 | tf_op jit(solution)/shard_map/ppermute | solution.py:48
  15.1 31.9 %collective-permute-start.6 = (bf16[16,104,128]{2,1,0:T(8,128)(2,1)}, bf16[16,104,128]{2,1,0:T(8,128)(2,1)}, u32[]{:S(2)}, u32[]{:S(2)}) collective-permute-start(bf16[16,104,128]{2,1,0:T(8,128)(2,1)} %branch_share.4.refs_0_), channel_id=1, source_target_pairs={{0,2},{1,3},{2,0},{3,1},{4,6},{5,7},{6,4},{7,5},{8,10},{9,11},{10,... | collective-permute-start | bytes 1277960 | tf_op jit(solution)/shard_map/ppermute | solution.py:44
  16.6 11.0 %collective-permute-start.1 = (bf16[8,6400]{1,0:T(8,128)(2,1)}, bf16[8,6400]{1,0:T(8,128)(2,1)}, u32[]{:S(2)}, u32[]{:S(2)}) collective-permute-start(bf16[8,6400]{1,0:T(8,128)(2,1)} %edge.3.refs_0_), channel_id=1, source_target_pairs={{0,4},{4,8},{8,12},{12,16},{16,20},{20,24},{24,28},{28,32},{32,36}... | collective-permute-start | bytes 307208 | tf_op jit(solution)/shard_map/ppermute | solution.py:48
  17.8 29.2 %collective-permute-start.7 = (bf16[16,104,128]{2,1,0:T(8,128)(2,1)}, bf16[16,104,128]{2,1,0:T(8,128)(2,1)}, u32[]{:S(2)}, u32[]{:S(2)}) collective-permute-start(bf16[16,104,128]{2,1,0:T(8,128)(2,1)} %branch_share.5.refs_0_), channel_id=1, source_target_pairs={{0,3},{1,2},{2,1},{3,0},{4,7},{5,6},{6,5},{7,4},{8,11},{9,10},{10,... | collective-permute-start | bytes 1277960 | tf_op jit(solution)/shard_map/ppermute | solution.py:44
  21.4 24.3 %collective-permute-start.5 = (bf16[16,104,128]{2,1,0:T(8,128)(2,1)}, bf16[16,104,128]{2,1,0:T(8,128)(2,1)}, u32[]{:S(2)}, u32[]{:S(2)}) collective-permute-start(bf16[16,104,128]{2,1,0:T(8,128)(2,1)} %branch_share.6.refs_0_), channel_id=1, source_target_pairs={{0,1},{1,0},{2,3},{3,2},{4,5},{5,4},{6,7},{7,6},{8,9},{9,8},{10,11... | collective-permute-start | bytes 1277960 | tf_op jit(solution)/shard_map/ppermute | solution.py:44
  38.4 9.5 %collective-permute-start.2 = (bf16[8,104,128]{2,1,0:T(8,128)(2,1)}, bf16[8,104,128]{2,1,0:T(8,128)(2,1)S(1)}, u32[]{:S(2)}, u32[]{:S(2)}) collective-permute-start(bf16[8,104,128]{2,1,0:T(8,128)(2,1)} %get-tuple-element.78), channel_id=1, source_target_pairs={{0,1},{1,0},{2,3},{3,2},{4,5},{5,4},{6,7},{7,6},{8,9},{9,8},{10,11... | collective-permute-start | bytes 638984 | tf_op jit(solution)/shard_map/ppermute | solution.py:44
  40.6 10.4 %collective-permute-start.3 = (bf16[8,104,128]{2,1,0:T(8,128)(2,1)}, bf16[8,104,128]{2,1,0:T(8,128)(2,1)}, u32[]{:S(2)}, u32[]{:S(2)}) collective-permute-start(bf16[8,104,128]{2,1,0:T(8,128)(2,1)} %get-tuple-element.79), channel_id=1, source_target_pairs={{0,2},{1,3},{2,0},{3,1},{4,6},{5,7},{6,4},{7,5},{8,10},{9,11},{10,... | collective-permute-start | bytes 638984 | tf_op jit(solution)/shard_map/ppermute | solution.py:44
  45.7 7.8 %collective-permute-start.4 = (bf16[8,104,128]{2,1,0:T(8,128)(2,1)S(1)}, bf16[8,104,128]{2,1,0:T(8,128)(2,1)}, u32[]{:S(2)}, u32[]{:S(2)}) collective-permute-start(bf16[8,104,128]{2,1,0:T(8,128)(2,1)S(1)} %copy-done.30), channel_id=1, source_target_pairs={{0,3},{1,2},{2,1},{3,0},{4,7},{5,6},{6,5},{7,4},{8,11},{9,10},{10,... | collective-permute-start | bytes 638984 | tf_op jit(solution)/shard_map/ppermute | solution.py:44
  47.0 21.6 %collective-permute-start.10 = (bf16[8,104,128]{2,1,0:T(8,128)(2,1)}, bf16[8,104,128]{2,1,0:T(8,128)(2,1)S(1)}, u32[]{:S(2)}, u32[]{:S(2)}) collective-permute-start(bf16[8,104,128]{2,1,0:T(8,128)(2,1)} %get-tuple-element.104), channel_id=1, source_target_pairs={{0,3},{1,2},{2,1},{3,0},{4,7},{5,6},{6,5},{7,4},{8,11},{9,10},{10,... | collective-permute-start | bytes 638984 | tf_op jit(solution)/shard_map/ppermute | solution.py:44
  47.5 21.1 %collective-permute-start.8 = (bf16[8,104,128]{2,1,0:T(8,128)(2,1)}, bf16[8,104,128]{2,1,0:T(8,128)(2,1)S(1)}, u32[]{:S(2)}, u32[]{:S(2)}) collective-permute-start(bf16[8,104,128]{2,1,0:T(8,128)(2,1)} %get-tuple-element.102), channel_id=1, source_target_pairs={{0,1},{1,0},{2,3},{3,2},{4,5},{5,4},{6,7},{7,6},{8,9},{9,8},{10,11... | collective-permute-start | bytes 638984 | tf_op jit(solution)/shard_map/ppermute | solution.py:44
  47.8 20.8 %collective-permute-start.9 = (bf16[8,104,128]{2,1,0:T(8,128)(2,1)}, bf16[8,104,128]{2,1,0:T(8,128)(2,1)S(1)}, u32[]{:S(2)}, u32[]{:S(2)}) collective-permute-start(bf16[8,104,128]{2,1,0:T(8,128)(2,1)} %get-tuple-element.103), channel_id=1, source_target_pairs={{0,2},{1,3},{2,0},{3,1},{4,6},{5,7},{6,4},{7,5},{8,10},{9,11},{10,... | collective-permute-start | bytes 638984 | tf_op jit(solution)/shard_map/ppermute | solution.py:44
  69.4 24.2 %collective-permute-start.11 = (bf16[2,8,104,128]{3,2,1,0:T(8,128)(2,1)}, bf16[2,8,104,128]{3,2,1,0:T(8,128)(2,1)S(1)}, u32[]{:S(2)}, u32[]{:S(2)}) collective-permute-start(bf16[2,8,104,128]{3,2,1,0:T(8,128)(2,1)} %get-tuple-element.114), channel_id=1, source_target_pairs={{0,1},{1,0},{2,3},{3,2},{4,5},{5,4},{6,7},{7,6},{8,9},{9,8},{10,11... | collective-permute-start | bytes 1277960 | tf_op jit(solution)/shard_map/ppermute | solution.py:44
  69.4 24.2 %collective-permute-start.12 = (bf16[2,8,104,128]{3,2,1,0:T(8,128)(2,1)}, bf16[2,8,104,128]{3,2,1,0:T(8,128)(2,1)S(1)}, u32[]{:S(2)}, u32[]{:S(2)}) collective-permute-start(bf16[2,8,104,128]{3,2,1,0:T(8,128)(2,1)} %get-tuple-element.115), channel_id=1, source_target_pairs={{0,2},{1,3},{2,0},{3,1},{4,6},{5,7},{6,4},{7,5},{8,10},{9,11},{10,... | collective-permute-start | bytes 1277960 | tf_op jit(solution)/shard_map/ppermute | solution.py:44
  70.6 24.0 %collective-permute-start.13 = (bf16[2,8,104,128]{3,2,1,0:T(8,128)(2,1)}, bf16[2,8,104,128]{3,2,1,0:T(8,128)(2,1)}, u32[]{:S(2)}, u32[]{:S(2)}) collective-permute-start(bf16[2,8,104,128]{3,2,1,0:T(8,128)(2,1)} %get-tuple-element.116), channel_id=1, source_target_pairs={{0,3},{1,2},{2,1},{3,0},{4,7},{5,6},{6,5},{7,4},{8,11},{9,10},{10,... | collective-permute-start | bytes 1277960 | tf_op jit(solution)/shard_map/ppermute | solution.py:44
  94.6 6.0 %collective-permute-start.15 = (bf16[8,104,128]{2,1,0:T(8,128)(2,1)}, bf16[8,104,128]{2,1,0:T(8,128)(2,1)S(1)}, u32[]{:S(2)}, u32[]{:S(2)}) collective-permute-start(bf16[8,104,128]{2,1,0:T(8,128)(2,1)} %get-tuple-element.120), channel_id=1, source_target_pairs={{0,1},{1,0},{2,3},{3,2},{4,5},{5,4},{6,7},{7,6},{8,9},{9,8},{10,11... | collective-permute-start | bytes 638984 | tf_op jit(solution)/shard_map/ppermute | solution.py:44
  95.1 7.1 %collective-permute-start.16 = (bf16[8,104,128]{2,1,0:T(8,128)(2,1)}, bf16[8,104,128]{2,1,0:T(8,128)(2,1)S(1)}, u32[]{:S(2)}, u32[]{:S(2)}) collective-permute-start(bf16[8,104,128]{2,1,0:T(8,128)(2,1)} %get-tuple-element.121), channel_id=1, source_target_pairs={{0,2},{1,3},{2,0},{3,1},{4,6},{5,7},{6,4},{7,5},{8,10},{9,11},{10,... | collective-permute-start | bytes 638984 | tf_op jit(solution)/shard_map/ppermute | solution.py:44
  96.1 10.7 %collective-permute-start.17 = (bf16[8,104,128]{2,1,0:T(8,128)(2,1)}, bf16[8,104,128]{2,1,0:T(8,128)(2,1)S(1)}, u32[]{:S(2)}, u32[]{:S(2)}) collective-permute-start(bf16[8,104,128]{2,1,0:T(8,128)(2,1)} %get-tuple-element.122), channel_id=1, source_target_pairs={{0,3},{1,2},{2,1},{3,0},{4,7},{5,6},{6,5},{7,4},{8,11},{9,10},{10,... | collective-permute-start | bytes 638984 | tf_op jit(solution)/shard_map/ppermute | solution.py:44
  107.5 26.2 %all-to-all-start = ((bf16[16,328,128]{2,1,0:T(8,128)(2,1)}), bf16[16,328,128]{2,1,0:T(8,128)(2,1)S(1)}, u32[]{:S(2)}, u32[]{:S(2)}) async-start(bf16[16,328,128]{2,1,0:T(8,128)(2,1)} %bitcast.28), calls=%async_computation | async-start | bytes 2686976 | tf_op jit(solution)/shard_map/all_to_all | solution.py:523
  111.8 21.8 %collective-permute-start.20 = (bf16[8,104,128]{2,1,0:T(8,128)(2,1)}, bf16[8,104,128]{2,1,0:T(8,128)(2,1)}, u32[]{:S(2)}, u32[]{:S(2)}) collective-permute-start(bf16[8,104,128]{2,1,0:T(8,128)(2,1)} %get-tuple-element.139), channel_id=1, source_target_pairs={{0,1},{1,0},{2,3},{3,2},{4,5},{5,4},{6,7},{7,6},{8,9},{9,8},{10,11... | collective-permute-start | bytes 638984 | tf_op jit(solution)/shard_map/ppermute | solution.py:44
  112.7 21.0 %collective-permute-start.21 = (bf16[8,104,128]{2,1,0:T(8,128)(2,1)}, bf16[8,104,128]{2,1,0:T(8,128)(2,1)}, u32[]{:S(2)}, u32[]{:S(2)}) collective-permute-start(bf16[8,104,128]{2,1,0:T(8,128)(2,1)} %get-tuple-element.140), channel_id=1, source_target_pairs={{0,2},{1,3},{2,0},{3,1},{4,6},{5,7},{6,4},{7,5},{8,10},{9,11},{10,... | collective-permute-start | bytes 638984 | tf_op jit(solution)/shard_map/ppermute | solution.py:44
  112.9 20.8 %collective-permute-start.22 = (bf16[8,104,128]{2,1,0:T(8,128)(2,1)}, bf16[8,104,128]{2,1,0:T(8,128)(2,1)}, u32[]{:S(2)}, u32[]{:S(2)}) collective-permute-start(bf16[8,104,128]{2,1,0:T(8,128)(2,1)} %get-tuple-element.141), channel_id=1, source_target_pairs={{0,3},{1,2},{2,1},{3,0},{4,7},{5,6},{6,5},{7,4},{8,11},{9,10},{10,... | collective-permute-start | bytes 638984 | tf_op jit(solution)/shard_map/ppermute | solution.py:44
  117.6 13.2 %collective-permute-start.18 = (bf16[8,8,832]{2,1,0:T(8,128)(2,1)}, bf16[8,8,832]{2,1,0:T(8,128)(2,1)S(1)}, u32[]{:S(2)}, u32[]{:S(2)}) collective-permute-start(bf16[8,8,832]{2,1,0:T(8,128)(2,1)} %get-tuple-element.136), channel_id=1, source_target_pairs={{0,124},{4,0},{8,4},{12,8},{16,12},{20,16},{24,20},{28,24},{32,28}... | collective-permute-start | bytes 319496 | tf_op jit(solution)/shard_map/ppermute | solution.py:48
  123.5 10.2 %collective-permute-start.19 = (bf16[8,8,832]{2,1,0:T(8,128)(2,1)}, bf16[8,8,832]{2,1,0:T(8,128)(2,1)S(1)}, u32[]{:S(2)}, u32[]{:S(2)}) collective-permute-start(bf16[8,8,832]{2,1,0:T(8,128)(2,1)} %get-tuple-element.137), channel_id=1, source_target_pairs={{0,4},{4,8},{8,12},{12,16},{16,20},{20,24},{24,28},{28,32},{32,36}... | collective-permute-start | bytes 319496 | tf_op jit(solution)/shard_map/ppermute | solution.py:48
  141.9 26.8 %all-to-all-start.1 = ((bf16[16,328,128]{2,1,0:T(8,128)(2,1)}), bf16[16,328,128]{2,1,0:T(8,128)(2,1)}, u32[]{:S(2)}, u32[]{:S(2)}) async-start(bf16[16,328,128]{2,1,0:T(8,128)(2,1)} %plane_copies.1), calls=%async_computation.1 | async-start | bytes 2686976 | tf_op jit(solution)/shard_map/all_to_all | solution.py:523
  (36 other events, 238.0 us)

commit v5 on v4

--- a/solution.py
+++ b/solution.py
@@ -143,7 +143,7 @@
             out_specs=[pl.BlockSpec((HR, GROUP, LANES), lambda i, me: (0, i, 0))] * 8,
             scratch_shapes=[pltpu.VMEM((4, QR, GROUP, LANES), F32)],
         ),
-        compiler_params=pltpu.CompilerParams(vmem_limit_bytes=32 << 20),
+        compiler_params=pltpu.CompilerParams(vmem_limit_bytes=VMEM),
         cost_estimate=cost(9),
         name="conv_forward",
     )(me, state, rim, pattern, bias)

time: 181 us -> 192 us (1.061)
  waiting for transfers between devices: 27.4 us -> 32.7 us
  local copies, waits for them, and re-layouts: 13.5 us -> 18.7 us
  starting transfers between devices: 47.9 us -> 44.5 us
  Pallas kernels: 84 us -> 86.1 us
    unnamed x64 -> x72, local copies, waits for them, and re-layouts: 8.55 us -> 12.8 us
    pallas_call x1, Pallas kernels: 8.96 us -> 11.9 us  [conv_forward(): pl.pallas_call(forward_kernel, out_shape=[share] * 8, grid_spec=pltpu.Pre...]
  transfers between devices with their start and end apart: 29 -> 29, of which waited for: 11 -> 11; matrix products, arithmetic and copies ran while one was open for 6% -> 7% of each run, Pallas kernels for 42% -> 41%
where the time goes in v5:
time: 192 us; the launch traced here: 190 us
  Pallas kernels  86.1 us (45%)
  starting transfers between devices  44.5 us (23%)
  waiting for transfers between devices  32.7 us (17%)
  local copies, waits for them, and re-layouts  18.7 us (10%)
  other arithmetic  4.04 us (2%)
  matrix products  3.13 us (2%)
    pallas_call x2, Pallas kernels, mlp(): pl.pallas_call(functools.partial(mlp_kernel, half), out_shape=[jax.ShapeD...  37.1 us
    ppermute x21, starting transfers between devices, ch_swap(): return lax.ppermute(x, 'ch', [(i, i ^ k) for i in range(4)])  18.9 us
    ppermute x4, starting transfers between devices, lon_shift(): return lax.ppermute(x, 'lon', [(i, (i + d) % 32) for i in range(32)])  14.4 us
    ppermute x4, waiting for transfers between devices, lon_shift(): return lax.ppermute(x, 'lon', [(i, (i + d) % 32) for i in range(32)])  13.8 us
    pallas_call x1, Pallas kernels, conv_backward(): pl.pallas_call(backward_kernel, out_shape=jax.ShapeDtypeStruct((LC, ROWS,...  13.2 us
    ppermute x21, waiting for transfers between devices, ch_swap(): return lax.ppermute(x, 'ch', [(i, i ^ k) for i in range(4)])  12.9 us
    unnamed x72, local copies, waits for them, and re-layouts  12.8 us
    pallas_call x1, Pallas kernels, conv_forward(): pl.pallas_call(forward_kernel, out_shape=[share] * 8, grid_spec=pltpu.Pre...  11.9 us
  transfers between devices with their start and end apart: 29, of which 11 were waited for; matrix products, arithmetic and copies ran while one was open for 7% of the time, Pallas kernels for 41%

profile of v5, /device:TPU:1, one launch (start us, length us, event | category | flops | bytes accessed | tf_op | source)
XLA Modules:
  0.0 190.3 jit_solution(11491629980132266852)
XLA Ops:
  3.5 9.5 %collective-permute-start = (bf16[8,6400]{1,0:T(8,128)(2,1)}, bf16[8,6400]{1,0:T(8,128)(2,1)}, u32[]{:S(2)}, u32[]{:S(2)}) collective-permute-start(bf16[8,6400]{1,0:T(8,128)(2,1)} %edge.2.refs_0_), channel_id=1, source_target_pairs={{0,124},{4,0},{8,4},{12,8},{16,12},{20,16},{24,20},{28,24},{32,28}... | collective-permute-start | bytes 307208 | tf_op jit(solution)/shard_map/ppermute | solution.py:48
  17.7 2.4 %collective-permute-start.7 = (bf16[16,104,128]{2,1,0:T(8,128)(2,1)S(1)}, bf16[16,104,128]{2,1,0:T(8,128)(2,1)}, u32[]{:S(2)}, u32[]{:S(2)}) collective-permute-start(bf16[16,104,128]{2,1,0:T(8,128)(2,1)S(1)} %branch_share.5.refs_0_), channel_id=1, source_target_pairs={{0,3},{1,2},{2,1},{3,0},{4,7},{5,6},{6,5},{7,4},{8,11},{9,10},{10,... | collective-permute-start | bytes 1277960 | tf_op jit(solution)/shard_map/ppermute | solution.py:44
  24.5 3.6 %collective-permute-done.1 = bf16[8,6400]{1,0:T(8,128)(2,1)S(1)} collective-permute-done((bf16[8,6400]{1,0:T(8,128)(2,1)}, bf16[8,6400]{1,0:T(8,128)(2,1)S(1)}, u32[]{:S(2)}, u32[]{:S(2)}) %collective-permute-start.1) | collective-permute-done | bytes 102432 | tf_op jit(solution)/shard_map/ppermute | solution.py:48
  28.1 2.7 %convolution_convert_fusion = bf16[6400,128]{1,0:T(8,128)(2,1)} fusion(bf16[8,6400]{1,0:T(8,128)(2,1)S(1)} %collective-permute-done.1, bf16[8,6400]{1,0:T(8,128)(2,1)} %collective-permute-done, bf16[8,128]{1,0:T(8,128)(2,1)S(1)} %get-tuple-element.155.pick, bf16[8,128]{1,0:T(8,128)(2,1)S(1)} %get-tuple-element.154.pick), kind=kOutput, calls=%fused_computation | convolution fusion | flops 27451392 | bytes 1847296 | tf_op jit(solution)/shard_map/dot_general | solution.py:32
  31.6 11.9 %conv_forward.1 = (bf16[8,104,128]{2,1,0:T(8,128)(2,1)}, bf16[8,104,128]{2,1,0:T(8,128)(2,1)}, bf16[8,104,128]{2,1,0:T(8,128)(2,1)}, bf16[8,104,128]{2,1,0:T(8,1...) custom-call(s32[1]{0:T(128)} %bitcast.me_ref, ...), custom_call_target="tpu_custom_call" | custom-call | bytes 29700000 | tf_op jit(solution)/shard_map/conv_forward/pallas_call | solution.py:131
  43.5 2.6 %collective-permute-start.2 = (bf16[8,104,128]{2,1,0:T(8,128)(2,1)}, bf16[8,104,128]{2,1,0:T(8,128)(2,1)}, u32[]{:S(2)}, u32[]{:S(2)}) collective-permute-start(bf16[8,104,128]{2,1,0:T(8,128)(2,1)} %get-tuple-element.78), channel_id=1, source_target_pairs={{0,1},{1,0},{2,3},{3,2},{4,5},{5,4},{6,7},{7,6},{8,9},{9,8},{10,11... | collective-permute-start | bytes 638984 | tf_op jit(solution)/shard_map/ppermute | solution.py:44
  51.6 3.7 %padded_weights.1 = (bf16[416,1600]{1,0:T(8,128)(2,1)}, bf16[1600,416]{1,0:T(8,128)(2,1)}, bf16[416,1600]{1,0:T(8,128)(2,1)}, bf16[1600,416]{1,0:T(8,128)(2,1)}) custom-call(bf16[400,1600]{1,0:T(8,128)(2,1)S(1)} %copy-done.11, bf16[400,1600]{1,0:T(8,128)(2,1)S(1)} %bitcast.26, bf16[400,416]{1,0:T(8,128)(2,1)S(1)} %copy-done.10, ...), custom_call_target="tpu_custom_call" | custom-call | bytes 16500000 | tf_op jit(solution)/shard_map/padded_weights/pallas_call | solution.py:418
  60.3 2.8 %collective-permute-done.4.refs_3_ = bf16[8,104,128]{2,1,0:T(8,128)(2,1)S(1)} collective-permute-done((bf16[8,104,128]{2,1,0:T(8,128)(2,1)S(1)}, bf16[8,104,128]{2,1,0:T(8,128)(2,1)S(1)}, u32[]{:S(2)}, u32[]{:S(2)}) %collective-permute-start.4) | collective-permute-done | bytes 213024 | tf_op jit(solution)/shard_map/ppermute | solution.py:44
  63.8 15.0 %mlp_a.1 = (bf16[2,8,104,128]{3,2,1,0:T(8,128)(2,1)}, bf16[2,8,104,128]{3,2,1,0:T(8,128)(2,1)}, bf16[2,8,104,128]{3,2,1,0:T(8,128)(2,1)}, bf16[2,8,104,128]{3,2,...) custom-call(s32[1]{0:T(128)} %bitcast.me_ref, s32[1]{0:T(128)} %bitcast.1.core_ref, ...), custom_call_target="tpu_custom_call" | custom-call | bytes 46200000 | tf_op jit(solution)/shard_map/mlp_a/pallas_call | solution.py:334
  81.8 22.1 %mlp_b.1 = (bf16[8,104,128]{2,1,0:T(8,128)(2,1)}, bf16[8,104,128]{2,1,0:T(8,128)(2,1)}, bf16[8,104,128]{2,1,0:T(8,128)(2,1)}, bf16[8,104,128]{2,1,0:T(8,128)(2,1...) custom-call(s32[1]{0:T(128)} %bitcast.me_ref, ...), custom_call_target="tpu_custom_call" | custom-call | bytes 72600000 | tf_op jit(solution)/shard_map/mlp_b/pallas_call | solution.py:334
  108.1 2.7 %add_convert_fusion = bf16[5248,128]{1,0:T(8,128)(2,1)} fusion(bf16[5248,128]{1,0:T(8,128)(2,1)S(1)} %collective-permute-done.14, bf16[5248,128]{1,0:T(8,128)(2,1)} %get-tuple-element.117), kind=kLoop, calls=%fused_computation.1 | loop fusion | flops 2686976 | bytes 4030464 | tf_op jit(solution)/shard_map/convert_element_type | solution.py:672
  112.4 4.7 %collective-permute-done.17.refs_7_ = bf16[8,104,128]{2,1,0:T(8,128)(2,1)S(1)} collective-permute-done((bf16[8,104,128]{2,1,0:T(8,128)(2,1)}, bf16[8,104,128]{2,1,0:T(8,128)(2,1)S(1)}, u32[]{:S(2)}, u32[]{:S(2)}) %collective-permute-start.17) | collective-permute-done | bytes 213024 | tf_op jit(solution)/shard_map/ppermute | solution.py:44
  117.7 3.7 %all-to-all-start = ((bf16[16,328,128]{2,1,0:T(8,128)(2,1)}), bf16[16,328,128]{2,1,0:T(8,128)(2,1)S(1)}, u32[]{:S(2)}, u32[]{:S(2)}) async-start(bf16[16,328,128]{2,1,0:T(8,128)(2,1)} %bitcast.28), calls=%async_computation | async-start | bytes 2686976 | tf_op jit(solution)/shard_map/all_to_all | solution.py:523
  124.8 2.2 %piece_edges.1 = (bf16[8,8,832]{2,1,0:T(8,128)(2,1)}, bf16[8,8,832]{2,1,0:T(8,128)(2,1)}) custom-call(bf16[16,128]{1,0:T(8,128)(2,1)S(1)} %pad_maximum_fusion.1.pick, bf16[2,8,104,128]{3,2,1,0:T(8,128)(2,1)S(1)} %copy-done.4, bf16[2,8,104,128]{3,2,1,0:T(8,128)(2,1)S(1)} %collective-permute-done.11.refs_1_, bf16[2,8,104,128]{3,2,1,0:T(8,128)(2,1)S(1)} %copy-done.7, ...), custom_call_target="tpu_custom_call" | custom-call | bytes 6600000 | tf_op jit(solution)/shard_map/piece_edges/pallas_call | solution.py:481
  127.0 4.8 %collective-permute-start.18 = (bf16[8,8,832]{2,1,0:T(8,128)(2,1)}, bf16[8,8,832]{2,1,0:T(8,128)(2,1)S(1)}, u32[]{:S(2)}, u32[]{:S(2)}) collective-permute-start(bf16[8,8,832]{2,1,0:T(8,128)(2,1)} %get-tuple-element.136), channel_id=1, source_target_pairs={{0,124},{4,0},{8,4},{12,8},{16,12},{20,16},{24,20},{28,24},{32,28}... | collective-permute-start | bytes 319496 | tf_op jit(solution)/shard_map/ppermute | solution.py:48
  131.9 9.1 %collective-permute-done.18.first = bf16[8,8,832]{2,1,0:T(8,128)(2,1)S(1)} collective-permute-done((bf16[8,8,832]{2,1,0:T(8,128)(2,1)}, bf16[8,8,832]{2,1,0:T(8,128)(2,1)S(1)}, u32[]{:S(2)}, u32[]{:S(2)}) %collective-permute-start.18) | collective-permute-done | bytes 106528 | tf_op jit(solution)/shard_map/ppermute | solution.py:48
  142.1 1.7 all-to-all-done.refs_0_
  149.0 2.7 %collective-permute-done.25 = bf16[328,128]{1,0:T(8,128)(2,1)S(1)} collective-permute-done((bf16[328,128]{1,0:T(8,128)(2,1)S(1)}, bf16[328,128]{1,0:T(8,128)(2,1)S(1)}, u32[]{:S(2)}, u32[]{:S(2)}) %collective-permute-start.25) | collective-permute-done | bytes 84000 | tf_op jit(solution)/shard_map/ppermute | solution.py:612
  152.9 4.9 %all-to-all-start.1 = ((bf16[16,328,128]{2,1,0:T(8,128)(2,1)}), bf16[16,328,128]{2,1,0:T(8,128)(2,1)}, u32[]{:S(2)}, u32[]{:S(2)}) async-start(bf16[16,328,128]{2,1,0:T(8,128)(2,1)} %plane_copies.1), calls=%async_computation.1 | async-start | bytes 2686976 | tf_op jit(solution)/shard_map/all_to_all | solution.py:523
  158.8 5.1 %update.1 = bf16[100,64,128]{2,1,0:T(8,128)(2,1)} custom-call(s32[1]{0:T(128)} %bitcast.me_ref, bf16[2,8,104,128]{3,2,1,0:T(8,128)(2,1)} %get-tuple-element.128.refs_16_.refs_0_, bf16[2,8,104,128]{3,2,1,0:T(8,128)(2,1)} %copy-done.5, bf16[2,8,104,128]{3,2,1,0:T(8,128)(2,1)} %copy-done.6, bf16[2,8,104,128]{3,2,1,0:T(8,128)(2,1)} %collective-permute-done.13.refs_3_, ...), custom_call_target="tpu_custom_call" | custom-call | bytes 14520000 | tf_op jit(solution)/shard_map/update/pallas_call | solution.py:378
  165.8 13.2 %conv_backward.1 = bf16[100,64,128]{2,1,0:T(8,128)(2,1)} custom-call(s32[1]{0:T(128)} %bitcast.me_ref, bf16[2,8,104,128]{3,2,1,0:T(8,128)(2,1)} %get-tuple-element.128.refs_16_.refs_0_, bf16[2,8,104,128]{3,2,1,0:T(8,128)(2,1)} %copy-done.5, bf16[2,8,104,128]{3,2,1,0:T(8,128)(2,1)} %copy-done.6, bf16[2,8,104,128]{3,2,1,0:T(8,128)(2,1)} %collective-permute-done.13.refs_3_, ...), custom_call_target="tpu_custom_call" | custom-call | bytes 33000000 | tf_op jit(solution)/shard_map/conv_backward/pallas_call | solution.py:171
  179.0 2.5 %collective-permute-start.26 = (bf16[5248,128]{1,0:T(8,128)(2,1)}, bf16[5248,128]{1,0:T(8,128)(2,1)S(1)}, u32[]{:S(2)}, u32[]{:S(2)}) collective-permute-start(bf16[5248,128]{1,0:T(8,128)(2,1)} %bitcast.9.own), channel_id=1, source_target_pairs={{0,1},{1,0},{2,3},{3,2},{4,5},{5,4},{6,7},{7,6},{8,9},{9,8},{10,11... | collective-permute-start | bytes 4030472 | tf_op jit(solution)/shard_map/ppermute | solution.py:44
  181.6 2.8 %collective-permute-done.26.other = bf16[5248,128]{1,0:T(8,128)(2,1)S(1)} collective-permute-done((bf16[5248,128]{1,0:T(8,128)(2,1)}, bf16[5248,128]{1,0:T(8,128)(2,1)S(1)}, u32[]{:S(2)}, u32[]{:S(2)}) %collective-permute-start.26) | collective-permute-done | bytes 1343520 | tf_op jit(solution)/shard_map/ppermute | solution.py:44
  184.4 5.9 %finish.1 = (f32[400,1600]{1,0:T(8,128)}, f32[400,1600]{1,0:T(8,128)}) custom-call(s32[1]{0:T(128)} %bitcast.1.core_ref, bf16[5248,128]{1,0:T(8,128)(2,1)} %bitcast.9.own, bf16[5248,128]{1,0:T(8,128)(2,1)S(1)} %collective-permute-done.26.other, bf16[400,416]{1,0:T(8,128)(2,1)S(1)} %fusion.1.pad), custom_call_target="tpu_custom_call" | custom-call | bytes 19800000 | tf_op jit(solution)/shard_map/finish/pallas_call | solution.py:590
  (151 shorter events, 46.9 us)
Async XLA Ops:
  3.5 24.6 %collective-permute-start = (bf16[8,6400]{1,0:T(8,128)(2,1)}, bf16[8,6400]{1,0:T(8,128)(2,1)}, u32[]{:S(2)}, u32[]{:S(2)}) collective-permute-start(bf16[8,6400]{1,0:T(8,128)(2,1)} %edge.2.refs_0_), channel_id=1, source_target_pairs={{0,124},{4,0},{8,4},{12,8},{16,12},{20,16},{24,20},{28,24},{32,28}... | collective-permute-start | bytes 307208 | tf_op jit(solution)/shard_map/ppermute | solution.py:48
  15.7 40.6 %collective-permute-start.6 = (bf16[16,104,128]{2,1,0:T(8,128)(2,1)}, bf16[16,104,128]{2,1,0:T(8,128)(2,1)}, u32[]{:S(2)}, u32[]{:S(2)}) collective-permute-start(bf16[16,104,128]{2,1,0:T(8,128)(2,1)} %branch_share.4.refs_0_), channel_id=1, source_target_pairs={{0,2},{1,3},{2,0},{3,1},{4,6},{5,7},{6,4},{7,5},{8,10},{9,11},{10,... | collective-permute-start | bytes 1277960 | tf_op jit(solution)/shard_map/ppermute | solution.py:44
  17.2 10.9 %collective-permute-start.1 = (bf16[8,6400]{1,0:T(8,128)(2,1)}, bf16[8,6400]{1,0:T(8,128)(2,1)S(1)}, u32[]{:S(2)}, u32[]{:S(2)}) collective-permute-start(bf16[8,6400]{1,0:T(8,128)(2,1)} %edge.3.refs_0_), channel_id=1, source_target_pairs={{0,4},{4,8},{8,12},{12,16},{16,20},{20,24},{24,28},{28,32},{32,36}... | collective-permute-start | bytes 307208 | tf_op jit(solution)/shard_map/ppermute | solution.py:48
  17.7 38.6 %collective-permute-start.7 = (bf16[16,104,128]{2,1,0:T(8,128)(2,1)S(1)}, bf16[16,104,128]{2,1,0:T(8,128)(2,1)}, u32[]{:S(2)}, u32[]{:S(2)}) collective-permute-start(bf16[16,104,128]{2,1,0:T(8,128)(2,1)S(1)} %branch_share.5.refs_0_), channel_id=1, source_target_pairs={{0,3},{1,2},{2,1},{3,0},{4,7},{5,6},{6,5},{7,4},{8,11},{9,10},{10,... | collective-permute-start | bytes 1277960 | tf_op jit(solution)/shard_map/ppermute | solution.py:44
  20.5 34.8 %collective-permute-start.5 = (bf16[16,104,128]{2,1,0:T(8,128)(2,1)S(1)}, bf16[16,104,128]{2,1,0:T(8,128)(2,1)}, u32[]{:S(2)}, u32[]{:S(2)}) collective-permute-start(bf16[16,104,128]{2,1,0:T(8,128)(2,1)S(1)} %branch_share.6.refs_0_), channel_id=1, source_target_pairs={{0,1},{1,0},{2,3},{3,2},{4,5},{5,4},{6,7},{7,6},{8,9},{9,8},{10,11... | collective-permute-start | bytes 1277960 | tf_op jit(solution)/shard_map/ppermute | solution.py:44
  43.5 13.9 %collective-permute-start.2 = (bf16[8,104,128]{2,1,0:T(8,128)(2,1)}, bf16[8,104,128]{2,1,0:T(8,128)(2,1)}, u32[]{:S(2)}, u32[]{:S(2)}) collective-permute-start(bf16[8,104,128]{2,1,0:T(8,128)(2,1)} %get-tuple-element.78), channel_id=1, source_target_pairs={{0,1},{1,0},{2,3},{3,2},{4,5},{5,4},{6,7},{7,6},{8,9},{9,8},{10,11... | collective-permute-start | bytes 638984 | tf_op jit(solution)/shard_map/ppermute | solution.py:44
  46.2 14.1 %collective-permute-start.3 = (bf16[8,104,128]{2,1,0:T(8,128)(2,1)}, bf16[8,104,128]{2,1,0:T(8,128)(2,1)}, u32[]{:S(2)}, u32[]{:S(2)}) collective-permute-start(bf16[8,104,128]{2,1,0:T(8,128)(2,1)} %get-tuple-element.79), channel_id=1, source_target_pairs={{0,2},{1,3},{2,0},{3,1},{4,6},{5,7},{6,4},{7,5},{8,10},{9,11},{10,... | collective-permute-start | bytes 638984 | tf_op jit(solution)/shard_map/ppermute | solution.py:44
  55.3 7.8 %collective-permute-start.4 = (bf16[8,104,128]{2,1,0:T(8,128)(2,1)S(1)}, bf16[8,104,128]{2,1,0:T(8,128)(2,1)S(1)}, u32[]{:S(2)}, u32[]{:S(2)}) collective-permute-start(bf16[8,104,128]{2,1,0:T(8,128)(2,1)S(1)} %copy-done.34), channel_id=1, source_target_pairs={{0,3},{1,2},{2,1},{3,0},{4,7},{5,6},{6,5},{7,4},{8,11},{9,10},{10,... | collective-permute-start | bytes 638984 | tf_op jit(solution)/shard_map/ppermute | solution.py:44
  56.3 22.5 %collective-permute-start.10 = (bf16[8,104,128]{2,1,0:T(8,128)(2,1)}, bf16[8,104,128]{2,1,0:T(8,128)(2,1)S(1)}, u32[]{:S(2)}, u32[]{:S(2)}) collective-permute-start(bf16[8,104,128]{2,1,0:T(8,128)(2,1)} %get-tuple-element.104), channel_id=1, source_target_pairs={{0,3},{1,2},{2,1},{3,0},{4,7},{5,6},{6,5},{7,4},{8,11},{9,10},{10,... | collective-permute-start | bytes 638984 | tf_op jit(solution)/shard_map/ppermute | solution.py:44
  57.1 21.8 %collective-permute-start.8 = (bf16[8,104,128]{2,1,0:T(8,128)(2,1)}, bf16[8,104,128]{2,1,0:T(8,128)(2,1)S(1)}, u32[]{:S(2)}, u32[]{:S(2)}) collective-permute-start(bf16[8,104,128]{2,1,0:T(8,128)(2,1)} %get-tuple-element.102), channel_id=1, source_target_pairs={{0,1},{1,0},{2,3},{3,2},{4,5},{5,4},{6,7},{7,6},{8,9},{9,8},{10,11... | collective-permute-start | bytes 638984 | tf_op jit(solution)/shard_map/ppermute | solution.py:44
  57.4 21.4 %collective-permute-start.9 = (bf16[8,104,128]{2,1,0:T(8,128)(2,1)}, bf16[8,104,128]{2,1,0:T(8,128)(2,1)S(1)}, u32[]{:S(2)}, u32[]{:S(2)}) collective-permute-start(bf16[8,104,128]{2,1,0:T(8,128)(2,1)} %get-tuple-element.103), channel_id=1, source_target_pairs={{0,2},{1,3},{2,0},{3,1},{4,6},{5,7},{6,4},{7,5},{8,10},{9,11},{10,... | collective-permute-start | bytes 638984 | tf_op jit(solution)/shard_map/ppermute | solution.py:44
  79.6 24.2 %collective-permute-start.11 = (bf16[2,8,104,128]{3,2,1,0:T(8,128)(2,1)}, bf16[2,8,104,128]{3,2,1,0:T(8,128)(2,1)S(1)}, u32[]{:S(2)}, u32[]{:S(2)}) collective-permute-start(bf16[2,8,104,128]{3,2,1,0:T(8,128)(2,1)} %get-tuple-element.114), channel_id=1, source_target_pairs={{0,1},{1,0},{2,3},{3,2},{4,5},{5,4},{6,7},{7,6},{8,9},{9,8},{10,11... | collective-permute-start | bytes 1277960 | tf_op jit(solution)/shard_map/ppermute | solution.py:44
  79.7 24.3 %collective-permute-start.12 = (bf16[2,8,104,128]{3,2,1,0:T(8,128)(2,1)}, bf16[2,8,104,128]{3,2,1,0:T(8,128)(2,1)S(1)}, u32[]{:S(2)}, u32[]{:S(2)}) collective-permute-start(bf16[2,8,104,128]{3,2,1,0:T(8,128)(2,1)} %get-tuple-element.115), channel_id=1, source_target_pairs={{0,2},{1,3},{2,0},{3,1},{4,6},{5,7},{6,4},{7,5},{8,10},{9,11},{10,... | collective-permute-start | bytes 1277960 | tf_op jit(solution)/shard_map/ppermute | solution.py:44
  80.5 24.3 %collective-permute-start.13 = (bf16[2,8,104,128]{3,2,1,0:T(8,128)(2,1)}, bf16[2,8,104,128]{3,2,1,0:T(8,128)(2,1)}, u32[]{:S(2)}, u32[]{:S(2)}) collective-permute-start(bf16[2,8,104,128]{3,2,1,0:T(8,128)(2,1)} %get-tuple-element.116), channel_id=1, source_target_pairs={{0,3},{1,2},{2,1},{3,0},{4,7},{5,6},{6,5},{7,4},{8,11},{9,10},{10,... | collective-permute-start | bytes 1277960 | tf_op jit(solution)/shard_map/ppermute | solution.py:44
  104.8 6.0 %collective-permute-start.15 = (bf16[8,104,128]{2,1,0:T(8,128)(2,1)}, bf16[8,104,128]{2,1,0:T(8,128)(2,1)S(1)}, u32[]{:S(2)}, u32[]{:S(2)}) collective-permute-start(bf16[8,104,128]{2,1,0:T(8,128)(2,1)} %get-tuple-element.120), channel_id=1, source_target_pairs={{0,1},{1,0},{2,3},{3,2},{4,5},{5,4},{6,7},{7,6},{8,9},{9,8},{10,11... | collective-permute-start | bytes 638984 | tf_op jit(solution)/shard_map/ppermute | solution.py:44
  105.3 7.1 %collective-permute-start.16 = (bf16[8,104,128]{2,1,0:T(8,128)(2,1)}, bf16[8,104,128]{2,1,0:T(8,128)(2,1)S(1)}, u32[]{:S(2)}, u32[]{:S(2)}) collective-permute-start(bf16[8,104,128]{2,1,0:T(8,128)(2,1)} %get-tuple-element.121), channel_id=1, source_target_pairs={{0,2},{1,3},{2,0},{3,1},{4,6},{5,7},{6,4},{7,5},{8,10},{9,11},{10,... | collective-permute-start | bytes 638984 | tf_op jit(solution)/shard_map/ppermute | solution.py:44
  106.0 11.0 %collective-permute-start.17 = (bf16[8,104,128]{2,1,0:T(8,128)(2,1)}, bf16[8,104,128]{2,1,0:T(8,128)(2,1)S(1)}, u32[]{:S(2)}, u32[]{:S(2)}) collective-permute-start(bf16[8,104,128]{2,1,0:T(8,128)(2,1)} %get-tuple-element.122), channel_id=1, source_target_pairs={{0,3},{1,2},{2,1},{3,0},{4,7},{5,6},{6,5},{7,4},{8,11},{9,10},{10,... | collective-permute-start | bytes 638984 | tf_op jit(solution)/shard_map/ppermute | solution.py:44
  117.7 26.2 %all-to-all-start = ((bf16[16,328,128]{2,1,0:T(8,128)(2,1)}), bf16[16,328,128]{2,1,0:T(8,128)(2,1)S(1)}, u32[]{:S(2)}, u32[]{:S(2)}) async-start(bf16[16,328,128]{2,1,0:T(8,128)(2,1)} %bitcast.28), calls=%async_computation | async-start | bytes 2686976 | tf_op jit(solution)/shard_map/all_to_all | solution.py:523
  121.4 22.4 %collective-permute-start.20 = (bf16[8,104,128]{2,1,0:T(8,128)(2,1)}, bf16[8,104,128]{2,1,0:T(8,128)(2,1)}, u32[]{:S(2)}, u32[]{:S(2)}) collective-permute-start(bf16[8,104,128]{2,1,0:T(8,128)(2,1)} %get-tuple-element.139), channel_id=1, source_target_pairs={{0,1},{1,0},{2,3},{3,2},{4,5},{5,4},{6,7},{7,6},{8,9},{9,8},{10,11... | collective-permute-start | bytes 638984 | tf_op jit(solution)/shard_map/ppermute | solution.py:44
  122.0 21.9 %collective-permute-start.21 = (bf16[8,104,128]{2,1,0:T(8,128)(2,1)}, bf16[8,104,128]{2,1,0:T(8,128)(2,1)}, u32[]{:S(2)}, u32[]{:S(2)}) collective-permute-start(bf16[8,104,128]{2,1,0:T(8,128)(2,1)} %get-tuple-element.140), channel_id=1, source_target_pairs={{0,2},{1,3},{2,0},{3,1},{4,6},{5,7},{6,4},{7,5},{8,10},{9,11},{10,... | collective-permute-start | bytes 638984 | tf_op jit(solution)/shard_map/ppermute | solution.py:44
  122.8 21.1 %collective-permute-start.22 = (bf16[8,104,128]{2,1,0:T(8,128)(2,1)}, bf16[8,104,128]{2,1,0:T(8,128)(2,1)}, u32[]{:S(2)}, u32[]{:S(2)}) collective-permute-start(bf16[8,104,128]{2,1,0:T(8,128)(2,1)} %get-tuple-element.141), channel_id=1, source_target_pairs={{0,3},{1,2},{2,1},{3,0},{4,7},{5,6},{6,5},{7,4},{8,11},{9,10},{10,... | collective-permute-start | bytes 638984 | tf_op jit(solution)/shard_map/ppermute | solution.py:44
  127.0 13.9 %collective-permute-start.18 = (bf16[8,8,832]{2,1,0:T(8,128)(2,1)}, bf16[8,8,832]{2,1,0:T(8,128)(2,1)S(1)}, u32[]{:S(2)}, u32[]{:S(2)}) collective-permute-start(bf16[8,8,832]{2,1,0:T(8,128)(2,1)} %get-tuple-element.136), channel_id=1, source_target_pairs={{0,124},{4,0},{8,4},{12,8},{16,12},{20,16},{24,20},{28,24},{32,28}... | collective-permute-start | bytes 319496 | tf_op jit(solution)/shard_map/ppermute | solution.py:48
  131.9 10.2 %collective-permute-start.19 = (bf16[8,8,832]{2,1,0:T(8,128)(2,1)}, bf16[8,8,832]{2,1,0:T(8,128)(2,1)S(1)}, u32[]{:S(2)}, u32[]{:S(2)}) collective-permute-start(bf16[8,8,832]{2,1,0:T(8,128)(2,1)} %get-tuple-element.137), channel_id=1, source_target_pairs={{0,4},{4,8},{8,12},{12,16},{16,20},{20,24},{24,28},{28,32},{32,36}... | collective-permute-start | bytes 319496 | tf_op jit(solution)/shard_map/ppermute | solution.py:48
  152.9 26.0 %all-to-all-start.1 = ((bf16[16,328,128]{2,1,0:T(8,128)(2,1)}), bf16[16,328,128]{2,1,0:T(8,128)(2,1)}, u32[]{:S(2)}, u32[]{:S(2)}) async-start(bf16[16,328,128]{2,1,0:T(8,128)(2,1)} %plane_copies.1), calls=%async_computation.1 | async-start | bytes 2686976 | tf_op jit(solution)/shard_map/all_to_all | solution.py:523
  (40 other events, 235.4 us)
